TPU v7x, 128 devices: a whole 4x4x4 slice. The times are simulated.
128 devices in a mesh: ax: 32 (over x, y, core), rad: 4 (over z).
Axes of the slice: x: 4, y: 4, z: 4, core: 2. Of those that a mesh axis runs over, the one named last changes fastest.
Arguments:
- couplings: bfloat16 [32, 10, 1728, 1728], P('ax', None, 'rad'), may hold values from -0.071777344 to 0.071777344
- pivots: float32 [32, 1728, 1728], P('ax', 'rad'), may hold values from -0.02946892 to 1.0294689
- pattern: int32 [32, 10, 9, 9], P('ax'), may hold values 0 or 1
- krylov: float32 [32, 32, 1728], P('ax', None, 'rad'), may hold values from -6 to 6
Outputs:
- basis_block: float32 [32, 16, 1728], P('ax', None, 'rad')
- coefficients: float32 [32, 16], replicated
- upper: float32 [16, 16], replicated
All inputs are finite; a program needn't handle non-finite values. No bound on the sum of `pattern` on one device may be relied on, other than what follows from the above.
Results may differ from a plain program's by a relative error of at most 0.0003.
Values sent between devices are 32-bit elements; how exact they have to be, the bound alone decides.
No kernel may reach another device: no remote copies, remote signals or barrier semaphores. Data moves between devices by JAX's collectives and lax.ppermute only.
A program may use at most 128 MiB of HBM per device.

v0:
```python
import functools

import jax
import jax.numpy as jnp
from jax import lax
from jax.experimental import pallas as pl
from jax.experimental.pallas import tpu as pltpu
from jax.sharding import Mesh
from jax.sharding import PartitionSpec as P

NRHS = 16
GROUP = 48
precise = lax.Precision.HIGHEST


VMEM = pl.BlockSpec(memory_space=pltpu.VMEM)
SMEM = pl.BlockSpec(memory_space=pltpu.SMEM)
ANY = pl.BlockSpec(memory_space=pl.ANY)


def near(value):
    return pltpu.with_memory_space_constraint(value, pltpu.VMEM)


def far(value):
    return pltpu.with_memory_space_constraint(value, pltpu.HBM)


def made(shape, dtype=jnp.float32):
    return pltpu.VMEM(shape, dtype)


def nt_dot(a, b, precision=None):
    return lax.dot_general(
        a, b, (((1,), (1,)), ((), ())), precision=precision,
        preferred_element_type=jnp.float32,
    )


def nn_dot(a, b, precision=None):
    return lax.dot_general(
        a, b, (((1,), (0,)), ((), ())), precision=precision,
        preferred_element_type=jnp.float32,
    )


def split2(value):
    high = value.astype(jnp.bfloat16)
    low = (value - high.astype(jnp.float32)).astype(jnp.bfloat16)
    return high, low


def prep_kernel(rung, fields, slots, pattern_ref, couplings_ref, _, out_ref, keeps, sems):
    block = lax.axis_index(("chip", "core"))
    rad = lax.axis_index("rad")
    odd = (block // (1 << rung)) % 2
    rows, width = out_ref.shape[1:]
    points = width // fields
    cut = (rows // GROUP + 1) // 2 * GROUP
    kinds = [2 * rung + odd, 2 * rung + 1 - odd][:slots]
    copies = []
    for part, (start, size) in enumerate(((0, cut), (cut, rows - cut))):
        for slot, kind in enumerate(kinds):
            copy = pltpu.make_async_copy(
                couplings_ref.at[0, kind, pl.ds(start, size)],
                out_ref.at[slot, pl.ds(start, size)],
                sems.at[slot, part],
            )
            copy.start(priority=(slot + part) % 2 if slots == 1 else slot)
            copies.append((slot, start, size, copy))
    first = rad * rows // points
    col_field = lax.broadcasted_iota(jnp.int32, (8, width), 1) // points
    at_field = [col_field == col for col in range(fields)]
    for slot, kind in enumerate(kinds):
        for local in range(keeps.shape[1]):
            keep = jnp.zeros((8, width), jnp.float32)
            for col in range(fields):
                bit = pattern_ref[jnp.minimum(first + local, fields - 1), col, 0, kind]
                keep = jnp.where(at_field[col], bit.astype(jnp.float32), keep)
            keeps[slot, local] = jnp.concatenate([keep, keep], axis=0).astype(jnp.bfloat16)
    for slot, start, size, copy in copies:
        copy.wait()
        for group in range(start, start + size, GROUP):
            keep = keeps[slot, (rad * rows + group) // points - first]
            for tile in range(GROUP // 16):
                at = pl.ds(group + tile * 16, 16)
                out_ref[slot, at, :] = out_ref[slot, at, :] * keep


def prep(rung, slots, pattern, couplings, after):
    rows, width = couplings.shape[2:]
    fields = pattern.shape[0]
    spanned = rows // (width // fields) + 1
    return pl.pallas_call(
        functools.partial(prep_kernel, rung, fields, slots),
        out_shape=made((slots, rows, width), jnp.bfloat16),
        in_specs=[SMEM, ANY, ANY if rung == 0 else VMEM],
        out_specs=VMEM,
        scratch_shapes=[
            pltpu.VMEM((slots, spanned, 16, width), jnp.bfloat16),
            pltpu.SemaphoreType.DMA((slots, 2)),
        ],
        compiler_params=pltpu.CompilerParams(vmem_limit_bytes=4 << 20),
    )(pattern, far(couplings), after if rung == 0 else near(after))


def pivot_kernel(pivots_ref, _, out_ref, stage, sems):
    rows = pivots_ref.shape[1]
    part = rows // 3
    copies = []
    for i in range(3):
        copy = pltpu.make_async_copy(
            pivots_ref.at[0, pl.ds(i * part, part)], stage.at[pl.ds(i * part, part)], sems.at[i]
        )
        copy.start(priority=i % 2)
        copies.append(copy)
    for i, copy in enumerate(copies):
        copy.wait()
        for tile in range(part // 16):
            at = pl.ds(i * part + tile * 16, 16)
            high, low = split2(stage[at, :])
            out_ref[0, at, :] = high
            out_ref[1, at, :] = low


def prep_pivots(pivots, after):
    rows, width = pivots.shape[1:]
    return pl.pallas_call(
        pivot_kernel,
        out_shape=made((2, rows, width), jnp.bfloat16),
        in_specs=[ANY, VMEM],
        out_specs=VMEM,
        scratch_shapes=[pltpu.VMEM((rows, width), jnp.float32), pltpu.SemaphoreType.DMA((3,))],
        compiler_params=pltpu.CompilerParams(vmem_limit_bytes=8 << 20),
        name="prep_pivots",
    )(far(pivots), near(after))


def gather_rows(slices, whole):
    rad = lax.axis_index("rad")
    for m, piece in enumerate(slices):
        first = piece.shape[0] - NRHS if piece.shape[0] > NRHS + 8 else 0
        whole[rad ^ m] = piece[first : first + NRHS, :]
    v = jnp.concatenate([whole[t] for t in range(4)], axis=1)
    return jnp.concatenate(split2(v), axis=0)


def level_kernel(slots, s0, s1, s2, s3, w_ref, *rest):
    g_ref = rest[0] if len(rest) == slots + 2 else None
    outs, whole = rest[-slots - 1 : -1], rest[-1]
    if g_ref is None:
        stored = s0[...]
        product = nt_dot(stored, stored, precise)
        g = jnp.concatenate([product[8 * i : 8 * i + 8] for i in range(4)], axis=1)
    else:
        g = g_ref[...]
    lhs = gather_rows((s0, s1, s2, s3), whole)
    for slot in range(slots):
        both = nt_dot(lhs, w_ref[slot])
        outs[slot][:NRHS, :] = both[:NRHS] + both[NRHS:]
    outs[0][NRHS:, :128] = g
    outs[0][NRHS:, 128:] = jnp.zeros((8, outs[0].shape[1] - 128), jnp.float32)


def level(slots, slices, weights, g):
    rows = weights.shape[1]
    args = (*slices, weights) if g is None else (*slices, weights, g)
    shapes = [(NRHS + 8, rows), (NRHS, rows)][:slots]
    return pl.pallas_call(
        functools.partial(level_kernel, slots),
        out_shape=[made(s) for s in shapes],
        in_specs=[VMEM] * len(args),
        out_specs=[VMEM] * slots,
        scratch_shapes=[pltpu.VMEM((4, NRHS, rows), jnp.float32)],
        compiler_params=pltpu.CompilerParams(vmem_limit_bytes=4 << 20),
        name="level",
    )(*map(near, args))


def solve_kernel(s0, s1, s2, s3, p_ref, stored_ref, x_ref, part_ref, g_ref, whole, gs):
    rad = lax.axis_index("rad")
    lhs = gather_rows((s0, s1, s2, s3), whole)
    both = nt_dot(lhs, p_ref[0])
    x = both[:NRHS] + both[NRHS:] + nt_dot(lhs[:NRHS], p_ref[1])
    x_ref[...] = x
    t = jnp.concatenate(
        [nt_dot(x, stored_ref[0], precise), nt_dot(x, x, precise)], axis=1
    )
    part_ref[...] = jnp.concatenate(
        [t[:8], t[8:], jnp.zeros((8, 32), jnp.float32)], axis=1
    )
    for m, piece in enumerate((s0, s1, s2, s3)):
        gs[rad ^ m] = piece[NRHS:, :128]
    g_ref[...] = (gs[0] + gs[1]) + (gs[2] + gs[3])


def solve(slices, pivots, krylov):
    rows = pivots.shape[1]
    return pl.pallas_call(
        solve_kernel,
        out_shape=[
            made((NRHS, rows)),
            made((8, 128)),
            made((8, 128)),
        ],
        in_specs=[VMEM] * 6,
        out_specs=[VMEM] * 3,
        scratch_shapes=[
            pltpu.VMEM((4, NRHS, rows), jnp.float32),
            pltpu.VMEM((4, 8, 128), jnp.float32),
        ],
        compiler_params=pltpu.CompilerParams(vmem_limit_bytes=8 << 20),
        name="solve",
    )(*map(near, (*slices, pivots, krylov)))


def finish_kernel(total, parts_ref, g_ref, x_ref, stored_ref, basis_ref, coef_ref, upper_ref):
    s = jnp.sum(parts_ref[...], axis=0) * (1.0 / total)
    t = jnp.concatenate([s[:, :48], s[:, 48:96]], axis=0)
    gs = g_ref[...] * (1.0 / total)
    g = jnp.concatenate([gs[:, 32 * i : 32 * i + 32] for i in range(4)], axis=0)
    ct = t[:, :32]
    xx = t[:, 32:48]
    coef_ref[...] = ct
    stored = stored_ref[0]
    remainder = x_ref[...] - nn_dot(ct, stored, precise)
    gram = xx - nt_dot(2.0 * ct - nn_dot(ct, g, precise), ct, precise)
    row = lax.broadcasted_iota(jnp.int32, (NRHS, 2 * NRHS), 0)
    col = lax.broadcasted_iota(jnp.int32, (NRHS, 2 * NRHS), 1)
    eye = (lax.broadcasted_iota(jnp.int32, (NRHS, NRHS), 0)
           == lax.broadcasted_iota(jnp.int32, (NRHS, NRHS), 1)).astype(jnp.float32)
    a = jnp.concatenate([gram, eye], axis=1)
    for k in range(NRHS - 1):
        factor = a[:, k : k + 1] / a[k : k + 1, k : k + 1]
        a = jnp.where(row > k, a - factor * a[k : k + 1, :], a)
    diag = jnp.sum(jnp.where(row == col, a, 0.0), axis=1, keepdims=True)
    a = a * lax.rsqrt(diag)
    u = a[:, :NRHS]
    upper_ref[...] = jnp.where(row[:, :NRHS] <= col[:, :NRHS], u, 0.0)
    basis_ref[0] = nn_dot(a[:, NRHS:], remainder, precise)


def finish(total, parts, g, x, krylov):
    rows = x.shape[1]
    stored = krylov.shape[1]
    return pl.pallas_call(
        functools.partial(finish_kernel, total),
        out_shape=[
            jax.ShapeDtypeStruct((1, NRHS, rows), jnp.float32),
            jax.ShapeDtypeStruct((NRHS, stored), jnp.float32),
            jax.ShapeDtypeStruct((NRHS, NRHS), jnp.float32),
        ],
        in_specs=[VMEM] * 4,
        out_specs=[VMEM] * 3,
        compiler_params=pltpu.CompilerParams(vmem_limit_bytes=8 << 20),
        name="finish",
    )(*map(near, (parts, g, x, krylov)))


ALL = ("chip", "core", "rad")


def swap(value, blocks, rads, stride, parity):
    pairs = []
    for a in range(blocks):
        up = ((a // stride) + parity) % 2 == 0
        b = (a + stride if up else a - stride) % blocks
        pairs += [(a * rads + r, b * rads + r) for r in range(rads)]
    return lax.ppermute(value, ALL, pairs)


def gather(value, blocks, rads):
    out = [value]
    for m in range(1, rads):
        pairs = [(a * rads + r, a * rads + (r ^ m)) for a in range(blocks) for r in range(rads)]
        out.append(lax.ppermute(value, ALL, pairs))
    return out


def step(couplings, pivots, pattern, krylov):
    width = couplings.shape[3]
    blocks = lax.axis_size("chip") * lax.axis_size("core")
    rads = lax.axis_size("rad")
    levels = blocks.bit_length() - 1
    block = lax.axis_index(("chip", "core"))
    pattern = pattern.transpose(2, 3, 0, 1)
    slices = gather(krylov[0], blocks, rads)
    weights = prep(0, 2, pattern, couplings, krylov)
    g = None
    residue = krylov[0, krylov.shape[1] - NRHS :, :]
    for rung in range(levels):
        stride = 1 << rung
        last = rung == levels - 1
        sent = level(1 if last else 2, slices, weights, g)
        if last:
            weights = prep_pivots(pivots, sent[0])
        else:
            weights = prep(rung + 1, 1 if rung + 2 == levels else 2, pattern, couplings, sent[0])
        got = swap(sent[0], blocks, rads, stride, 0)
        other = None if last else swap(sent[1], blocks, rads, stride, 1)
        residue = residue - got[:NRHS]
        g = (sent[0][NRHS:, :128] if g is None else g) + got[NRHS:, :128]
        if not last:
            place = block // stride
            inside = jnp.where(place % 2 == 0, place > 0, place < blocks // stride - 1)
            residue = residue - jnp.where(inside, other, 0.0)
            payload = residue
        else:
            tail = jnp.pad(g, ((0, 0), (0, residue.shape[1] - 128)))
            payload = jnp.concatenate([residue, tail], axis=0)
        slices = gather(payload, blocks, rads)
    x, part, g = solve(slices, weights, krylov)
    part = part + swap(part, blocks, rads, 1, 0)
    chips = blocks // 2 * rads
    parts = lax.all_to_all(
        jnp.broadcast_to(part[None], (chips,) + part.shape), ("chip", "rad"), 0, 0
    )
    basis, coefficients, upper = finish(blocks * width, parts, g, x, krylov)
    return (basis, coefficients.T, upper)


def solution(mesh):
    blocks, rads = mesh.shape["ax"], mesh.shape["rad"]
    split = Mesh(mesh.devices.reshape(blocks // 2, 2, rads), ALL)
    ax = ("chip", "core")
    return jax.shard_map(
        step,
        mesh=split,
        in_specs=(
            P(ax, None, "rad", None),
            P(ax, "rad", None),
            P(ax, None, None, None),
            P(ax, None, "rad"),
        ),
        out_specs=(P(ax, None, "rad"), P(), P()),
        check_vma=False,
    )
```

profile of v0, /device:TPU:1, one launch (start us, length us, event | category | flops | bytes accessed | tf_op | source)
XLA Modules:
  0.0 114.3 jit_solution(7670411353804271734)
XLA Ops:
  0.6 2.5 %collective-permute-start = (f32[32,432]{1,0:T(8,128)}, f32[32,432]{1,0:T(8,128)S(1)}, u32[]{:S(2)}, u32[]{:S(2)}) collective-permute-start(f32[32,432]{1,0:T(8,128)} %bitcast.5), channel_id=1, source_target_pairs={{0,1},{1,0},{2,3},{3,2},{4,5},{5,4},{6,7},{7,6},{8,9},{9,8},{10,11... | collective-permute-start | bytes 165896 | tf_op jit(solution)/shard_map/ppermute | solution.py:276
  3.2 3.3 %collective-permute-start.1 = (f32[32,432]{1,0:T(8,128)}, f32[32,432]{1,0:T(8,128)S(1)}, u32[]{:S(2)}, u32[]{:S(2)}) collective-permute-start(f32[32,432]{1,0:T(8,128)} %bitcast.6), channel_id=1, source_target_pairs={{0,2},{1,3},{2,0},{3,1},{4,6},{5,7},{6,4},{7,5},{8,10},{9,11},{10,... | collective-permute-start | bytes 165896 | tf_op jit(solution)/shard_map/ppermute | solution.py:276
  8.2 3.2 %shard_map.67.w_ref = bf16[2,432,1728]{2,1,0:T(8,128)(2,1)S(1)} custom-call(s32[9,9,1,10]{3,2,1,0:T(1,128)S(1)} %bitcast.9, bf16[1,10,432,1728]{3,2,1,0:T(8,128)(2,1)} %couplings_ref.9, f32[1,32,432]{2,1,0:T(8,128)S(1)} %copy-done), custom_call_target="tpu_custom_call" | custom-call | tf_op jit(solution)/shard_map/pallas_call | solution.py:94
  12.4 2.0 %collective-permute-start.3 = (f32[24,432]{1,0:T(8,128)S(1)}, f32[24,432]{1,0:T(8,128)S(1)}, u32[]{:S(2)}, u32[]{:S(2)}) collective-permute-start(f32[24,432]{1,0:T(8,128)S(1)} %get-tuple-element.17._), channel_id=1, source_target_pairs={{0,4},{1,5},{2,6},{3,7},{4,0},{5,1},{6,2},{7,3},{8,12},{9,13},{10,... | collective-permute-start | bytes 124424 | tf_op jit(solution)/shard_map/ppermute | solution.py:269
  15.7 3.2 %shard_map.68.w_ref = bf16[2,432,1728]{2,1,0:T(8,128)(2,1)S(1)} custom-call(s32[9,9,1,10]{3,2,1,0:T(1,128)S(1)} %bitcast.10, bf16[1,10,432,1728]{3,2,1,0:T(8,128)(2,1)} %couplings_ref.9, f32[24,432]{1,0:T(8,128)S(1)} %get-tuple-element.17._), custom_call_target="tpu_custom_call" | custom-call | tf_op jit(solution)/shard_map/pallas_call | solution.py:94
  19.0 3.3 %collective-permute-start.6 = (f32[16,432]{1,0:T(8,128)S(1)}, f32[16,432]{1,0:T(8,128)S(1)}, u32[]{:S(2)}, u32[]{:S(2)}) collective-permute-start(f32[16,432]{1,0:T(8,128)S(1)} %fusion.3.s0), channel_id=1, source_target_pairs={{0,2},{1,3},{2,0},{3,1},{4,6},{5,7},{6,4},{7,5},{8,10},{9,11},{10,... | collective-permute-start | bytes 82952 | tf_op jit(solution)/shard_map/ppermute | solution.py:276
  23.9 2.3 %collective-permute-done.7.s3 = f32[16,432]{1,0:T(8,128)S(1)} collective-permute-done((f32[16,432]{1,0:T(8,128)S(1)}, f32[16,432]{1,0:T(8,128)S(1)}, u32[]{:S(2)}, u32[]{:S(2)}) %collective-permute-start.7) | collective-permute-done | bytes 27680 | tf_op jit(solution)/shard_map/ppermute | solution.py:276
  28.8 5.6 %collective-permute-start.9 = (f32[16,432]{1,0:T(8,128)S(1)}, f32[16,432]{1,0:T(8,128)S(1)}, u32[]{:S(2)}, u32[]{:S(2)}) collective-permute-start(f32[16,432]{1,0:T(8,128)S(1)} %get-tuple-element.20), channel_id=1, source_target_pairs={{0,120},{1,121},{2,122},{3,123},{4,124},{5,125},{6,126},{7,127},{8... | collective-permute-start | bytes 82952 | tf_op jit(solution)/shard_map/ppermute | solution.py:269
  34.4 3.2 %shard_map.69.w_ref = bf16[2,432,1728]{2,1,0:T(8,128)(2,1)S(1)} custom-call(s32[9,9,1,10]{3,2,1,0:T(1,128)S(1)} %bitcast.11, bf16[1,10,432,1728]{3,2,1,0:T(8,128)(2,1)} %couplings_ref.9, f32[24,432]{1,0:T(8,128)S(1)} %get-tuple-element.19._), custom_call_target="tpu_custom_call" | custom-call | tf_op jit(solution)/shard_map/pallas_call | solution.py:94
  39.4 2.1 %collective-permute-start.12 = (f32[16,432]{1,0:T(8,128)S(1)}, f32[16,432]{1,0:T(8,128)S(1)}, u32[]{:S(2)}, u32[]{:S(2)}) collective-permute-start(f32[16,432]{1,0:T(8,128)S(1)} %fusion.2.s0), channel_id=1, source_target_pairs={{0,3},{1,2},{2,1},{3,0},{4,7},{5,6},{6,5},{7,4},{8,11},{9,10},{10,... | collective-permute-start | bytes 82952 | tf_op jit(solution)/shard_map/ppermute | solution.py:276
  44.3 2.0 %collective-permute-start.14 = (f32[16,432]{1,0:T(8,128)S(1)}, f32[16,432]{1,0:T(8,128)S(1)}, u32[]{:S(2)}, u32[]{:S(2)}) collective-permute-start(f32[16,432]{1,0:T(8,128)S(1)} %get-tuple-element.22), channel_id=1, source_target_pairs={{0,112},{1,113},{2,114},{3,115},{4,116},{5,117},{6,118},{7,119},{8... | collective-permute-start | bytes 82952 | tf_op jit(solution)/shard_map/ppermute | solution.py:269
  46.3 3.2 %shard_map.70.w_ref = bf16[2,432,1728]{2,1,0:T(8,128)(2,1)S(1)} custom-call(s32[9,9,1,10]{3,2,1,0:T(1,128)S(1)} %bitcast.12, bf16[1,10,432,1728]{3,2,1,0:T(8,128)(2,1)} %couplings_ref.9, f32[24,432]{1,0:T(8,128)S(1)} %get-tuple-element.21._), custom_call_target="tpu_custom_call" | custom-call | tf_op jit(solution)/shard_map/pallas_call | solution.py:94
  50.9 3.3 %collective-permute-start.16 = (f32[16,432]{1,0:T(8,128)S(1)}, f32[16,432]{1,0:T(8,128)S(1)}, u32[]{:S(2)}, u32[]{:S(2)}) collective-permute-start(f32[16,432]{1,0:T(8,128)S(1)} %fusion.1.s0), channel_id=1, source_target_pairs={{0,2},{1,3},{2,0},{3,1},{4,6},{5,7},{6,4},{7,5},{8,10},{9,11},{10,... | collective-permute-start | bytes 82952 | tf_op jit(solution)/shard_map/ppermute | solution.py:276
  55.9 2.2 %collective-permute-done.17.s3 = f32[16,432]{1,0:T(8,128)S(1)} collective-permute-done((f32[16,432]{1,0:T(8,128)S(1)}, f32[16,432]{1,0:T(8,128)S(1)}, u32[]{:S(2)}, u32[]{:S(2)}) %collective-permute-start.17) | collective-permute-done | bytes 27680 | tf_op jit(solution)/shard_map/ppermute | solution.py:276
  60.0 2.7 %shard_map.71.w_ref = bf16[1,432,1728]{2,1,0:T(8,128)(2,1)S(1)} custom-call(s32[9,9,1,10]{3,2,1,0:T(1,128)S(1)} %bitcast.13, bf16[1,10,432,1728]{3,2,1,0:T(8,128)(2,1)} %couplings_ref.9, f32[24,432]{1,0:T(8,128)S(1)} %get-tuple-element.23._), custom_call_target="tpu_custom_call" | custom-call | tf_op jit(solution)/shard_map/pallas_call | solution.py:94
  64.0 1.7 %collective-permute-start.21 = (f32[16,432]{1,0:T(8,128)S(1)}, f32[16,432]{1,0:T(8,128)S(1)}, u32[]{:S(2)}, u32[]{:S(2)}) collective-permute-start(f32[16,432]{1,0:T(8,128)S(1)} %fusion.s0), channel_id=1, source_target_pairs={{0,2},{1,3},{2,0},{3,1},{4,6},{5,7},{6,4},{7,5},{8,10},{9,11},{10,... | collective-permute-start | bytes 82952 | tf_op jit(solution)/shard_map/ppermute | solution.py:276
  65.8 2.1 %collective-permute-start.22 = (f32[16,432]{1,0:T(8,128)S(1)}, f32[16,432]{1,0:T(8,128)S(1)}, u32[]{:S(2)}, u32[]{:S(2)}) collective-permute-start(f32[16,432]{1,0:T(8,128)S(1)} %fusion.s0), channel_id=1, source_target_pairs={{0,3},{1,2},{2,1},{3,0},{4,7},{5,6},{6,5},{7,4},{8,11},{9,10},{10,... | collective-permute-start | bytes 82952 | tf_op jit(solution)/shard_map/ppermute | solution.py:276
  71.4 3.4 %collective-permute-done.23 = f32[24,432]{1,0:T(8,128)S(1)} collective-permute-done((f32[24,432]{1,0:T(8,128)S(1)}, f32[24,432]{1,0:T(8,128)S(1)}, u32[]{:S(2)}, u32[]{:S(2)}) %collective-permute-start.23) | collective-permute-done | bytes 41504 | tf_op jit(solution)/shard_map/ppermute | solution.py:269
  75.1 3.4 %collective-permute-start.25 = (f32[24,432]{1,0:T(8,128)S(1)}, f32[24,432]{1,0:T(8,128)S(1)}, u32[]{:S(2)}, u32[]{:S(2)}) collective-permute-start(f32[24,432]{1,0:T(8,128)S(1)} %select_maximum_fusion.s0), channel_id=1, source_target_pairs={{0,2},{1,3},{2,0},{3,1},{4,6},{5,7},{6,4},{7,5},{8,10},{9,11},{10,... | collective-permute-start | bytes 124424 | tf_op jit(solution)/shard_map/ppermute | solution.py:276
  78.7 2.1 %prep_pivots.1.p_ref = bf16[2,432,1728]{2,1,0:T(8,128)(2,1)S(1)} custom-call(f32[1,432,1728]{2,1,0:T(8,128)} %pivots_ref.1, f32[24,432]{1,0:T(8,128)S(1)} %level.9._), custom_call_target="tpu_custom_call" | custom-call | tf_op jit(solution)/shard_map/prep_pivots/pallas_call | solution.py:128
  80.9 1.7 %collective-permute-done.26.s3 = f32[24,432]{1,0:T(8,128)S(1)} collective-permute-done((f32[24,432]{1,0:T(8,128)S(1)}, f32[24,432]{1,0:T(8,128)S(1)}, u32[]{:S(2)}, u32[]{:S(2)}) %collective-permute-start.26) | collective-permute-done | bytes 41504 | tf_op jit(solution)/shard_map/ppermute | solution.py:276
  84.1 12.4 %collective-permute-start.27 = (f32[8,128]{1,0:T(8,128)S(1)}, f32[8,128]{1,0:T(8,128)S(1)}, u32[]{:S(2)}, u32[]{:S(2)}) collective-permute-start(f32[8,128]{1,0:T(8,128)S(1)} %get-tuple-element.25), channel_id=1, source_target_pairs={{0,4},{1,5},{2,6},{3,7},{4,0},{5,1},{6,2},{7,3},{8,12},{9,13},{10,... | collective-permute-start | bytes 12296 | tf_op jit(solution)/shard_map/ppermute | solution.py:269
  97.3 14.3 %all_to_all.5.parts_ref = f32[64,8,128]{2,1,0:T(8,128)S(1)} all-to-all(f32[64,8,128]{2,1,0:T(8,128)S(1)} %broadcast_in_dim.14), channel_id=1, replica_groups=mesh['chip'=16,'core'=2,'rad'=4] {'chip','rad'}, dimensions={0} | all-to-all | bytes 524288 | tf_op jit(solution)/shard_map/all_to_all | solution.py:315
  111.6 2.7 %finish.1 = (f32[1,16,432]{2,1,0:T(8,128)}, f32[16,32]{1,0:T(8,128)}, f32[16,16]{1,0:T(8,128)}) custom-call(f32[64,8,128]{2,1,0:T(8,128)S(1)} %all_to_all.5.parts_ref, f32[8,128]{1,0:T(8,128)S(1)} %get-tuple-element.26.g_ref, f32[16,432]{1,0:T(8,128)S(1)} %get-tuple-element.27.x_ref, f32[1,32,432]{2,1,0:T(8,128)S(1)} %copy-done.1), custom_call_target="tpu_custom_call" | custom-call | tf_op jit(solution)/shard_map/finish/pallas_call | solution.py:246
  (67 shorter events, 25.5 us)
Async XLA Ops:
  0.6 10.7 %collective-permute-start = (f32[32,432]{1,0:T(8,128)}, f32[32,432]{1,0:T(8,128)S(1)}, u32[]{:S(2)}, u32[]{:S(2)}) collective-permute-start(f32[32,432]{1,0:T(8,128)} %bitcast.5), channel_id=1, source_target_pairs={{0,1},{1,0},{2,3},{3,2},{4,5},{5,4},{6,7},{7,6},{8,9},{9,8},{10,11... | collective-permute-start | bytes 165896 | tf_op jit(solution)/shard_map/ppermute | solution.py:276
  3.2 8.2 %collective-permute-start.1 = (f32[32,432]{1,0:T(8,128)}, f32[32,432]{1,0:T(8,128)S(1)}, u32[]{:S(2)}, u32[]{:S(2)}) collective-permute-start(f32[32,432]{1,0:T(8,128)} %bitcast.6), channel_id=1, source_target_pairs={{0,2},{1,3},{2,0},{3,1},{4,6},{5,7},{6,4},{7,5},{8,10},{9,11},{10,... | collective-permute-start | bytes 165896 | tf_op jit(solution)/shard_map/ppermute | solution.py:276
  6.5 4.9 %collective-permute-start.2 = (f32[32,432]{1,0:T(8,128)}, f32[32,432]{1,0:T(8,128)S(1)}, u32[]{:S(2)}, u32[]{:S(2)}) collective-permute-start(f32[32,432]{1,0:T(8,128)} %bitcast.7), channel_id=1, source_target_pairs={{0,3},{1,2},{2,1},{3,0},{4,7},{5,6},{6,5},{7,4},{8,11},{9,10},{10,... | collective-permute-start | bytes 165896 | tf_op jit(solution)/shard_map/ppermute | solution.py:276
  12.4 6.5 %collective-permute-start.3 = (f32[24,432]{1,0:T(8,128)S(1)}, f32[24,432]{1,0:T(8,128)S(1)}, u32[]{:S(2)}, u32[]{:S(2)}) collective-permute-start(f32[24,432]{1,0:T(8,128)S(1)} %get-tuple-element.17._), channel_id=1, source_target_pairs={{0,4},{1,5},{2,6},{3,7},{4,0},{5,1},{6,2},{7,3},{8,12},{9,13},{10,... | collective-permute-start | bytes 124424 | tf_op jit(solution)/shard_map/ppermute | solution.py:269
  14.4 4.4 %collective-permute-start.4 = (f32[16,432]{1,0:T(8,128)S(1)}, f32[16,432]{1,0:T(8,128)S(1)}, u32[]{:S(2)}, u32[]{:S(2)}) collective-permute-start(f32[16,432]{1,0:T(8,128)S(1)} %get-tuple-element.18), channel_id=1, source_target_pairs={{0,124},{1,125},{2,126},{3,127},{4,8},{5,9},{6,10},{7,11},{8,4},{9... | collective-permute-start | bytes 82952 | tf_op jit(solution)/shard_map/ppermute | solution.py:269
  19.0 4.9 %collective-permute-start.6 = (f32[16,432]{1,0:T(8,128)S(1)}, f32[16,432]{1,0:T(8,128)S(1)}, u32[]{:S(2)}, u32[]{:S(2)}) collective-permute-start(f32[16,432]{1,0:T(8,128)S(1)} %fusion.3.s0), channel_id=1, source_target_pairs={{0,2},{1,3},{2,0},{3,1},{4,6},{5,7},{6,4},{7,5},{8,10},{9,11},{10,... | collective-permute-start | bytes 82952 | tf_op jit(solution)/shard_map/ppermute | solution.py:276
  22.3 4.0 %collective-permute-start.7 = (f32[16,432]{1,0:T(8,128)S(1)}, f32[16,432]{1,0:T(8,128)S(1)}, u32[]{:S(2)}, u32[]{:S(2)}) collective-permute-start(f32[16,432]{1,0:T(8,128)S(1)} %fusion.3.s0), channel_id=1, source_target_pairs={{0,3},{1,2},{2,1},{3,0},{4,7},{5,6},{6,5},{7,4},{8,11},{9,10},{10,... | collective-permute-start | bytes 82952 | tf_op jit(solution)/shard_map/ppermute | solution.py:276
  27.1 10.4 %collective-permute-start.8 = (f32[24,432]{1,0:T(8,128)S(1)}, f32[24,432]{1,0:T(8,128)S(1)}, u32[]{:S(2)}, u32[]{:S(2)}) collective-permute-start(f32[24,432]{1,0:T(8,128)S(1)} %get-tuple-element.19._), channel_id=1, source_target_pairs={{0,8},{1,9},{2,10},{3,11},{4,12},{5,13},{6,14},{7,15},{8,0},{9,1},... | collective-permute-start | bytes 124424 | tf_op jit(solution)/shard_map/ppermute | solution.py:269
  28.8 8.8 %collective-permute-start.9 = (f32[16,432]{1,0:T(8,128)S(1)}, f32[16,432]{1,0:T(8,128)S(1)}, u32[]{:S(2)}, u32[]{:S(2)}) collective-permute-start(f32[16,432]{1,0:T(8,128)S(1)} %get-tuple-element.20), channel_id=1, source_target_pairs={{0,120},{1,121},{2,122},{3,123},{4,124},{5,125},{6,126},{7,127},{8... | collective-permute-start | bytes 82952 | tf_op jit(solution)/shard_map/ppermute | solution.py:269
  37.7 4.3 %collective-permute-start.11 = (f32[16,432]{1,0:T(8,128)S(1)}, f32[16,432]{1,0:T(8,128)S(1)}, u32[]{:S(2)}, u32[]{:S(2)}) collective-permute-start(f32[16,432]{1,0:T(8,128)S(1)} %fusion.2.s0), channel_id=1, source_target_pairs={{0,2},{1,3},{2,0},{3,1},{4,6},{5,7},{6,4},{7,5},{8,10},{9,11},{10,... | collective-permute-start | bytes 82952 | tf_op jit(solution)/shard_map/ppermute | solution.py:276
  39.4 4.0 %collective-permute-start.12 = (f32[16,432]{1,0:T(8,128)S(1)}, f32[16,432]{1,0:T(8,128)S(1)}, u32[]{:S(2)}, u32[]{:S(2)}) collective-permute-start(f32[16,432]{1,0:T(8,128)S(1)} %fusion.2.s0), channel_id=1, source_target_pairs={{0,3},{1,2},{2,1},{3,0},{4,7},{5,6},{6,5},{7,4},{8,11},{9,10},{10,... | collective-permute-start | bytes 82952 | tf_op jit(solution)/shard_map/ppermute | solution.py:276
  44.3 6.5 %collective-permute-start.13 = (f32[24,432]{1,0:T(8,128)S(1)}, f32[24,432]{1,0:T(8,128)S(1)}, u32[]{:S(2)}, u32[]{:S(2)}) collective-permute-start(f32[24,432]{1,0:T(8,128)S(1)} %get-tuple-element.21._), channel_id=1, source_target_pairs={{0,16},{1,17},{2,18},{3,19},{4,20},{5,21},{6,22},{7,23},{8,24},{9,... | collective-permute-start | bytes 124424 | tf_op jit(solution)/shard_map/ppermute | solution.py:269
  44.3 6.4 %collective-permute-start.14 = (f32[16,432]{1,0:T(8,128)S(1)}, f32[16,432]{1,0:T(8,128)S(1)}, u32[]{:S(2)}, u32[]{:S(2)}) collective-permute-start(f32[16,432]{1,0:T(8,128)S(1)} %get-tuple-element.22), channel_id=1, source_target_pairs={{0,112},{1,113},{2,114},{3,115},{4,116},{5,117},{6,118},{7,119},{8... | collective-permute-start | bytes 82952 | tf_op jit(solution)/shard_map/ppermute | solution.py:269
  50.9 5.0 %collective-permute-start.16 = (f32[16,432]{1,0:T(8,128)S(1)}, f32[16,432]{1,0:T(8,128)S(1)}, u32[]{:S(2)}, u32[]{:S(2)}) collective-permute-start(f32[16,432]{1,0:T(8,128)S(1)} %fusion.1.s0), channel_id=1, source_target_pairs={{0,2},{1,3},{2,0},{3,1},{4,6},{5,7},{6,4},{7,5},{8,10},{9,11},{10,... | collective-permute-start | bytes 82952 | tf_op jit(solution)/shard_map/ppermute | solution.py:276
  54.1 4.0 %collective-permute-start.17 = (f32[16,432]{1,0:T(8,128)S(1)}, f32[16,432]{1,0:T(8,128)S(1)}, u32[]{:S(2)}, u32[]{:S(2)}) collective-permute-start(f32[16,432]{1,0:T(8,128)S(1)} %fusion.1.s0), channel_id=1, source_target_pairs={{0,3},{1,2},{2,1},{3,0},{4,7},{5,6},{6,5},{7,4},{8,11},{9,10},{10,... | collective-permute-start | bytes 82952 | tf_op jit(solution)/shard_map/ppermute | solution.py:276
  59.0 4.9 %collective-permute-start.18 = (f32[24,432]{1,0:T(8,128)S(1)}, f32[24,432]{1,0:T(8,128)S(1)}, u32[]{:S(2)}, u32[]{:S(2)}) collective-permute-start(f32[24,432]{1,0:T(8,128)S(1)} %get-tuple-element.23._), channel_id=1, source_target_pairs={{0,32},{1,33},{2,34},{3,35},{4,36},{5,37},{6,38},{7,39},{8,40},{9,... | collective-permute-start | bytes 124424 | tf_op jit(solution)/shard_map/ppermute | solution.py:269
  60.0 4.0 %collective-permute-start.19 = (f32[16,432]{1,0:T(8,128)S(1)}, f32[16,432]{1,0:T(8,128)S(1)}, u32[]{:S(2)}, u32[]{:S(2)}) collective-permute-start(f32[16,432]{1,0:T(8,128)S(1)} %get-tuple-element.24), channel_id=1, source_target_pairs={{0,96},{1,97},{2,98},{3,99},{4,100},{5,101},{6,102},{7,103},{8,104... | collective-permute-start | bytes 82952 | tf_op jit(solution)/shard_map/ppermute | solution.py:269
  64.0 4.3 %collective-permute-start.21 = (f32[16,432]{1,0:T(8,128)S(1)}, f32[16,432]{1,0:T(8,128)S(1)}, u32[]{:S(2)}, u32[]{:S(2)}) collective-permute-start(f32[16,432]{1,0:T(8,128)S(1)} %fusion.s0), channel_id=1, source_target_pairs={{0,2},{1,3},{2,0},{3,1},{4,6},{5,7},{6,4},{7,5},{8,10},{9,11},{10,... | collective-permute-start | bytes 82952 | tf_op jit(solution)/shard_map/ppermute | solution.py:276
  65.8 4.0 %collective-permute-start.22 = (f32[16,432]{1,0:T(8,128)S(1)}, f32[16,432]{1,0:T(8,128)S(1)}, u32[]{:S(2)}, u32[]{:S(2)}) collective-permute-start(f32[16,432]{1,0:T(8,128)S(1)} %fusion.s0), channel_id=1, source_target_pairs={{0,3},{1,2},{2,1},{3,0},{4,7},{5,6},{6,5},{7,4},{8,11},{9,10},{10,... | collective-permute-start | bytes 82952 | tf_op jit(solution)/shard_map/ppermute | solution.py:276
  70.3 4.5 %collective-permute-start.23 = (f32[24,432]{1,0:T(8,128)S(1)}, f32[24,432]{1,0:T(8,128)S(1)}, u32[]{:S(2)}, u32[]{:S(2)}) collective-permute-start(f32[24,432]{1,0:T(8,128)S(1)} %level.9._), channel_id=1, source_target_pairs={{0,64},{1,65},{2,66},{3,67},{4,68},{5,69},{6,70},{7,71},{8,72},{9,... | collective-permute-start | bytes 124424 | tf_op jit(solution)/shard_map/ppermute | solution.py:269
  74.8 6.1 %collective-permute-start.24 = (f32[24,432]{1,0:T(8,128)S(1)}, f32[24,432]{1,0:T(8,128)S(1)}, u32[]{:S(2)}, u32[]{:S(2)}) collective-permute-start(f32[24,432]{1,0:T(8,128)S(1)} %select_maximum_fusion.s0), channel_id=1, source_target_pairs={{0,1},{1,0},{2,3},{3,2},{4,5},{5,4},{6,7},{7,6},{8,9},{9,8},{10,11... | collective-permute-start | bytes 124424 | tf_op jit(solution)/shard_map/ppermute | solution.py:276
  75.1 5.8 %collective-permute-start.25 = (f32[24,432]{1,0:T(8,128)S(1)}, f32[24,432]{1,0:T(8,128)S(1)}, u32[]{:S(2)}, u32[]{:S(2)}) collective-permute-start(f32[24,432]{1,0:T(8,128)S(1)} %select_maximum_fusion.s0), channel_id=1, source_target_pairs={{0,2},{1,3},{2,0},{3,1},{4,6},{5,7},{6,4},{7,5},{8,10},{9,11},{10,... | collective-permute-start | bytes 124424 | tf_op jit(solution)/shard_map/ppermute | solution.py:276
  78.5 4.2 %collective-permute-start.26 = (f32[24,432]{1,0:T(8,128)S(1)}, f32[24,432]{1,0:T(8,128)S(1)}, u32[]{:S(2)}, u32[]{:S(2)}) collective-permute-start(f32[24,432]{1,0:T(8,128)S(1)} %select_maximum_fusion.s0), channel_id=1, source_target_pairs={{0,3},{1,2},{2,1},{3,0},{4,7},{5,6},{6,5},{7,4},{8,11},{9,10},{10,... | collective-permute-start | bytes 124424 | tf_op jit(solution)/shard_map/ppermute | solution.py:276
  84.1 13.2 %collective-permute-start.27 = (f32[8,128]{1,0:T(8,128)S(1)}, f32[8,128]{1,0:T(8,128)S(1)}, u32[]{:S(2)}, u32[]{:S(2)}) collective-permute-start(f32[8,128]{1,0:T(8,128)S(1)} %get-tuple-element.25), channel_id=1, source_target_pairs={{0,4},{1,5},{2,6},{3,7},{4,0},{5,1},{6,2},{7,3},{8,12},{9,13},{10,... | collective-permute-start | bytes 12296 | tf_op jit(solution)/shard_map/ppermute | solution.py:269
  (8 other events, 25.0 us)
where the time goes:
time: 115 us; the launch traced here: 114 us
  starting transfers between devices  52.5 us (46%)
  Pallas kernels  25.8 us (22%)
  waiting for transfers between devices  19 us (17%)
  blocking collectives  14.3 us (12%)
  local copies, waits for them, and re-layouts  1.72 us (1%)
    ppermute x10, starting transfers between devices, swap(): return lax.ppermute(value, ALL, pairs)  27 us
    ppermute x18, starting transfers between devices, gather(): out.append(lax.ppermute(value, ALL, pairs))  25.5 us
    pallas_call x5, Pallas kernels, prep(): pl.pallas_call(functools.partial(prep_kernel, rung, fields, slots), out_s...  15.3 us
    all_to_all x1, blocking collectives, step(): lax.all_to_all(jnp.broadcast_to(part[None], (chips,) + part.shape), ('chi...  14.3 us
    ppermute x18, waiting for transfers between devices, gather(): out.append(lax.ppermute(value, ALL, pairs))  12.3 us
    ppermute x10, waiting for transfers between devices, swap(): return lax.ppermute(value, ALL, pairs)  6.72 us
    pallas_call x5, Pallas kernels, level(): pl.pallas_call(functools.partial(level_kernel, slots), out_shape=[made(s)...  4.26 us
    pallas_call x1, Pallas kernels, finish(): pl.pallas_call(functools.partial(finish_kernel, total), out_shape=[jax.Sh...  2.71 us
  transfers between devices with their start and end apart: 28, of which 13 were waited for; matrix products, arithmetic and copies ran while one was open for 0% of the time, Pallas kernels for 15%

commit v1 on v0

--- a/solution.py
+++ b/solution.py
@@ -9,7 +9,6 @@
 from jax.sharding import PartitionSpec as P
 
 NRHS = 16
-GROUP = 48
 precise = lax.Precision.HIGHEST
 
 
@@ -50,58 +49,69 @@
     return high, low
 
 
-def prep_kernel(rung, fields, slots, pattern_ref, couplings_ref, _, out_ref, keeps, sems):
-    block = lax.axis_index(("chip", "core"))
-    rad = lax.axis_index("rad")
-    odd = (block // (1 << rung)) % 2
-    rows, width = out_ref.shape[1:]
+def masks_kernel(pattern_ref, out_ref):
+    spanned, kinds_pad, width = out_ref.shape
+    fields, _, _, kinds = pattern_ref.shape
     points = width // fields
-    cut = (rows // GROUP + 1) // 2 * GROUP
-    kinds = [2 * rung + odd, 2 * rung + 1 - odd][:slots]
+    first = lax.axis_index("rad") * (width // lax.axis_size("rad")) // points
+    col_field = lax.broadcasted_iota(jnp.int32, (kinds_pad, width), 1) // points
+    for local in range(spanned):
+        field = jnp.minimum(first + local, fields - 1)
+        rows = [pattern_ref[field, col, :, :].astype(jnp.float32) for col in range(fields)]
+        table = jnp.concatenate(rows, axis=0)
+        table = jnp.concatenate(
+            [table, jnp.zeros((fields, 128 - kinds), jnp.float32)], axis=1
+        )
+        table = jnp.concatenate([table, jnp.zeros((16 - fields, 128), jnp.float32)], axis=0)
+        by_kind = table.T[:kinds_pad]
+        keep = jnp.zeros((kinds_pad, width), jnp.float32)
+        for col in range(fields):
+            keep = jnp.where(col_field == col, by_kind[:, col : col + 1], keep)
+        out_ref[local] = keep
+
+
+def make_masks(pattern, rows, width):
+    fields, _, _, _ = pattern.shape
+    spanned = rows // (width // fields) + 1
+    return pl.pallas_call(
+        masks_kernel,
+        out_shape=made((spanned, 16, width)),
+        in_specs=[VMEM],
+        out_specs=VMEM,
+        compiler_params=pltpu.CompilerParams(vmem_limit_bytes=4 << 20),
+        name="masks",
+    )(near(pattern))
+
+
+def kind_of(rung, slot):
+    odd = (lax.axis_index(("chip", "core")) // (1 << rung)) % 2
+    return 2 * rung + (odd if slot == 0 else 1 - odd)
+
+
+def fetch_kernel(rung, slots, couplings_ref, *rest):
+    out_ref, sems = rest[-2:]
     copies = []
-    for part, (start, size) in enumerate(((0, cut), (cut, rows - cut))):
-        for slot, kind in enumerate(kinds):
-            copy = pltpu.make_async_copy(
-                couplings_ref.at[0, kind, pl.ds(start, size)],
-                out_ref.at[slot, pl.ds(start, size)],
-                sems.at[slot, part],
-            )
-            copy.start(priority=(slot + part) % 2 if slots == 1 else slot)
-            copies.append((slot, start, size, copy))
-    first = rad * rows // points
-    col_field = lax.broadcasted_iota(jnp.int32, (8, width), 1) // points
-    at_field = [col_field == col for col in range(fields)]
-    for slot, kind in enumerate(kinds):
-        for local in range(keeps.shape[1]):
-            keep = jnp.zeros((8, width), jnp.float32)
-            for col in range(fields):
-                bit = pattern_ref[jnp.minimum(first + local, fields - 1), col, 0, kind]
-                keep = jnp.where(at_field[col], bit.astype(jnp.float32), keep)
-            keeps[slot, local] = jnp.concatenate([keep, keep], axis=0).astype(jnp.bfloat16)
-    for slot, start, size, copy in copies:
+    for slot in range(slots):
+        copy = pltpu.make_async_copy(
+            couplings_ref.at[0, kind_of(rung, slot)], out_ref.at[slot], sems.at[slot]
+        )
+        copy.start(priority=slot)
+        copies.append(copy)
+    for copy in copies:
         copy.wait()
-        for group in range(start, start + size, GROUP):
-            keep = keeps[slot, (rad * rows + group) // points - first]
-            for tile in range(GROUP // 16):
-                at = pl.ds(group + tile * 16, 16)
-                out_ref[slot, at, :] = out_ref[slot, at, :] * keep
-
-
-def prep(rung, slots, pattern, couplings, after):
+
+
+def fetch(rung, slots, couplings, after=None):
     rows, width = couplings.shape[2:]
-    fields = pattern.shape[0]
-    spanned = rows // (width // fields) + 1
-    return pl.pallas_call(
-        functools.partial(prep_kernel, rung, fields, slots),
+    args = (far(couplings),) if after is None else (far(couplings), near(after))
+    return pl.pallas_call(
+        functools.partial(fetch_kernel, rung, slots),
         out_shape=made((slots, rows, width), jnp.bfloat16),
-        in_specs=[SMEM, ANY, ANY if rung == 0 else VMEM],
+        in_specs=[ANY, VMEM][: len(args)],
         out_specs=VMEM,
-        scratch_shapes=[
-            pltpu.VMEM((slots, spanned, 16, width), jnp.bfloat16),
-            pltpu.SemaphoreType.DMA((slots, 2)),
-        ],
+        scratch_shapes=[pltpu.SemaphoreType.DMA((slots,))],
         compiler_params=pltpu.CompilerParams(vmem_limit_bytes=4 << 20),
-    )(pattern, far(couplings), after if rung == 0 else near(after))
+    )(*args)
 
 
 def pivot_kernel(pivots_ref, _, out_ref, stage, sems):
@@ -145,7 +155,7 @@
     return jnp.concatenate(split2(v), axis=0)
 
 
-def level_kernel(slots, s0, s1, s2, s3, w_ref, *rest):
+def level_kernel(rung, slots, points, s0, s1, s2, s3, w_ref, masks_ref, *rest):
     g_ref = rest[0] if len(rest) == slots + 2 else None
     outs, whole = rest[-slots - 1 : -1], rest[-1]
     if g_ref is None:
@@ -155,19 +165,35 @@
     else:
         g = g_ref[...]
     lhs = gather_rows((s0, s1, s2, s3), whole)
+    spanned = masks_ref.shape[0]
+    rows = w_ref.shape[1]
+    offset = lax.axis_index("rad") * rows
+    first = offset // points
+    row = offset + lax.broadcasted_iota(jnp.int32, (NRHS, rows), 1)
     for slot in range(slots):
-        both = nt_dot(lhs, w_ref[slot])
-        outs[slot][:NRHS, :] = both[:NRHS] + both[NRHS:]
+        kind = kind_of(rung, slot)
+        parts = []
+        for local in range(spanned):
+            keep = masks_ref[local, pl.ds(kind, 1), :]
+            keep = jnp.broadcast_to(keep, (16, keep.shape[1])).astype(jnp.bfloat16)
+            parts.append(lhs * jnp.concatenate([keep, keep], axis=0))
+        product = nt_dot(jnp.concatenate(parts, axis=0), w_ref[slot])
+        push = None
+        for local in reversed(range(spanned)):
+            at = 2 * NRHS * local
+            one = product[at : at + NRHS] + product[at + NRHS : at + 2 * NRHS]
+            push = one if push is None else jnp.where(row < (first + local + 1) * points, one, push)
+        outs[slot][:NRHS, :] = push
     outs[0][NRHS:, :128] = g
     outs[0][NRHS:, 128:] = jnp.zeros((8, outs[0].shape[1] - 128), jnp.float32)
 
 
-def level(slots, slices, weights, g):
+def level(rung, slots, points, slices, weights, masks, g):
     rows = weights.shape[1]
-    args = (*slices, weights) if g is None else (*slices, weights, g)
+    args = (*slices, weights, masks) if g is None else (*slices, weights, masks, g)
     shapes = [(NRHS + 8, rows), (NRHS, rows)][:slots]
     return pl.pallas_call(
-        functools.partial(level_kernel, slots),
+        functools.partial(level_kernel, rung, slots, points),
         out_shape=[made(s) for s in shapes],
         in_specs=[VMEM] * len(args),
         out_specs=[VMEM] * slots,
@@ -285,17 +311,19 @@
     block = lax.axis_index(("chip", "core"))
     pattern = pattern.transpose(2, 3, 0, 1)
     slices = gather(krylov[0], blocks, rads)
-    weights = prep(0, 2, pattern, couplings, krylov)
+    weights = fetch(0, 2, couplings)
+    masks = make_masks(pattern, couplings.shape[2], width)
+    points = width // pattern.shape[0]
     g = None
     residue = krylov[0, krylov.shape[1] - NRHS :, :]
     for rung in range(levels):
         stride = 1 << rung
         last = rung == levels - 1
-        sent = level(1 if last else 2, slices, weights, g)
+        sent = level(rung, 1 if last else 2, points, slices, weights, masks, g)
         if last:
             weights = prep_pivots(pivots, sent[0])
         else:
-            weights = prep(rung + 1, 1 if rung + 2 == levels else 2, pattern, couplings, sent[0])
+            weights = fetch(rung + 1, 1 if rung + 2 == levels else 2, couplings, sent[0])
         got = swap(sent[0], blocks, rads, stride, 0)
         other = None if last else swap(sent[1], blocks, rads, stride, 1)
         residue = residue - got[:NRHS]

time: 115 us -> 115 us (level)
  Pallas kernels: 25.8 us -> 20 us
  waiting for transfers between devices: 19 us -> 21.6 us
  blocking collectives: 14.3 us -> 16.5 us
  starting transfers between devices: 52.5 us -> 54.4 us
  local copies, waits for them, and re-layouts: 1.72 us -> 0.03 us
    pallas_call x10 -> x11, Pallas kernels: 19.6 us -> 13.8 us  [the longest x5 8.93 us: fetch(): pl.pallas_call(functools.partial(fetch_kernel, rung, slots), out_shape=ma...]
    ppermute x10, waiting for transfers between devices: 6.72 us -> 8.99 us  [swap(): return lax.ppermute(value, ALL, pairs)]
    all_to_all x1, blocking collectives: 14.3 us -> 16.5 us  [step(): lax.all_to_all(jnp.broadcast_to(part[None], (chips,) + part.shape), ('chi...]
    ppermute x10, starting transfers between devices: 27 us -> 28.9 us  [swap(): return lax.ppermute(value, ALL, pairs)]
    unnamed x8 -> x4, local copies, waits for them, and re-layouts: 1.69 us -> 0.01 us
  transfers between devices with their start and end apart: 28 -> 28, of which waited for: 13 -> 15; matrix products, arithmetic and copies ran while one was open for 0% -> 0% of each run, Pallas kernels for 15% -> 10%
where the time goes in v1:
time: 115 us; the launch traced here: 114 us
  starting transfers between devices  54.4 us (47%)
  waiting for transfers between devices  21.6 us (19%)
  Pallas kernels  20 us (17%)
  blocking collectives  16.5 us (14%)
    ppermute x10, starting transfers between devices, swap(): return lax.ppermute(value, ALL, pairs)  28.9 us
    ppermute x18, starting transfers between devices, gather(): out.append(lax.ppermute(value, ALL, pairs))  25.5 us
    all_to_all x1, blocking collectives, step(): lax.all_to_all(jnp.broadcast_to(part[None], (chips,) + part.shape), ('chi...  16.5 us
    ppermute x18, waiting for transfers between devices, gather(): out.append(lax.ppermute(value, ALL, pairs))  12.6 us
    ppermute x10, waiting for transfers between devices, swap(): return lax.ppermute(value, ALL, pairs)  8.99 us
    pallas_call x5, Pallas kernels, fetch(): pl.pallas_call(functools.partial(fetch_kernel, rung, slots), out_shape=ma...  8.93 us
    pallas_call x5, Pallas kernels, level(): pl.pallas_call(functools.partial(level_kernel, rung, slots, points), out_...  4.49 us
    pallas_call x1, Pallas kernels, finish(): pl.pallas_call(functools.partial(finish_kernel, total), out_shape=[jax.Sh...  2.71 us
  transfers between devices with their start and end apart: 28, of which 15 were waited for; matrix products, arithmetic and copies ran while one was open for 0% of the time, Pallas kernels for 10%

profile of v1, /device:TPU:1, one launch (start us, length us, event | category | flops | bytes accessed | tf_op | source)
XLA Modules:
  0.0 113.7 jit_solution(7578509291227076343)
XLA Ops:
  0.7 2.5 %collective-permute-start = (f32[32,432]{1,0:T(8,128)}, f32[32,432]{1,0:T(8,128)S(1)}, u32[]{:S(2)}, u32[]{:S(2)}) collective-permute-start(f32[32,432]{1,0:T(8,128)} %bitcast.5), channel_id=1, source_target_pairs={{0,1},{1,0},{2,3},{3,2},{4,5},{5,4},{6,7},{7,6},{8,9},{9,8},{10,11... | collective-permute-start | bytes 165896 | tf_op jit(solution)/shard_map/ppermute | solution.py:302
  3.2 3.3 %collective-permute-start.1 = (f32[32,432]{1,0:T(8,128)}, f32[32,432]{1,0:T(8,128)S(1)}, u32[]{:S(2)}, u32[]{:S(2)}) collective-permute-start(f32[32,432]{1,0:T(8,128)} %bitcast.6), channel_id=1, source_target_pairs={{0,2},{1,3},{2,0},{3,1},{4,6},{5,7},{6,4},{7,5},{8,10},{9,11},{10,... | collective-permute-start | bytes 165896 | tf_op jit(solution)/shard_map/ppermute | solution.py:302
  6.5 1.9 %shard_map.67.w_ref = bf16[2,432,1728]{2,1,0:T(8,128)(2,1)S(1)} custom-call(bf16[1,10,432,1728]{3,2,1,0:T(8,128)(2,1)} %couplings_ref.9), custom_call_target="tpu_custom_call" | custom-call | tf_op jit(solution)/shard_map/pallas_call | solution.py:107
  9.3 1.8 %collective-permute-done.2.s3 = f32[32,432]{1,0:T(8,128)S(1)} collective-permute-done((f32[32,432]{1,0:T(8,128)}, f32[32,432]{1,0:T(8,128)S(1)}, u32[]{:S(2)}, u32[]{:S(2)}) %collective-permute-start.2) | collective-permute-done | bytes 55328 | tf_op jit(solution)/shard_map/ppermute | solution.py:302
  12.2 2.3 %collective-permute-start.3 = (f32[24,432]{1,0:T(8,128)S(1)}, f32[24,432]{1,0:T(8,128)S(1)}, u32[]{:S(2)}, u32[]{:S(2)}) collective-permute-start(f32[24,432]{1,0:T(8,128)S(1)} %get-tuple-element.17.rest_0_), channel_id=1, source_target_pairs={{0,4},{1,5},{2,6},{3,7},{4,0},{5,1},{6,2},{7,3},{8,12},{9,13},{10,... | collective-permute-start | bytes 124424 | tf_op jit(solution)/shard_map/ppermute | solution.py:295
  15.8 1.9 %shard_map.68.w_ref = bf16[2,432,1728]{2,1,0:T(8,128)(2,1)S(1)} custom-call(bf16[1,10,432,1728]{3,2,1,0:T(8,128)(2,1)} %couplings_ref.9, f32[24,432]{1,0:T(8,128)S(1)} %get-tuple-element.17.rest_0_), custom_call_target="tpu_custom_call" | custom-call | tf_op jit(solution)/shard_map/pallas_call | solution.py:107
  18.9 2.9 %collective-permute-start.7 = (f32[16,432]{1,0:T(8,128)S(1)}, f32[16,432]{1,0:T(8,128)S(1)}, u32[]{:S(2)}, u32[]{:S(2)}) collective-permute-start(f32[16,432]{1,0:T(8,128)S(1)} %fusion.3.s0), channel_id=1, source_target_pairs={{0,3},{1,2},{2,1},{3,0},{4,7},{5,6},{6,5},{7,4},{8,11},{9,10},{10,... | collective-permute-start | bytes 82952 | tf_op jit(solution)/shard_map/ppermute | solution.py:302
  25.6 6.9 %collective-permute-start.9 = (f32[16,432]{1,0:T(8,128)S(1)}, f32[16,432]{1,0:T(8,128)S(1)}, u32[]{:S(2)}, u32[]{:S(2)}) collective-permute-start(f32[16,432]{1,0:T(8,128)S(1)} %get-tuple-element.20), channel_id=1, source_target_pairs={{0,120},{1,121},{2,122},{3,123},{4,124},{5,125},{6,126},{7,127},{8... | collective-permute-start | bytes 82952 | tf_op jit(solution)/shard_map/ppermute | solution.py:295
  32.5 1.9 %shard_map.69.w_ref = bf16[2,432,1728]{2,1,0:T(8,128)(2,1)S(1)} custom-call(bf16[1,10,432,1728]{3,2,1,0:T(8,128)(2,1)} %couplings_ref.9, f32[24,432]{1,0:T(8,128)S(1)} %get-tuple-element.19.rest_0_), custom_call_target="tpu_custom_call" | custom-call | tf_op jit(solution)/shard_map/pallas_call | solution.py:107
  35.1 3.3 %collective-permute-start.11 = (f32[16,432]{1,0:T(8,128)S(1)}, f32[16,432]{1,0:T(8,128)S(1)}, u32[]{:S(2)}, u32[]{:S(2)}) collective-permute-start(f32[16,432]{1,0:T(8,128)S(1)} %fusion.2.s0), channel_id=1, source_target_pairs={{0,2},{1,3},{2,0},{3,1},{4,6},{5,7},{6,4},{7,5},{8,10},{9,11},{10,... | collective-permute-start | bytes 82952 | tf_op jit(solution)/shard_map/ppermute | solution.py:302
  40.1 2.3 %collective-permute-done.12.s3 = f32[16,432]{1,0:T(8,128)S(1)} collective-permute-done((f32[16,432]{1,0:T(8,128)S(1)}, f32[16,432]{1,0:T(8,128)S(1)}, u32[]{:S(2)}, u32[]{:S(2)}) %collective-permute-start.12) | collective-permute-done | bytes 27680 | tf_op jit(solution)/shard_map/ppermute | solution.py:302
  43.5 2.0 %collective-permute-start.14 = (f32[16,432]{1,0:T(8,128)S(1)}, f32[16,432]{1,0:T(8,128)S(1)}, u32[]{:S(2)}, u32[]{:S(2)}) collective-permute-start(f32[16,432]{1,0:T(8,128)S(1)} %get-tuple-element.22), channel_id=1, source_target_pairs={{0,112},{1,113},{2,114},{3,115},{4,116},{5,117},{6,118},{7,119},{8... | collective-permute-start | bytes 82952 | tf_op jit(solution)/shard_map/ppermute | solution.py:295
  45.5 1.9 %shard_map.70.w_ref = bf16[2,432,1728]{2,1,0:T(8,128)(2,1)S(1)} custom-call(bf16[1,10,432,1728]{3,2,1,0:T(8,128)(2,1)} %couplings_ref.9, f32[24,432]{1,0:T(8,128)S(1)} %get-tuple-element.21.rest_0_), custom_call_target="tpu_custom_call" | custom-call | tf_op jit(solution)/shard_map/pallas_call | solution.py:107
  47.4 2.5 %collective-permute-done.14 = f32[16,432]{1,0:T(8,128)S(1)} collective-permute-done((f32[16,432]{1,0:T(8,128)S(1)}, f32[16,432]{1,0:T(8,128)S(1)}, u32[]{:S(2)}, u32[]{:S(2)}) %collective-permute-start.14) | collective-permute-done | bytes 27680 | tf_op jit(solution)/shard_map/ppermute | solution.py:295
  51.2 2.7 %collective-permute-start.17 = (f32[16,432]{1,0:T(8,128)S(1)}, f32[16,432]{1,0:T(8,128)S(1)}, u32[]{:S(2)}, u32[]{:S(2)}) collective-permute-start(f32[16,432]{1,0:T(8,128)S(1)} %fusion.1.s0), channel_id=1, source_target_pairs={{0,3},{1,2},{2,1},{3,0},{4,7},{5,6},{6,5},{7,4},{8,11},{9,10},{10,... | collective-permute-start | bytes 82952 | tf_op jit(solution)/shard_map/ppermute | solution.py:302
  58.8 1.8 %collective-permute-done.19 = f32[16,432]{1,0:T(8,128)S(1)} collective-permute-done((f32[16,432]{1,0:T(8,128)S(1)}, f32[16,432]{1,0:T(8,128)S(1)}, u32[]{:S(2)}, u32[]{:S(2)}) %collective-permute-start.19) | collective-permute-done | bytes 27680 | tf_op jit(solution)/shard_map/ppermute | solution.py:295
  61.0 3.3 %collective-permute-start.21 = (f32[16,432]{1,0:T(8,128)S(1)}, f32[16,432]{1,0:T(8,128)S(1)}, u32[]{:S(2)}, u32[]{:S(2)}) collective-permute-start(f32[16,432]{1,0:T(8,128)S(1)} %fusion.s0), channel_id=1, source_target_pairs={{0,2},{1,3},{2,0},{3,1},{4,6},{5,7},{6,4},{7,5},{8,10},{9,11},{10,... | collective-permute-start | bytes 82952 | tf_op jit(solution)/shard_map/ppermute | solution.py:302
  65.9 2.3 %collective-permute-done.22.s3 = f32[16,432]{1,0:T(8,128)S(1)} collective-permute-done((f32[16,432]{1,0:T(8,128)S(1)}, f32[16,432]{1,0:T(8,128)S(1)}, u32[]{:S(2)}, u32[]{:S(2)}) %collective-permute-start.22) | collective-permute-done | bytes 27680 | tf_op jit(solution)/shard_map/ppermute | solution.py:302
  69.7 3.6 %collective-permute-done.23 = f32[24,432]{1,0:T(8,128)S(1)} collective-permute-done((f32[24,432]{1,0:T(8,128)S(1)}, f32[24,432]{1,0:T(8,128)S(1)}, u32[]{:S(2)}, u32[]{:S(2)}) %collective-permute-start.23) | collective-permute-done | bytes 41504 | tf_op jit(solution)/shard_map/ppermute | solution.py:295
  75.0 2.4 %collective-permute-start.26 = (f32[24,432]{1,0:T(8,128)S(1)}, f32[24,432]{1,0:T(8,128)S(1)}, u32[]{:S(2)}, u32[]{:S(2)}) collective-permute-start(f32[24,432]{1,0:T(8,128)S(1)} %select_maximum_fusion.s0), channel_id=1, source_target_pairs={{0,3},{1,2},{2,1},{3,0},{4,7},{5,6},{6,5},{7,4},{8,11},{9,10},{10,... | collective-permute-start | bytes 124424 | tf_op jit(solution)/shard_map/ppermute | solution.py:302
  77.3 2.1 %prep_pivots.1.p_ref = bf16[2,432,1728]{2,1,0:T(8,128)(2,1)S(1)} custom-call(f32[1,432,1728]{2,1,0:T(8,128)} %pivots_ref.1, f32[24,432]{1,0:T(8,128)S(1)} %level.9._), custom_call_target="tpu_custom_call" | custom-call | tf_op jit(solution)/shard_map/prep_pivots/pallas_call | solution.py:138
  80.9 12.7 %collective-permute-start.27 = (f32[8,128]{1,0:T(8,128)S(1)}, f32[8,128]{1,0:T(8,128)S(1)}, u32[]{:S(2)}, u32[]{:S(2)}) collective-permute-start(f32[8,128]{1,0:T(8,128)S(1)} %get-tuple-element.25), channel_id=1, source_target_pairs={{0,4},{1,5},{2,6},{3,7},{4,0},{5,1},{6,2},{7,3},{8,12},{9,13},{10,... | collective-permute-start | bytes 12296 | tf_op jit(solution)/shard_map/ppermute | solution.py:295
  94.5 16.5 %all_to_all.5.parts_ref = f32[64,8,128]{2,1,0:T(8,128)S(1)} all-to-all(f32[64,8,128]{2,1,0:T(8,128)S(1)} %broadcast_in_dim.14), channel_id=1, replica_groups=mesh['chip'=16,'core'=2,'rad'=4] {'chip','rad'}, dimensions={0} | all-to-all | bytes 524288 | tf_op jit(solution)/shard_map/all_to_all | solution.py:343
  111.0 2.7 %finish.1 = (f32[1,16,432]{2,1,0:T(8,128)}, f32[16,32]{1,0:T(8,128)}, f32[16,16]{1,0:T(8,128)}) custom-call(f32[64,8,128]{2,1,0:T(8,128)S(1)} %all_to_all.5.parts_ref, f32[8,128]{1,0:T(8,128)S(1)} %get-tuple-element.26.g_ref, f32[16,432]{1,0:T(8,128)S(1)} %get-tuple-element.27.x_ref, f32[1,32,432]{2,1,0:T(8,128)S(1)} %copy-done), custom_call_target="tpu_custom_call" | custom-call | tf_op jit(solution)/shard_map/finish/pallas_call | solution.py:272
  (64 shorter events, 25.1 us)
Async XLA Ops:
  0.7 8.1 %collective-permute-start = (f32[32,432]{1,0:T(8,128)}, f32[32,432]{1,0:T(8,128)S(1)}, u32[]{:S(2)}, u32[]{:S(2)}) collective-permute-start(f32[32,432]{1,0:T(8,128)} %bitcast.5), channel_id=1, source_target_pairs={{0,1},{1,0},{2,3},{3,2},{4,5},{5,4},{6,7},{7,6},{8,9},{9,8},{10,11... | collective-permute-start | bytes 165896 | tf_op jit(solution)/shard_map/ppermute | solution.py:302
  3.2 6.1 %collective-permute-start.1 = (f32[32,432]{1,0:T(8,128)}, f32[32,432]{1,0:T(8,128)S(1)}, u32[]{:S(2)}, u32[]{:S(2)}) collective-permute-start(f32[32,432]{1,0:T(8,128)} %bitcast.6), channel_id=1, source_target_pairs={{0,2},{1,3},{2,0},{3,1},{4,6},{5,7},{6,4},{7,5},{8,10},{9,11},{10,... | collective-permute-start | bytes 165896 | tf_op jit(solution)/shard_map/ppermute | solution.py:302
  6.5 4.7 %collective-permute-start.2 = (f32[32,432]{1,0:T(8,128)}, f32[32,432]{1,0:T(8,128)S(1)}, u32[]{:S(2)}, u32[]{:S(2)}) collective-permute-start(f32[32,432]{1,0:T(8,128)} %bitcast.7), channel_id=1, source_target_pairs={{0,3},{1,2},{2,1},{3,0},{4,7},{5,6},{6,5},{7,4},{8,11},{9,10},{10,... | collective-permute-start | bytes 165896 | tf_op jit(solution)/shard_map/ppermute | solution.py:302
  12.2 5.7 %collective-permute-start.3 = (f32[24,432]{1,0:T(8,128)S(1)}, f32[24,432]{1,0:T(8,128)S(1)}, u32[]{:S(2)}, u32[]{:S(2)}) collective-permute-start(f32[24,432]{1,0:T(8,128)S(1)} %get-tuple-element.17.rest_0_), channel_id=1, source_target_pairs={{0,4},{1,5},{2,6},{3,7},{4,0},{5,1},{6,2},{7,3},{8,12},{9,13},{10,... | collective-permute-start | bytes 124424 | tf_op jit(solution)/shard_map/ppermute | solution.py:295
  18.0 4.3 %collective-permute-start.6 = (f32[16,432]{1,0:T(8,128)S(1)}, f32[16,432]{1,0:T(8,128)S(1)}, u32[]{:S(2)}, u32[]{:S(2)}) collective-permute-start(f32[16,432]{1,0:T(8,128)S(1)} %fusion.3.s0), channel_id=1, source_target_pairs={{0,2},{1,3},{2,0},{3,1},{4,6},{5,7},{6,4},{7,5},{8,10},{9,11},{10,... | collective-permute-start | bytes 82952 | tf_op jit(solution)/shard_map/ppermute | solution.py:302
  18.9 4.2 %collective-permute-start.7 = (f32[16,432]{1,0:T(8,128)S(1)}, f32[16,432]{1,0:T(8,128)S(1)}, u32[]{:S(2)}, u32[]{:S(2)}) collective-permute-start(f32[16,432]{1,0:T(8,128)S(1)} %fusion.3.s0), channel_id=1, source_target_pairs={{0,3},{1,2},{2,1},{3,0},{4,7},{5,6},{6,5},{7,4},{8,11},{9,10},{10,... | collective-permute-start | bytes 82952 | tf_op jit(solution)/shard_map/ppermute | solution.py:302
  24.1 10.3 %collective-permute-start.8 = (f32[24,432]{1,0:T(8,128)S(1)}, f32[24,432]{1,0:T(8,128)S(1)}, u32[]{:S(2)}, u32[]{:S(2)}) collective-permute-start(f32[24,432]{1,0:T(8,128)S(1)} %get-tuple-element.19.rest_0_), channel_id=1, source_target_pairs={{0,8},{1,9},{2,10},{3,11},{4,12},{5,13},{6,14},{7,15},{8,0},{9,1},... | collective-permute-start | bytes 124424 | tf_op jit(solution)/shard_map/ppermute | solution.py:295
  25.6 8.8 %collective-permute-start.9 = (f32[16,432]{1,0:T(8,128)S(1)}, f32[16,432]{1,0:T(8,128)S(1)}, u32[]{:S(2)}, u32[]{:S(2)}) collective-permute-start(f32[16,432]{1,0:T(8,128)S(1)} %get-tuple-element.20), channel_id=1, source_target_pairs={{0,120},{1,121},{2,122},{3,123},{4,124},{5,125},{6,126},{7,127},{8... | collective-permute-start | bytes 82952 | tf_op jit(solution)/shard_map/ppermute | solution.py:295
  34.5 4.0 %collective-permute-start.10 = (f32[16,432]{1,0:T(8,128)S(1)}, f32[16,432]{1,0:T(8,128)S(1)}, u32[]{:S(2)}, u32[]{:S(2)}) collective-permute-start(f32[16,432]{1,0:T(8,128)S(1)} %fusion.2.s0), channel_id=1, source_target_pairs={{0,1},{1,0},{2,3},{3,2},{4,5},{5,4},{6,7},{7,6},{8,9},{9,8},{10,11... | collective-permute-start | bytes 82952 | tf_op jit(solution)/shard_map/ppermute | solution.py:302
  35.1 4.9 %collective-permute-start.11 = (f32[16,432]{1,0:T(8,128)S(1)}, f32[16,432]{1,0:T(8,128)S(1)}, u32[]{:S(2)}, u32[]{:S(2)}) collective-permute-start(f32[16,432]{1,0:T(8,128)S(1)} %fusion.2.s0), channel_id=1, source_target_pairs={{0,2},{1,3},{2,0},{3,1},{4,6},{5,7},{6,4},{7,5},{8,10},{9,11},{10,... | collective-permute-start | bytes 82952 | tf_op jit(solution)/shard_map/ppermute | solution.py:302
  38.4 4.0 %collective-permute-start.12 = (f32[16,432]{1,0:T(8,128)S(1)}, f32[16,432]{1,0:T(8,128)S(1)}, u32[]{:S(2)}, u32[]{:S(2)}) collective-permute-start(f32[16,432]{1,0:T(8,128)S(1)} %fusion.2.s0), channel_id=1, source_target_pairs={{0,3},{1,2},{2,1},{3,0},{4,7},{5,6},{6,5},{7,4},{8,11},{9,10},{10,... | collective-permute-start | bytes 82952 | tf_op jit(solution)/shard_map/ppermute | solution.py:302
  43.4 6.6 %collective-permute-start.13 = (f32[24,432]{1,0:T(8,128)S(1)}, f32[24,432]{1,0:T(8,128)S(1)}, u32[]{:S(2)}, u32[]{:S(2)}) collective-permute-start(f32[24,432]{1,0:T(8,128)S(1)} %get-tuple-element.21.rest_0_), channel_id=1, source_target_pairs={{0,16},{1,17},{2,18},{3,19},{4,20},{5,21},{6,22},{7,23},{8,24},{9,... | collective-permute-start | bytes 124424 | tf_op jit(solution)/shard_map/ppermute | solution.py:295
  43.5 6.5 %collective-permute-start.14 = (f32[16,432]{1,0:T(8,128)S(1)}, f32[16,432]{1,0:T(8,128)S(1)}, u32[]{:S(2)}, u32[]{:S(2)}) collective-permute-start(f32[16,432]{1,0:T(8,128)S(1)} %get-tuple-element.22), channel_id=1, source_target_pairs={{0,112},{1,113},{2,114},{3,115},{4,116},{5,117},{6,118},{7,119},{8... | collective-permute-start | bytes 82952 | tf_op jit(solution)/shard_map/ppermute | solution.py:295
  50.0 4.6 %collective-permute-start.16 = (f32[16,432]{1,0:T(8,128)S(1)}, f32[16,432]{1,0:T(8,128)S(1)}, u32[]{:S(2)}, u32[]{:S(2)}) collective-permute-start(f32[16,432]{1,0:T(8,128)S(1)} %fusion.1.s0), channel_id=1, source_target_pairs={{0,2},{1,3},{2,0},{3,1},{4,6},{5,7},{6,4},{7,5},{8,10},{9,11},{10,... | collective-permute-start | bytes 82952 | tf_op jit(solution)/shard_map/ppermute | solution.py:302
  51.2 4.0 %collective-permute-start.17 = (f32[16,432]{1,0:T(8,128)S(1)}, f32[16,432]{1,0:T(8,128)S(1)}, u32[]{:S(2)}, u32[]{:S(2)}) collective-permute-start(f32[16,432]{1,0:T(8,128)S(1)} %fusion.1.s0), channel_id=1, source_target_pairs={{0,3},{1,2},{2,1},{3,0},{4,7},{5,6},{6,5},{7,4},{8,11},{9,10},{10,... | collective-permute-start | bytes 82952 | tf_op jit(solution)/shard_map/ppermute | solution.py:302
  56.2 4.4 %collective-permute-start.18 = (f32[24,432]{1,0:T(8,128)S(1)}, f32[24,432]{1,0:T(8,128)S(1)}, u32[]{:S(2)}, u32[]{:S(2)}) collective-permute-start(f32[24,432]{1,0:T(8,128)S(1)} %get-tuple-element.23.rest_0_), channel_id=1, source_target_pairs={{0,32},{1,33},{2,34},{3,35},{4,36},{5,37},{6,38},{7,39},{8,40},{9,... | collective-permute-start | bytes 124424 | tf_op jit(solution)/shard_map/ppermute | solution.py:295
  56.3 4.3 %collective-permute-start.19 = (f32[16,432]{1,0:T(8,128)S(1)}, f32[16,432]{1,0:T(8,128)S(1)}, u32[]{:S(2)}, u32[]{:S(2)}) collective-permute-start(f32[16,432]{1,0:T(8,128)S(1)} %get-tuple-element.24), channel_id=1, source_target_pairs={{0,96},{1,97},{2,98},{3,99},{4,100},{5,101},{6,102},{7,103},{8,104... | collective-permute-start | bytes 82952 | tf_op jit(solution)/shard_map/ppermute | solution.py:295
  61.0 4.9 %collective-permute-start.21 = (f32[16,432]{1,0:T(8,128)S(1)}, f32[16,432]{1,0:T(8,128)S(1)}, u32[]{:S(2)}, u32[]{:S(2)}) collective-permute-start(f32[16,432]{1,0:T(8,128)S(1)} %fusion.s0), channel_id=1, source_target_pairs={{0,2},{1,3},{2,0},{3,1},{4,6},{5,7},{6,4},{7,5},{8,10},{9,11},{10,... | collective-permute-start | bytes 82952 | tf_op jit(solution)/shard_map/ppermute | solution.py:302
  64.3 4.0 %collective-permute-start.22 = (f32[16,432]{1,0:T(8,128)S(1)}, f32[16,432]{1,0:T(8,128)S(1)}, u32[]{:S(2)}, u32[]{:S(2)}) collective-permute-start(f32[16,432]{1,0:T(8,128)S(1)} %fusion.s0), channel_id=1, source_target_pairs={{0,3},{1,2},{2,1},{3,0},{4,7},{5,6},{6,5},{7,4},{8,11},{9,10},{10,... | collective-permute-start | bytes 82952 | tf_op jit(solution)/shard_map/ppermute | solution.py:302
  68.9 4.5 %collective-permute-start.23 = (f32[24,432]{1,0:T(8,128)S(1)}, f32[24,432]{1,0:T(8,128)S(1)}, u32[]{:S(2)}, u32[]{:S(2)}) collective-permute-start(f32[24,432]{1,0:T(8,128)S(1)} %level.9._), channel_id=1, source_target_pairs={{0,64},{1,65},{2,66},{3,67},{4,68},{5,69},{6,70},{7,71},{8,72},{9,... | collective-permute-start | bytes 124424 | tf_op jit(solution)/shard_map/ppermute | solution.py:295
  73.4 6.1 %collective-permute-start.24 = (f32[24,432]{1,0:T(8,128)S(1)}, f32[24,432]{1,0:T(8,128)S(1)}, u32[]{:S(2)}, u32[]{:S(2)}) collective-permute-start(f32[24,432]{1,0:T(8,128)S(1)} %select_maximum_fusion.s0), channel_id=1, source_target_pairs={{0,1},{1,0},{2,3},{3,2},{4,5},{5,4},{6,7},{7,6},{8,9},{9,8},{10,11... | collective-permute-start | bytes 124424 | tf_op jit(solution)/shard_map/ppermute | solution.py:302
  73.5 6.0 %collective-permute-start.25 = (f32[24,432]{1,0:T(8,128)S(1)}, f32[24,432]{1,0:T(8,128)S(1)}, u32[]{:S(2)}, u32[]{:S(2)}) collective-permute-start(f32[24,432]{1,0:T(8,128)S(1)} %select_maximum_fusion.s0), channel_id=1, source_target_pairs={{0,2},{1,3},{2,0},{3,1},{4,6},{5,7},{6,4},{7,5},{8,10},{9,11},{10,... | collective-permute-start | bytes 124424 | tf_op jit(solution)/shard_map/ppermute | solution.py:302
  75.0 4.5 %collective-permute-start.26 = (f32[24,432]{1,0:T(8,128)S(1)}, f32[24,432]{1,0:T(8,128)S(1)}, u32[]{:S(2)}, u32[]{:S(2)}) collective-permute-start(f32[24,432]{1,0:T(8,128)S(1)} %select_maximum_fusion.s0), channel_id=1, source_target_pairs={{0,3},{1,2},{2,1},{3,0},{4,7},{5,6},{6,5},{7,4},{8,11},{9,10},{10,... | collective-permute-start | bytes 124424 | tf_op jit(solution)/shard_map/ppermute | solution.py:302
  80.9 13.5 %collective-permute-start.27 = (f32[8,128]{1,0:T(8,128)S(1)}, f32[8,128]{1,0:T(8,128)S(1)}, u32[]{:S(2)}, u32[]{:S(2)}) collective-permute-start(f32[8,128]{1,0:T(8,128)S(1)} %get-tuple-element.25), channel_id=1, source_target_pairs={{0,4},{1,5},{2,6},{3,7},{4,0},{5,1},{6,2},{7,3},{8,12},{9,13},{10,... | collective-permute-start | bytes 12296 | tf_op jit(solution)/shard_map/ppermute | solution.py:295
  (6 other events, 33.5 us)

commit v2 on v1

--- a/solution.py
+++ b/solution.py
@@ -251,19 +251,26 @@
     stored = stored_ref[0]
     remainder = x_ref[...] - nn_dot(ct, stored, precise)
     gram = xx - nt_dot(2.0 * ct - nn_dot(ct, g, precise), ct, precise)
-    row = lax.broadcasted_iota(jnp.int32, (NRHS, 2 * NRHS), 0)
-    col = lax.broadcasted_iota(jnp.int32, (NRHS, 2 * NRHS), 1)
-    eye = (lax.broadcasted_iota(jnp.int32, (NRHS, NRHS), 0)
-           == lax.broadcasted_iota(jnp.int32, (NRHS, NRHS), 1)).astype(jnp.float32)
-    a = jnp.concatenate([gram, eye], axis=1)
+    sub = lax.broadcasted_iota(jnp.int32, (NRHS, 128), 0)
+    lane = lax.broadcasted_iota(jnp.int32, (NRHS, 128), 1)
+    rows = [jnp.broadcast_to(gram[:, i : i + 1], (NRHS, 128)) for i in range(NRHS)]
     for k in range(NRHS - 1):
-        factor = a[:, k : k + 1] / a[k : k + 1, k : k + 1]
-        a = jnp.where(row > k, a - factor * a[k : k + 1, :], a)
-    diag = jnp.sum(jnp.where(row == col, a, 0.0), axis=1, keepdims=True)
-    a = a * lax.rsqrt(diag)
-    u = a[:, :NRHS]
-    upper_ref[...] = jnp.where(row[:, :NRHS] <= col[:, :NRHS], u, 0.0)
-    basis_ref[0] = nn_dot(a[:, NRHS:], remainder, precise)
+        inverse = 1.0 / rows[k][k : k + 1, :]
+        at_pivot = sub == k
+        pivot_row = jnp.where(at_pivot, 1.0, rows[k])
+        for i in range(k + 1, NRHS):
+            factor = rows[i][k : k + 1, :] * inverse
+            rows[i] = jnp.where(at_pivot, 0.0, rows[i]) - factor * pivot_row
+    packed = rows[0]
+    for i in range(1, NRHS):
+        packed = jnp.where(lane == i, rows[i], packed)
+    on_diag = sub == lane
+    diag = jnp.sum(jnp.where(on_diag, packed, 0.0), axis=0, keepdims=True)
+    scale = lax.rsqrt(jnp.where(lane[:1] < NRHS, diag, 1.0))
+    lower = jnp.where(sub >= lane, packed, 0.0) * scale
+    inverse_t = jnp.where(on_diag, 1.0, jnp.where(sub < lane, packed, 0.0)) * scale
+    upper_ref[...] = lower.T[:NRHS, :]
+    basis_ref[0] = nn_dot(inverse_t.T[:NRHS, :], remainder, precise)
 
 
 def finish(total, parts, g, x, krylov):
@@ -320,10 +327,6 @@
         stride = 1 << rung
         last = rung == levels - 1
         sent = level(rung, 1 if last else 2, points, slices, weights, masks, g)
-        if last:
-            weights = prep_pivots(pivots, sent[0])
-        else:
-            weights = fetch(rung + 1, 1 if rung + 2 == levels else 2, couplings, sent[0])
         got = swap(sent[0], blocks, rads, stride, 0)
         other = None if last else swap(sent[1], blocks, rads, stride, 1)
         residue = residue - got[:NRHS]
@@ -337,6 +340,10 @@
             tail = jnp.pad(g, ((0, 0), (0, residue.shape[1] - 128)))
             payload = jnp.concatenate([residue, tail], axis=0)
         slices = gather(payload, blocks, rads)
+        if last:
+            weights = prep_pivots(pivots, payload)
+        else:
+            weights = fetch(rung + 1, 1 if rung + 2 == levels else 2, couplings, payload)
     x, part, g = solve(slices, weights, krylov)
     part = part + swap(part, blocks, rads, 1, 0)
     chips = blocks // 2 * rads

time: 115 us -> 114 us (level)
  waiting for transfers between devices: 21.6 us -> 19.1 us
  starting transfers between devices: 54.4 us -> 56.6 us
    ppermute x18, waiting for transfers between devices: 12.6 us -> 5.88 us  [gather(): out.append(lax.ppermute(value, ALL, pairs))]
    ppermute x10, waiting for transfers between devices: 8.99 us -> 13.2 us  [swap(): return lax.ppermute(value, ALL, pairs)]
    ppermute x10, starting transfers between devices: 28.9 us -> 31.1 us  [swap(): return lax.ppermute(value, ALL, pairs)]
  transfers between devices with their start and end apart: 28 -> 28, of which waited for: 15 -> 10; matrix products, arithmetic and copies ran while one was open for 0% -> 0% of each run, Pallas kernels for 10% -> 10%
where the time goes in v2:
time: 114 us; the launch traced here: 113 us
  starting transfers between devices  56.6 us (50%)
  waiting for transfers between devices  19.1 us (17%)
  Pallas kernels  19 us (17%)
  blocking collectives  16.9 us (15%)
    ppermute x10, starting transfers between devices, swap(): return lax.ppermute(value, ALL, pairs)  31.1 us
    ppermute x18, starting transfers between devices, gather(): out.append(lax.ppermute(value, ALL, pairs))  25.5 us
    all_to_all x1, blocking collectives, step(): lax.all_to_all(jnp.broadcast_to(part[None], (chips,) + part.shape), ('chi...  16.9 us
    ppermute x10, waiting for transfers between devices, swap(): return lax.ppermute(value, ALL, pairs)  13.2 us
    pallas_call x5, Pallas kernels, fetch(): pl.pallas_call(functools.partial(fetch_kernel, rung, slots), out_shape=ma...  8.93 us
    ppermute x18, waiting for transfers between devices, gather(): out.append(lax.ppermute(value, ALL, pairs))  5.88 us
    pallas_call x5, Pallas kernels, level(): pl.pallas_call(functools.partial(level_kernel, rung, slots, points), out_...  4.49 us
  transfers between devices with their start and end apart: 28, of which 10 were waited for; matrix products, arithmetic and copies ran while one was open for 0% of the time, Pallas kernels for 10%

profile of v2, /device:TPU:1, one launch (start us, length us, event | category | flops | bytes accessed | tf_op | source)
XLA Modules:
  0.0 112.7 jit_solution(10253489369964907050)
XLA Ops:
  0.7 2.5 %collective-permute-start = (f32[32,432]{1,0:T(8,128)}, f32[32,432]{1,0:T(8,128)S(1)}, u32[]{:S(2)}, u32[]{:S(2)}) collective-permute-start(f32[32,432]{1,0:T(8,128)} %bitcast.5), channel_id=1, source_target_pairs={{0,1},{1,0},{2,3},{3,2},{4,5},{5,4},{6,7},{7,6},{8,9},{9,8},{10,11... | collective-permute-start | bytes 165896 | tf_op jit(solution)/shard_map/ppermute | solution.py:309
  3.2 3.3 %collective-permute-start.1 = (f32[32,432]{1,0:T(8,128)}, f32[32,432]{1,0:T(8,128)S(1)}, u32[]{:S(2)}, u32[]{:S(2)}) collective-permute-start(f32[32,432]{1,0:T(8,128)} %bitcast.6), channel_id=1, source_target_pairs={{0,2},{1,3},{2,0},{3,1},{4,6},{5,7},{6,4},{7,5},{8,10},{9,11},{10,... | collective-permute-start | bytes 165896 | tf_op jit(solution)/shard_map/ppermute | solution.py:309
  6.5 1.9 %shard_map.67.w_ref = bf16[2,432,1728]{2,1,0:T(8,128)(2,1)S(1)} custom-call(bf16[1,10,432,1728]{3,2,1,0:T(8,128)(2,1)} %couplings_ref.9), custom_call_target="tpu_custom_call" | custom-call | tf_op jit(solution)/shard_map/pallas_call | solution.py:107
  9.3 1.8 %collective-permute-done.2.s3 = f32[32,432]{1,0:T(8,128)S(1)} collective-permute-done((f32[32,432]{1,0:T(8,128)}, f32[32,432]{1,0:T(8,128)S(1)}, u32[]{:S(2)}, u32[]{:S(2)}) %collective-permute-start.2) | collective-permute-done | bytes 55328 | tf_op jit(solution)/shard_map/ppermute | solution.py:309
  12.2 2.3 %collective-permute-start.3 = (f32[24,432]{1,0:T(8,128)S(1)}, f32[24,432]{1,0:T(8,128)S(1)}, u32[]{:S(2)}, u32[]{:S(2)}) collective-permute-start(f32[24,432]{1,0:T(8,128)S(1)} %get-tuple-element.17), channel_id=1, source_target_pairs={{0,4},{1,5},{2,6},{3,7},{4,0},{5,1},{6,2},{7,3},{8,12},{9,13},{10,... | collective-permute-start | bytes 124424 | tf_op jit(solution)/shard_map/ppermute | solution.py:302
  15.8 2.1 %collective-permute-done.4 = f32[16,432]{1,0:T(8,128)S(1)} collective-permute-done((f32[16,432]{1,0:T(8,128)S(1)}, f32[16,432]{1,0:T(8,128)S(1)}, u32[]{:S(2)}, u32[]{:S(2)}) %collective-permute-start.4) | collective-permute-done | bytes 27680 | tf_op jit(solution)/shard_map/ppermute | solution.py:302
  18.9 2.9 %collective-permute-start.7 = (f32[16,432]{1,0:T(8,128)S(1)}, f32[16,432]{1,0:T(8,128)S(1)}, u32[]{:S(2)}, u32[]{:S(2)}) collective-permute-start(f32[16,432]{1,0:T(8,128)S(1)} %fusion.3.rest_0_.s0), channel_id=1, source_target_pairs={{0,3},{1,2},{2,1},{3,0},{4,7},{5,6},{6,5},{7,4},{8,11},{9,10},{10,... | collective-permute-start | bytes 82952 | tf_op jit(solution)/shard_map/ppermute | solution.py:309
  21.8 1.9 %shard_map.68.w_ref = bf16[2,432,1728]{2,1,0:T(8,128)(2,1)S(1)} custom-call(bf16[1,10,432,1728]{3,2,1,0:T(8,128)(2,1)} %couplings_ref.9, f32[16,432]{1,0:T(8,128)S(1)} %fusion.3.rest_0_.s0), custom_call_target="tpu_custom_call" | custom-call | tf_op jit(solution)/shard_map/pallas_call | solution.py:107
  26.1 7.0 %collective-permute-start.9 = (f32[16,432]{1,0:T(8,128)S(1)}, f32[16,432]{1,0:T(8,128)S(1)}, u32[]{:S(2)}, u32[]{:S(2)}) collective-permute-start(f32[16,432]{1,0:T(8,128)S(1)} %get-tuple-element.20), channel_id=1, source_target_pairs={{0,120},{1,121},{2,122},{3,123},{4,124},{5,125},{6,126},{7,127},{8... | collective-permute-start | bytes 82952 | tf_op jit(solution)/shard_map/ppermute | solution.py:302
  34.6 3.2 %collective-permute-start.11 = (f32[16,432]{1,0:T(8,128)S(1)}, f32[16,432]{1,0:T(8,128)S(1)}, u32[]{:S(2)}, u32[]{:S(2)}) collective-permute-start(f32[16,432]{1,0:T(8,128)S(1)} %fusion.2.rest_0_.s0), channel_id=1, source_target_pairs={{0,2},{1,3},{2,0},{3,1},{4,6},{5,7},{6,4},{7,5},{8,10},{9,11},{10,... | collective-permute-start | bytes 82952 | tf_op jit(solution)/shard_map/ppermute | solution.py:309
  38.4 1.9 %shard_map.69.w_ref = bf16[2,432,1728]{2,1,0:T(8,128)(2,1)S(1)} custom-call(bf16[1,10,432,1728]{3,2,1,0:T(8,128)(2,1)} %couplings_ref.9, f32[16,432]{1,0:T(8,128)S(1)} %fusion.2.rest_0_.s0), custom_call_target="tpu_custom_call" | custom-call | tf_op jit(solution)/shard_map/pallas_call | solution.py:107
  42.9 2.6 %collective-permute-start.14 = (f32[16,432]{1,0:T(8,128)S(1)}, f32[16,432]{1,0:T(8,128)S(1)}, u32[]{:S(2)}, u32[]{:S(2)}) collective-permute-start(f32[16,432]{1,0:T(8,128)S(1)} %get-tuple-element.22), channel_id=1, source_target_pairs={{0,112},{1,113},{2,114},{3,115},{4,116},{5,117},{6,118},{7,119},{8... | collective-permute-start | bytes 82952 | tf_op jit(solution)/shard_map/ppermute | solution.py:302
  45.5 3.8 %collective-permute-done.14 = f32[16,432]{1,0:T(8,128)S(1)} collective-permute-done((f32[16,432]{1,0:T(8,128)S(1)}, f32[16,432]{1,0:T(8,128)S(1)}, u32[]{:S(2)}, u32[]{:S(2)}) %collective-permute-start.14) | collective-permute-done | bytes 27680 | tf_op jit(solution)/shard_map/ppermute | solution.py:302
  51.2 2.1 %collective-permute-start.17 = (f32[16,432]{1,0:T(8,128)S(1)}, f32[16,432]{1,0:T(8,128)S(1)}, u32[]{:S(2)}, u32[]{:S(2)}) collective-permute-start(f32[16,432]{1,0:T(8,128)S(1)} %fusion.1.rest_0_.s0), channel_id=1, source_target_pairs={{0,3},{1,2},{2,1},{3,0},{4,7},{5,6},{6,5},{7,4},{8,11},{9,10},{10,... | collective-permute-start | bytes 82952 | tf_op jit(solution)/shard_map/ppermute | solution.py:309
  53.3 1.9 %shard_map.70.w_ref = bf16[2,432,1728]{2,1,0:T(8,128)(2,1)S(1)} custom-call(bf16[1,10,432,1728]{3,2,1,0:T(8,128)(2,1)} %couplings_ref.9, f32[16,432]{1,0:T(8,128)S(1)} %fusion.1.rest_0_.s0), custom_call_target="tpu_custom_call" | custom-call | tf_op jit(solution)/shard_map/pallas_call | solution.py:107
  56.3 2.0 %collective-permute-start.19 = (f32[16,432]{1,0:T(8,128)S(1)}, f32[16,432]{1,0:T(8,128)S(1)}, u32[]{:S(2)}, u32[]{:S(2)}) collective-permute-start(f32[16,432]{1,0:T(8,128)S(1)} %get-tuple-element.24), channel_id=1, source_target_pairs={{0,96},{1,97},{2,98},{3,99},{4,100},{5,101},{6,102},{7,103},{8,104... | collective-permute-start | bytes 82952 | tf_op jit(solution)/shard_map/ppermute | solution.py:302
  58.3 2.0 %collective-permute-done.19 = f32[16,432]{1,0:T(8,128)S(1)} collective-permute-done((f32[16,432]{1,0:T(8,128)S(1)}, f32[16,432]{1,0:T(8,128)S(1)}, u32[]{:S(2)}, u32[]{:S(2)}) %collective-permute-start.19) | collective-permute-done | bytes 27680 | tf_op jit(solution)/shard_map/ppermute | solution.py:302
  60.5 3.2 %collective-permute-start.21 = (f32[16,432]{1,0:T(8,128)S(1)}, f32[16,432]{1,0:T(8,128)S(1)}, u32[]{:S(2)}, u32[]{:S(2)}) collective-permute-start(f32[16,432]{1,0:T(8,128)S(1)} %fusion.rest_0_.s0), channel_id=1, source_target_pairs={{0,2},{1,3},{2,0},{3,1},{4,6},{5,7},{6,4},{7,5},{8,10},{9,11},{10,... | collective-permute-start | bytes 82952 | tf_op jit(solution)/shard_map/ppermute | solution.py:309
  65.8 2.0 %collective-permute-done.22.s3 = f32[16,432]{1,0:T(8,128)S(1)} collective-permute-done((f32[16,432]{1,0:T(8,128)S(1)}, f32[16,432]{1,0:T(8,128)S(1)}, u32[]{:S(2)}, u32[]{:S(2)}) %collective-permute-start.22) | collective-permute-done | bytes 27680 | tf_op jit(solution)/shard_map/ppermute | solution.py:309
  69.7 3.1 %collective-permute-done.23 = f32[24,432]{1,0:T(8,128)S(1)} collective-permute-done((f32[24,432]{1,0:T(8,128)S(1)}, f32[24,432]{1,0:T(8,128)S(1)}, u32[]{:S(2)}, u32[]{:S(2)}) %collective-permute-start.23) | collective-permute-done | bytes 41504 | tf_op jit(solution)/shard_map/ppermute | solution.py:302
  74.7 2.1 %collective-permute-start.26 = (f32[24,432]{1,0:T(8,128)S(1)}, f32[24,432]{1,0:T(8,128)S(1)}, u32[]{:S(2)}, u32[]{:S(2)}) collective-permute-start(f32[24,432]{1,0:T(8,128)S(1)} %select_maximum_fusion._.s0), channel_id=1, source_target_pairs={{0,3},{1,2},{2,1},{3,0},{4,7},{5,6},{6,5},{7,4},{8,11},{9,10},{10,... | collective-permute-start | bytes 124424 | tf_op jit(solution)/shard_map/ppermute | solution.py:309
  76.8 2.1 %prep_pivots.1.p_ref = bf16[2,432,1728]{2,1,0:T(8,128)(2,1)S(1)} custom-call(f32[1,432,1728]{2,1,0:T(8,128)} %pivots_ref.1, f32[24,432]{1,0:T(8,128)S(1)} %select_maximum_fusion._.s0), custom_call_target="tpu_custom_call" | custom-call | tf_op jit(solution)/shard_map/prep_pivots/pallas_call | solution.py:138
  80.4 12.8 %collective-permute-start.27 = (f32[8,128]{1,0:T(8,128)S(1)}, f32[8,128]{1,0:T(8,128)S(1)}, u32[]{:S(2)}, u32[]{:S(2)}) collective-permute-start(f32[8,128]{1,0:T(8,128)S(1)} %get-tuple-element.25), channel_id=1, source_target_pairs={{0,4},{1,5},{2,6},{3,7},{4,0},{5,1},{6,2},{7,3},{8,12},{9,13},{10,... | collective-permute-start | bytes 12296 | tf_op jit(solution)/shard_map/ppermute | solution.py:302
  94.1 16.9 %all_to_all.5.parts_ref = f32[64,8,128]{2,1,0:T(8,128)S(1)} all-to-all(f32[64,8,128]{2,1,0:T(8,128)S(1)} %broadcast_in_dim.14), channel_id=1, replica_groups=mesh['chip'=16,'core'=2,'rad'=4] {'chip','rad'}, dimensions={0} | all-to-all | bytes 524288 | tf_op jit(solution)/shard_map/all_to_all | solution.py:350
  (64 shorter events, 24.0 us)
Async XLA Ops:
  0.7 8.1 %collective-permute-start = (f32[32,432]{1,0:T(8,128)}, f32[32,432]{1,0:T(8,128)S(1)}, u32[]{:S(2)}, u32[]{:S(2)}) collective-permute-start(f32[32,432]{1,0:T(8,128)} %bitcast.5), channel_id=1, source_target_pairs={{0,1},{1,0},{2,3},{3,2},{4,5},{5,4},{6,7},{7,6},{8,9},{9,8},{10,11... | collective-permute-start | bytes 165896 | tf_op jit(solution)/shard_map/ppermute | solution.py:309
  3.2 6.1 %collective-permute-start.1 = (f32[32,432]{1,0:T(8,128)}, f32[32,432]{1,0:T(8,128)S(1)}, u32[]{:S(2)}, u32[]{:S(2)}) collective-permute-start(f32[32,432]{1,0:T(8,128)} %bitcast.6), channel_id=1, source_target_pairs={{0,2},{1,3},{2,0},{3,1},{4,6},{5,7},{6,4},{7,5},{8,10},{9,11},{10,... | collective-permute-start | bytes 165896 | tf_op jit(solution)/shard_map/ppermute | solution.py:309
  6.5 4.7 %collective-permute-start.2 = (f32[32,432]{1,0:T(8,128)}, f32[32,432]{1,0:T(8,128)S(1)}, u32[]{:S(2)}, u32[]{:S(2)}) collective-permute-start(f32[32,432]{1,0:T(8,128)} %bitcast.7), channel_id=1, source_target_pairs={{0,3},{1,2},{2,1},{3,0},{4,7},{5,6},{6,5},{7,4},{8,11},{9,10},{10,... | collective-permute-start | bytes 165896 | tf_op jit(solution)/shard_map/ppermute | solution.py:309
  12.2 5.7 %collective-permute-start.3 = (f32[24,432]{1,0:T(8,128)S(1)}, f32[24,432]{1,0:T(8,128)S(1)}, u32[]{:S(2)}, u32[]{:S(2)}) collective-permute-start(f32[24,432]{1,0:T(8,128)S(1)} %get-tuple-element.17), channel_id=1, source_target_pairs={{0,4},{1,5},{2,6},{3,7},{4,0},{5,1},{6,2},{7,3},{8,12},{9,13},{10,... | collective-permute-start | bytes 124424 | tf_op jit(solution)/shard_map/ppermute | solution.py:302
  17.9 5.8 %collective-permute-start.5 = (f32[16,432]{1,0:T(8,128)S(1)}, f32[16,432]{1,0:T(8,128)S(1)}, u32[]{:S(2)}, u32[]{:S(2)}) collective-permute-start(f32[16,432]{1,0:T(8,128)S(1)} %fusion.3.rest_0_.s0), channel_id=1, source_target_pairs={{0,1},{1,0},{2,3},{3,2},{4,5},{5,4},{6,7},{7,6},{8,9},{9,8},{10,11... | collective-permute-start | bytes 82952 | tf_op jit(solution)/shard_map/ppermute | solution.py:309
  18.0 5.8 %collective-permute-start.6 = (f32[16,432]{1,0:T(8,128)S(1)}, f32[16,432]{1,0:T(8,128)S(1)}, u32[]{:S(2)}, u32[]{:S(2)}) collective-permute-start(f32[16,432]{1,0:T(8,128)S(1)} %fusion.3.rest_0_.s0), channel_id=1, source_target_pairs={{0,2},{1,3},{2,0},{3,1},{4,6},{5,7},{6,4},{7,5},{8,10},{9,11},{10,... | collective-permute-start | bytes 82952 | tf_op jit(solution)/shard_map/ppermute | solution.py:309
  18.9 4.8 %collective-permute-start.7 = (f32[16,432]{1,0:T(8,128)S(1)}, f32[16,432]{1,0:T(8,128)S(1)}, u32[]{:S(2)}, u32[]{:S(2)}) collective-permute-start(f32[16,432]{1,0:T(8,128)S(1)} %fusion.3.rest_0_.s0), channel_id=1, source_target_pairs={{0,3},{1,2},{2,1},{3,0},{4,7},{5,6},{6,5},{7,4},{8,11},{9,10},{10,... | collective-permute-start | bytes 82952 | tf_op jit(solution)/shard_map/ppermute | solution.py:309
  24.8 9.7 %collective-permute-start.8 = (f32[24,432]{1,0:T(8,128)S(1)}, f32[24,432]{1,0:T(8,128)S(1)}, u32[]{:S(2)}, u32[]{:S(2)}) collective-permute-start(f32[24,432]{1,0:T(8,128)S(1)} %get-tuple-element.19), channel_id=1, source_target_pairs={{0,8},{1,9},{2,10},{3,11},{4,12},{5,13},{6,14},{7,15},{8,0},{9,1},... | collective-permute-start | bytes 124424 | tf_op jit(solution)/shard_map/ppermute | solution.py:302
  26.1 8.4 %collective-permute-start.9 = (f32[16,432]{1,0:T(8,128)S(1)}, f32[16,432]{1,0:T(8,128)S(1)}, u32[]{:S(2)}, u32[]{:S(2)}) collective-permute-start(f32[16,432]{1,0:T(8,128)S(1)} %get-tuple-element.20), channel_id=1, source_target_pairs={{0,120},{1,121},{2,122},{3,123},{4,124},{5,125},{6,126},{7,127},{8... | collective-permute-start | bytes 82952 | tf_op jit(solution)/shard_map/ppermute | solution.py:302
  34.5 5.8 %collective-permute-start.10 = (f32[16,432]{1,0:T(8,128)S(1)}, f32[16,432]{1,0:T(8,128)S(1)}, u32[]{:S(2)}, u32[]{:S(2)}) collective-permute-start(f32[16,432]{1,0:T(8,128)S(1)} %fusion.2.rest_0_.s0), channel_id=1, source_target_pairs={{0,1},{1,0},{2,3},{3,2},{4,5},{5,4},{6,7},{7,6},{8,9},{9,8},{10,11... | collective-permute-start | bytes 82952 | tf_op jit(solution)/shard_map/ppermute | solution.py:309
  34.6 5.8 %collective-permute-start.11 = (f32[16,432]{1,0:T(8,128)S(1)}, f32[16,432]{1,0:T(8,128)S(1)}, u32[]{:S(2)}, u32[]{:S(2)}) collective-permute-start(f32[16,432]{1,0:T(8,128)S(1)} %fusion.2.rest_0_.s0), channel_id=1, source_target_pairs={{0,2},{1,3},{2,0},{3,1},{4,6},{5,7},{6,4},{7,5},{8,10},{9,11},{10,... | collective-permute-start | bytes 82952 | tf_op jit(solution)/shard_map/ppermute | solution.py:309
  42.8 6.6 %collective-permute-start.13 = (f32[24,432]{1,0:T(8,128)S(1)}, f32[24,432]{1,0:T(8,128)S(1)}, u32[]{:S(2)}, u32[]{:S(2)}) collective-permute-start(f32[24,432]{1,0:T(8,128)S(1)} %get-tuple-element.21), channel_id=1, source_target_pairs={{0,16},{1,17},{2,18},{3,19},{4,20},{5,21},{6,22},{7,23},{8,24},{9,... | collective-permute-start | bytes 124424 | tf_op jit(solution)/shard_map/ppermute | solution.py:302
  42.9 6.5 %collective-permute-start.14 = (f32[16,432]{1,0:T(8,128)S(1)}, f32[16,432]{1,0:T(8,128)S(1)}, u32[]{:S(2)}, u32[]{:S(2)}) collective-permute-start(f32[16,432]{1,0:T(8,128)S(1)} %get-tuple-element.22), channel_id=1, source_target_pairs={{0,112},{1,113},{2,114},{3,115},{4,116},{5,117},{6,118},{7,119},{8... | collective-permute-start | bytes 82952 | tf_op jit(solution)/shard_map/ppermute | solution.py:302
  49.3 5.8 %collective-permute-start.15 = (f32[16,432]{1,0:T(8,128)S(1)}, f32[16,432]{1,0:T(8,128)S(1)}, u32[]{:S(2)}, u32[]{:S(2)}) collective-permute-start(f32[16,432]{1,0:T(8,128)S(1)} %fusion.1.rest_0_.s0), channel_id=1, source_target_pairs={{0,1},{1,0},{2,3},{3,2},{4,5},{5,4},{6,7},{7,6},{8,9},{9,8},{10,11... | collective-permute-start | bytes 82952 | tf_op jit(solution)/shard_map/ppermute | solution.py:309
  49.4 5.8 %collective-permute-start.16 = (f32[16,432]{1,0:T(8,128)S(1)}, f32[16,432]{1,0:T(8,128)S(1)}, u32[]{:S(2)}, u32[]{:S(2)}) collective-permute-start(f32[16,432]{1,0:T(8,128)S(1)} %fusion.1.rest_0_.s0), channel_id=1, source_target_pairs={{0,2},{1,3},{2,0},{3,1},{4,6},{5,7},{6,4},{7,5},{8,10},{9,11},{10,... | collective-permute-start | bytes 82952 | tf_op jit(solution)/shard_map/ppermute | solution.py:309
  56.2 4.2 %collective-permute-start.18 = (f32[24,432]{1,0:T(8,128)S(1)}, f32[24,432]{1,0:T(8,128)S(1)}, u32[]{:S(2)}, u32[]{:S(2)}) collective-permute-start(f32[24,432]{1,0:T(8,128)S(1)} %get-tuple-element.23), channel_id=1, source_target_pairs={{0,32},{1,33},{2,34},{3,35},{4,36},{5,37},{6,38},{7,39},{8,40},{9,... | collective-permute-start | bytes 124424 | tf_op jit(solution)/shard_map/ppermute | solution.py:302
  60.4 5.4 %collective-permute-start.20 = (f32[16,432]{1,0:T(8,128)S(1)}, f32[16,432]{1,0:T(8,128)S(1)}, u32[]{:S(2)}, u32[]{:S(2)}) collective-permute-start(f32[16,432]{1,0:T(8,128)S(1)} %fusion.rest_0_.s0), channel_id=1, source_target_pairs={{0,1},{1,0},{2,3},{3,2},{4,5},{5,4},{6,7},{7,6},{8,9},{9,8},{10,11... | collective-permute-start | bytes 82952 | tf_op jit(solution)/shard_map/ppermute | solution.py:309
  60.5 5.3 %collective-permute-start.21 = (f32[16,432]{1,0:T(8,128)S(1)}, f32[16,432]{1,0:T(8,128)S(1)}, u32[]{:S(2)}, u32[]{:S(2)}) collective-permute-start(f32[16,432]{1,0:T(8,128)S(1)} %fusion.rest_0_.s0), channel_id=1, source_target_pairs={{0,2},{1,3},{2,0},{3,1},{4,6},{5,7},{6,4},{7,5},{8,10},{9,11},{10,... | collective-permute-start | bytes 82952 | tf_op jit(solution)/shard_map/ppermute | solution.py:309
  63.7 4.1 %collective-permute-start.22 = (f32[16,432]{1,0:T(8,128)S(1)}, f32[16,432]{1,0:T(8,128)S(1)}, u32[]{:S(2)}, u32[]{:S(2)}) collective-permute-start(f32[16,432]{1,0:T(8,128)S(1)} %fusion.rest_0_.s0), channel_id=1, source_target_pairs={{0,3},{1,2},{2,1},{3,0},{4,7},{5,6},{6,5},{7,4},{8,11},{9,10},{10,... | collective-permute-start | bytes 82952 | tf_op jit(solution)/shard_map/ppermute | solution.py:309
  68.4 4.5 %collective-permute-start.23 = (f32[24,432]{1,0:T(8,128)S(1)}, f32[24,432]{1,0:T(8,128)S(1)}, u32[]{:S(2)}, u32[]{:S(2)}) collective-permute-start(f32[24,432]{1,0:T(8,128)S(1)} %level.9), channel_id=1, source_target_pairs={{0,64},{1,65},{2,66},{3,67},{4,68},{5,69},{6,70},{7,71},{8,72},{9,... | collective-permute-start | bytes 124424 | tf_op jit(solution)/shard_map/ppermute | solution.py:302
  72.9 6.1 %collective-permute-start.24 = (f32[24,432]{1,0:T(8,128)S(1)}, f32[24,432]{1,0:T(8,128)S(1)}, u32[]{:S(2)}, u32[]{:S(2)}) collective-permute-start(f32[24,432]{1,0:T(8,128)S(1)} %select_maximum_fusion._.s0), channel_id=1, source_target_pairs={{0,1},{1,0},{2,3},{3,2},{4,5},{5,4},{6,7},{7,6},{8,9},{9,8},{10,11... | collective-permute-start | bytes 124424 | tf_op jit(solution)/shard_map/ppermute | solution.py:309
  73.0 6.0 %collective-permute-start.25 = (f32[24,432]{1,0:T(8,128)S(1)}, f32[24,432]{1,0:T(8,128)S(1)}, u32[]{:S(2)}, u32[]{:S(2)}) collective-permute-start(f32[24,432]{1,0:T(8,128)S(1)} %select_maximum_fusion._.s0), channel_id=1, source_target_pairs={{0,2},{1,3},{2,0},{3,1},{4,6},{5,7},{6,4},{7,5},{8,10},{9,11},{10,... | collective-permute-start | bytes 124424 | tf_op jit(solution)/shard_map/ppermute | solution.py:309
  74.7 4.3 %collective-permute-start.26 = (f32[24,432]{1,0:T(8,128)S(1)}, f32[24,432]{1,0:T(8,128)S(1)}, u32[]{:S(2)}, u32[]{:S(2)}) collective-permute-start(f32[24,432]{1,0:T(8,128)S(1)} %select_maximum_fusion._.s0), channel_id=1, source_target_pairs={{0,3},{1,2},{2,1},{3,0},{4,7},{5,6},{6,5},{7,4},{8,11},{9,10},{10,... | collective-permute-start | bytes 124424 | tf_op jit(solution)/shard_map/ppermute | solution.py:309
  80.4 13.7 %collective-permute-start.27 = (f32[8,128]{1,0:T(8,128)S(1)}, f32[8,128]{1,0:T(8,128)S(1)}, u32[]{:S(2)}, u32[]{:S(2)}) collective-permute-start(f32[8,128]{1,0:T(8,128)S(1)} %get-tuple-element.25), channel_id=1, source_target_pairs={{0,4},{1,5},{2,6},{3,7},{4,0},{5,1},{6,2},{7,3},{8,12},{9,13},{10,... | collective-permute-start | bytes 12296 | tf_op jit(solution)/shard_map/ppermute | solution.py:302
  (6 other events, 33.6 us)

commit v3 on v2

--- a/solution.py
+++ b/solution.py
@@ -155,45 +155,98 @@
     return jnp.concatenate(split2(v), axis=0)
 
 
-def level_kernel(rung, slots, points, s0, s1, s2, s3, w_ref, masks_ref, *rest):
-    g_ref = rest[0] if len(rest) == slots + 2 else None
-    outs, whole = rest[-slots - 1 : -1], rest[-1]
-    if g_ref is None:
-        stored = s0[...]
-        product = nt_dot(stored, stored, precise)
-        g = jnp.concatenate([product[8 * i : 8 * i + 8] for i in range(4)], axis=1)
-    else:
-        g = g_ref[...]
-    lhs = gather_rows((s0, s1, s2, s3), whole)
+OUTER = ((0, (("s", 0), 80)), (1280, (16, ("s", 3))))
+INNER = ((384, (48, ("s", 1), ("s", 2), 112)),)
+
+
+def half_push(kind, points, ranges, w_ref, slot, masks_ref, whole):
     spanned = masks_ref.shape[0]
     rows = w_ref.shape[1]
+    product = None
+    for start, items in ranges:
+        pieces = [
+            whole[item[1]] if isinstance(item, tuple) else jnp.zeros((NRHS, item), jnp.float32)
+            for item in items
+        ]
+        lhs = jnp.concatenate(split2(jnp.concatenate(pieces, axis=1)), axis=0)
+        size = lhs.shape[1]
+        parts = []
+        for local in range(spanned):
+            keep = masks_ref[local, pl.ds(kind, 1), start : start + size]
+            keep = jnp.broadcast_to(keep, (16, size)).astype(jnp.bfloat16)
+            parts.append(lhs * jnp.concatenate([keep, keep], axis=0))
+        one = nt_dot(jnp.concatenate(parts, axis=0), w_ref[slot, :, start : start + size])
+        product = one if product is None else product + one
     offset = lax.axis_index("rad") * rows
     first = offset // points
     row = offset + lax.broadcasted_iota(jnp.int32, (NRHS, rows), 1)
-    for slot in range(slots):
-        kind = kind_of(rung, slot)
-        parts = []
-        for local in range(spanned):
-            keep = masks_ref[local, pl.ds(kind, 1), :]
-            keep = jnp.broadcast_to(keep, (16, keep.shape[1])).astype(jnp.bfloat16)
-            parts.append(lhs * jnp.concatenate([keep, keep], axis=0))
-        product = nt_dot(jnp.concatenate(parts, axis=0), w_ref[slot])
-        push = None
-        for local in reversed(range(spanned)):
-            at = 2 * NRHS * local
-            one = product[at : at + NRHS] + product[at + NRHS : at + 2 * NRHS]
-            push = one if push is None else jnp.where(row < (first + local + 1) * points, one, push)
-        outs[slot][:NRHS, :] = push
-    outs[0][NRHS:, :128] = g
+    push = None
+    for local in reversed(range(spanned)):
+        at = 2 * NRHS * local
+        one = product[at : at + NRHS] + product[at + NRHS : at + 2 * NRHS]
+        push = one if push is None else jnp.where(row < (first + local + 1) * points, one, push)
+    return push
+
+
+def near_half_kernel(rung, slots, points, s0, s3, w_ref, masks_ref, *rest):
+    outs, whole = rest[:-1], rest[-1]
+    rad = lax.axis_index("rad")
+    for m, piece in ((0, s0), (3, s3)):
+        whole[rad ^ m] = piece[piece.shape[0] - NRHS :, :]
+    if len(outs) > slots:
+        stored = s0[...]
+        product = nt_dot(stored, stored, precise)
+        outs[slots][...] = jnp.concatenate([product[8 * i : 8 * i + 8] for i in range(4)], axis=1)
+
+    def run(ranges):
+        for slot in range(slots):
+            outs[slot][...] = half_push(
+                kind_of(rung, slot), points, ranges, w_ref, slot, masks_ref, whole
+            )
+
+    edge = (rad == 0) | (rad == 3)
+    pl.when(edge)(lambda: run(OUTER))
+    pl.when(jnp.logical_not(edge))(lambda: run(INNER))
+
+
+def far_half_kernel(rung, slots, points, s1, s2, w_ref, masks_ref, g_ref, *rest):
+    halves, outs, whole = rest[:slots], rest[slots:-1], rest[-1]
+    rad = lax.axis_index("rad")
+    for m, piece in ((1, s1), (2, s2)):
+        whole[rad ^ m] = piece[piece.shape[0] - NRHS :, :]
+
+    def run(ranges):
+        for slot in range(slots):
+            push = half_push(kind_of(rung, slot), points, ranges, w_ref, slot, masks_ref, whole)
+            outs[slot][:NRHS, :] = push + halves[slot][...]
+
+    edge = (rad == 0) | (rad == 3)
+    pl.when(edge)(lambda: run(INNER))
+    pl.when(jnp.logical_not(edge))(lambda: run(OUTER))
+    outs[0][NRHS:, :128] = g_ref[...]
     outs[0][NRHS:, 128:] = jnp.zeros((8, outs[0].shape[1] - 128), jnp.float32)
 
 
-def level(rung, slots, points, slices, weights, masks, g):
+def near_half(rung, slots, points, own, third, weights, masks):
     rows = weights.shape[1]
-    args = (*slices, weights, masks) if g is None else (*slices, weights, masks, g)
+    shapes = [(NRHS, rows)] * slots + [(8, 128)] * (rung == 0)
+    return pl.pallas_call(
+        functools.partial(near_half_kernel, rung, slots, points),
+        out_shape=[made(s) for s in shapes],
+        in_specs=[VMEM] * 4,
+        out_specs=[VMEM] * len(shapes),
+        scratch_shapes=[pltpu.VMEM((4, NRHS, rows), jnp.float32)],
+        compiler_params=pltpu.CompilerParams(vmem_limit_bytes=4 << 20),
+        name="nearhalf",
+    )(*map(near, (own, third, weights, masks)))
+
+
+def level(rung, slots, points, slices, weights, masks, g, halves):
+    rows = weights.shape[1]
+    args = (slices[1], slices[2], weights, masks, g, *halves)
     shapes = [(NRHS + 8, rows), (NRHS, rows)][:slots]
     return pl.pallas_call(
-        functools.partial(level_kernel, rung, slots, points),
+        functools.partial(far_half_kernel, rung, slots, points),
         out_shape=[made(s) for s in shapes],
         in_specs=[VMEM] * len(args),
         out_specs=[VMEM] * slots,
@@ -321,16 +374,21 @@
     weights = fetch(0, 2, couplings)
     masks = make_masks(pattern, couplings.shape[2], width)
     points = width // pattern.shape[0]
-    g = None
     residue = krylov[0, krylov.shape[1] - NRHS :, :]
     for rung in range(levels):
         stride = 1 << rung
         last = rung == levels - 1
-        sent = level(rung, 1 if last else 2, points, slices, weights, masks, g)
+        slots = 1 if last else 2
+        halves = near_half(rung, slots, points, slices[0], slices[3], weights, masks)
+        if rung == 0:
+            g = halves[slots]
+        sent = level(rung, slots, points, slices, weights, masks, g, halves[:slots])
+        if not last:
+            weights = fetch(rung + 1, 1 if rung + 2 == levels else 2, couplings, sent[0])
         got = swap(sent[0], blocks, rads, stride, 0)
         other = None if last else swap(sent[1], blocks, rads, stride, 1)
         residue = residue - got[:NRHS]
-        g = (sent[0][NRHS:, :128] if g is None else g) + got[NRHS:, :128]
+        g = g + got[NRHS:, :128]
         if not last:
             place = block // stride
             inside = jnp.where(place % 2 == 0, place > 0, place < blocks // stride - 1)
@@ -342,8 +400,6 @@
         slices = gather(payload, blocks, rads)
         if last:
             weights = prep_pivots(pivots, payload)
-        else:
-            weights = fetch(rung + 1, 1 if rung + 2 == levels else 2, couplings, payload)
     x, part, g = solve(slices, weights, krylov)
     part = part + swap(part, blocks, rads, 1, 0)
     chips = blocks // 2 * rads

time: 114 us -> 113 us (level)
  Pallas kernels: 19 us -> 20.9 us
  blocking collectives: 16.9 us -> 15 us
  starting transfers between devices: 56.6 us -> 54.9 us
  waiting for transfers between devices: 19.1 us -> 20.5 us
    ppermute x18, waiting for transfers between devices: 5.88 us -> 11.7 us  [gather(): out.append(lax.ppermute(value, ALL, pairs))]
    ppermute x10, waiting for transfers between devices: 13.2 us -> 8.84 us  [swap(): return lax.ppermute(value, ALL, pairs)]
    ppermute x10, starting transfers between devices: 31.1 us -> 28.8 us  [swap(): return lax.ppermute(value, ALL, pairs)]
    pallas_call x5 -> x10, Pallas kernels: 4.49 us -> 6.4 us  [the longest x5 3.25 us: near_half(): pl.pallas_call(functools.partial(near_half_kernel, rung, slots, points),...]
    all_to_all x1, blocking collectives: 16.9 us -> 15 us  [step(): lax.all_to_all(jnp.broadcast_to(part[None], (chips,) + part.shape), ('chi...]
  transfers between devices with their start and end apart: 28 -> 28, of which waited for: 10 -> 11; matrix products, arithmetic and copies ran while one was open for 0% -> 0% of each run, Pallas kernels for 10% -> 13%
where the time goes in v3:
time: 113 us
  starting transfers between devices  54.9 us (49%)
  Pallas kernels  20.9 us (18%)
  waiting for transfers between devices  20.5 us (18%)
  blocking collectives  15 us (13%)
    ppermute x10, starting transfers between devices, swap(): return lax.ppermute(value, ALL, pairs)  28.8 us
    ppermute x18, starting transfers between devices, gather(): out.append(lax.ppermute(value, ALL, pairs))  26.1 us
    all_to_all x1, blocking collectives, step(): lax.all_to_all(jnp.broadcast_to(part[None], (chips,) + part.shape), ('chi...  15 us
    ppermute x18, waiting for transfers between devices, gather(): out.append(lax.ppermute(value, ALL, pairs))  11.7 us
    pallas_call x5, Pallas kernels, fetch(): pl.pallas_call(functools.partial(fetch_kernel, rung, slots), out_shape=ma...  8.93 us
    ppermute x10, waiting for transfers between devices, swap(): return lax.ppermute(value, ALL, pairs)  8.84 us
    pallas_call x5, Pallas kernels, near_half(): pl.pallas_call(functools.partial(near_half_kernel, rung, slots, points),...  3.25 us
    pallas_call x5, Pallas kernels, level(): pl.pallas_call(functools.partial(far_half_kernel, rung, slots, points), o...  3.15 us
  transfers between devices with their start and end apart: 28, of which 11 were waited for; matrix products, arithmetic and copies ran while one was open for 0% of the time, Pallas kernels for 13%

profile of v3, /device:TPU:1, one launch (start us, length us, event | category | flops | bytes accessed | tf_op | source)
XLA Modules:
  0.0 112.5 jit_solution(6478815589678239872)
XLA Ops:
  0.7 4.7 %collective-permute-start.2 = (f32[32,432]{1,0:T(8,128)}, f32[32,432]{1,0:T(8,128)S(1)}, u32[]{:S(2)}, u32[]{:S(2)}) collective-permute-start(f32[32,432]{1,0:T(8,128)} %bitcast.5), channel_id=1, source_target_pairs={{0,3},{1,2},{2,1},{3,0},{4,7},{5,6},{6,5},{7,4},{8,11},{9,10},{10,... | collective-permute-start | bytes 165896 | tf_op jit(solution)/shard_map/ppermute | solution.py:362
  6.6 1.9 %shard_map.67.w_ref = bf16[2,432,1728]{2,1,0:T(8,128)(2,1)S(1)} custom-call(bf16[1,10,432,1728]{3,2,1,0:T(8,128)(2,1)} %couplings_ref.9), custom_call_target="tpu_custom_call" | custom-call | tf_op jit(solution)/shard_map/pallas_call | solution.py:107
  11.0 2.0 %collective-permute-start.3 = (f32[24,432]{1,0:T(8,128)S(1)}, f32[24,432]{1,0:T(8,128)S(1)}, u32[]{:S(2)}, u32[]{:S(2)}) collective-permute-start(f32[24,432]{1,0:T(8,128)S(1)} %get-tuple-element.29.rest_0_), channel_id=1, source_target_pairs={{0,4},{1,5},{2,6},{3,7},{4,0},{5,1},{6,2},{7,3},{8,12},{9,13},{10,... | collective-permute-start | bytes 124424 | tf_op jit(solution)/shard_map/ppermute | solution.py:355
  14.3 1.9 %shard_map.68.w_ref = bf16[2,432,1728]{2,1,0:T(8,128)(2,1)S(1)} custom-call(bf16[1,10,432,1728]{3,2,1,0:T(8,128)(2,1)} %couplings_ref.9, f32[24,432]{1,0:T(8,128)S(1)} %get-tuple-element.29.rest_0_), custom_call_target="tpu_custom_call" | custom-call | tf_op jit(solution)/shard_map/pallas_call | solution.py:107
  16.4 1.8 %collective-permute-start.5 = (f32[16,432]{1,0:T(8,128)S(1)}, f32[16,432]{1,0:T(8,128)S(1)}, u32[]{:S(2)}, u32[]{:S(2)}) collective-permute-start(f32[16,432]{1,0:T(8,128)S(1)} %fusion.3.s0), channel_id=1, source_target_pairs={{0,1},{1,0},{2,3},{3,2},{4,5},{5,4},{6,7},{7,6},{8,9},{9,8},{10,11... | collective-permute-start | bytes 82952 | tf_op jit(solution)/shard_map/ppermute | solution.py:362
  20.7 2.5 %collective-permute-done.7.s3 = f32[16,432]{1,0:T(8,128)S(1)} collective-permute-done((f32[16,432]{1,0:T(8,128)S(1)}, f32[16,432]{1,0:T(8,128)S(1)}, u32[]{:S(2)}, u32[]{:S(2)}) %collective-permute-start.7) | collective-permute-done | bytes 27680 | tf_op jit(solution)/shard_map/ppermute | solution.py:362
  24.6 1.7 %collective-permute-start.8 = (f32[24,432]{1,0:T(8,128)S(1)}, f32[24,432]{1,0:T(8,128)S(1)}, u32[]{:S(2)}, u32[]{:S(2)}) collective-permute-start(f32[24,432]{1,0:T(8,128)S(1)} %get-tuple-element.33.rest_0_), channel_id=1, source_target_pairs={{0,8},{1,9},{2,10},{3,11},{4,12},{5,13},{6,14},{7,15},{8,0},{9,1},... | collective-permute-start | bytes 124424 | tf_op jit(solution)/shard_map/ppermute | solution.py:355
  26.3 6.7 %collective-permute-start.9 = (f32[16,432]{1,0:T(8,128)S(1)}, f32[16,432]{1,0:T(8,128)S(1)}, u32[]{:S(2)}, u32[]{:S(2)}) collective-permute-start(f32[16,432]{1,0:T(8,128)S(1)} %get-tuple-element.34), channel_id=1, source_target_pairs={{0,120},{1,121},{2,122},{3,123},{4,124},{5,125},{6,126},{7,127},{8... | collective-permute-start | bytes 82952 | tf_op jit(solution)/shard_map/ppermute | solution.py:355
  33.0 1.9 %shard_map.69.w_ref = bf16[2,432,1728]{2,1,0:T(8,128)(2,1)S(1)} custom-call(bf16[1,10,432,1728]{3,2,1,0:T(8,128)(2,1)} %couplings_ref.9, f32[24,432]{1,0:T(8,128)S(1)} %get-tuple-element.33.rest_0_), custom_call_target="tpu_custom_call" | custom-call | tf_op jit(solution)/shard_map/pallas_call | solution.py:107
  35.0 2.6 %collective-permute-start.11 = (f32[16,432]{1,0:T(8,128)S(1)}, f32[16,432]{1,0:T(8,128)S(1)}, u32[]{:S(2)}, u32[]{:S(2)}) collective-permute-start(f32[16,432]{1,0:T(8,128)S(1)} %fusion.2.s0), channel_id=1, source_target_pairs={{0,2},{1,3},{2,0},{3,1},{4,6},{5,7},{6,4},{7,5},{8,10},{9,11},{10,... | collective-permute-start | bytes 82952 | tf_op jit(solution)/shard_map/ppermute | solution.py:362
  38.9 2.7 %collective-permute-done.12.s3 = f32[16,432]{1,0:T(8,128)S(1)} collective-permute-done((f32[16,432]{1,0:T(8,128)S(1)}, f32[16,432]{1,0:T(8,128)S(1)}, u32[]{:S(2)}, u32[]{:S(2)}) %collective-permute-start.12) | collective-permute-done | bytes 27680 | tf_op jit(solution)/shard_map/ppermute | solution.py:362
  43.1 2.0 %collective-permute-start.14 = (f32[16,432]{1,0:T(8,128)S(1)}, f32[16,432]{1,0:T(8,128)S(1)}, u32[]{:S(2)}, u32[]{:S(2)}) collective-permute-start(f32[16,432]{1,0:T(8,128)S(1)} %get-tuple-element.38), channel_id=1, source_target_pairs={{0,112},{1,113},{2,114},{3,115},{4,116},{5,117},{6,118},{7,119},{8... | collective-permute-start | bytes 82952 | tf_op jit(solution)/shard_map/ppermute | solution.py:355
  45.1 1.9 %shard_map.70.w_ref = bf16[2,432,1728]{2,1,0:T(8,128)(2,1)S(1)} custom-call(bf16[1,10,432,1728]{3,2,1,0:T(8,128)(2,1)} %couplings_ref.9, f32[24,432]{1,0:T(8,128)S(1)} %get-tuple-element.37.rest_0_), custom_call_target="tpu_custom_call" | custom-call | tf_op jit(solution)/shard_map/pallas_call | solution.py:107
  47.0 2.5 %collective-permute-done.14 = f32[16,432]{1,0:T(8,128)S(1)} collective-permute-done((f32[16,432]{1,0:T(8,128)S(1)}, f32[16,432]{1,0:T(8,128)S(1)}, u32[]{:S(2)}, u32[]{:S(2)}) %collective-permute-start.14) | collective-permute-done | bytes 27680 | tf_op jit(solution)/shard_map/ppermute | solution.py:355
  49.6 2.4 %collective-permute-start.16 = (f32[16,432]{1,0:T(8,128)S(1)}, f32[16,432]{1,0:T(8,128)S(1)}, u32[]{:S(2)}, u32[]{:S(2)}) collective-permute-start(f32[16,432]{1,0:T(8,128)S(1)} %fusion.1.s0), channel_id=1, source_target_pairs={{0,2},{1,3},{2,0},{3,1},{4,6},{5,7},{6,4},{7,5},{8,10},{9,11},{10,... | collective-permute-start | bytes 82952 | tf_op jit(solution)/shard_map/ppermute | solution.py:362
  53.5 2.5 %collective-permute-done.17.s3 = f32[16,432]{1,0:T(8,128)S(1)} collective-permute-done((f32[16,432]{1,0:T(8,128)S(1)}, f32[16,432]{1,0:T(8,128)S(1)}, u32[]{:S(2)}, u32[]{:S(2)}) %collective-permute-start.17) | collective-permute-done | bytes 27680 | tf_op jit(solution)/shard_map/ppermute | solution.py:362
  61.9 2.6 %collective-permute-start.21 = (f32[16,432]{1,0:T(8,128)S(1)}, f32[16,432]{1,0:T(8,128)S(1)}, u32[]{:S(2)}, u32[]{:S(2)}) collective-permute-start(f32[16,432]{1,0:T(8,128)S(1)} %fusion.s0), channel_id=1, source_target_pairs={{0,2},{1,3},{2,0},{3,1},{4,6},{5,7},{6,4},{7,5},{8,10},{9,11},{10,... | collective-permute-start | bytes 82952 | tf_op jit(solution)/shard_map/ppermute | solution.py:362
  65.7 2.7 %collective-permute-done.22.s3 = f32[16,432]{1,0:T(8,128)S(1)} collective-permute-done((f32[16,432]{1,0:T(8,128)S(1)}, f32[16,432]{1,0:T(8,128)S(1)}, u32[]{:S(2)}, u32[]{:S(2)}) %collective-permute-start.22) | collective-permute-done | bytes 27680 | tf_op jit(solution)/shard_map/ppermute | solution.py:362
  70.2 3.6 %collective-permute-done.23 = f32[24,432]{1,0:T(8,128)S(1)} collective-permute-done((f32[24,432]{1,0:T(8,128)S(1)}, f32[24,432]{1,0:T(8,128)S(1)}, u32[]{:S(2)}, u32[]{:S(2)}) %collective-permute-start.23) | collective-permute-done | bytes 41504 | tf_op jit(solution)/shard_map/ppermute | solution.py:355
  74.0 2.4 %collective-permute-start.25 = (f32[24,432]{1,0:T(8,128)S(1)}, f32[24,432]{1,0:T(8,128)S(1)}, u32[]{:S(2)}, u32[]{:S(2)}) collective-permute-start(f32[24,432]{1,0:T(8,128)S(1)} %select_maximum_fusion._.s0), channel_id=1, source_target_pairs={{0,2},{1,3},{2,0},{3,1},{4,6},{5,7},{6,4},{7,5},{8,10},{9,11},{10,... | collective-permute-start | bytes 124424 | tf_op jit(solution)/shard_map/ppermute | solution.py:362
  77.8 2.1 %prep_pivots.1.p_ref = bf16[2,432,1728]{2,1,0:T(8,128)(2,1)S(1)} custom-call(f32[1,432,1728]{2,1,0:T(8,128)} %pivots_ref.1, f32[24,432]{1,0:T(8,128)S(1)} %select_maximum_fusion._.s0), custom_call_target="tpu_custom_call" | custom-call | tf_op jit(solution)/shard_map/prep_pivots/pallas_call | solution.py:138
  82.0 13.0 %collective-permute-start.27 = (f32[8,128]{1,0:T(8,128)S(1)}, f32[8,128]{1,0:T(8,128)S(1)}, u32[]{:S(2)}, u32[]{:S(2)}) collective-permute-start(f32[8,128]{1,0:T(8,128)S(1)} %get-tuple-element.43), channel_id=1, source_target_pairs={{0,4},{1,5},{2,6},{3,7},{4,0},{5,1},{6,2},{7,3},{8,12},{9,13},{10,... | collective-permute-start | bytes 12296 | tf_op jit(solution)/shard_map/ppermute | solution.py:355
  95.8 15.0 %all_to_all.5.parts_ref = f32[64,8,128]{2,1,0:T(8,128)S(1)} all-to-all(f32[64,8,128]{2,1,0:T(8,128)S(1)} %broadcast_in_dim.14), channel_id=1, replica_groups=mesh['chip'=16,'core'=2,'rad'=4] {'chip','rad'}, dimensions={0} | all-to-all | bytes 524288 | tf_op jit(solution)/shard_map/all_to_all | solution.py:406
  110.9 1.7 %finish.1 = (f32[1,16,432]{2,1,0:T(8,128)}, f32[16,32]{1,0:T(8,128)}, f32[16,16]{1,0:T(8,128)}) custom-call(f32[64,8,128]{2,1,0:T(8,128)S(1)} %all_to_all.5.parts_ref, f32[8,128]{1,0:T(8,128)S(1)} %get-tuple-element.44.g_ref, f32[16,432]{1,0:T(8,128)S(1)} %get-tuple-element.45.x_ref, f32[1,32,432]{2,1,0:T(8,128)S(1)} %copy-done), custom_call_target="tpu_custom_call" | custom-call | tf_op jit(solution)/shard_map/finish/pallas_call | solution.py:332
  (69 shorter events, 26.5 us)
Async XLA Ops:
  0.7 8.2 %collective-permute-start.2 = (f32[32,432]{1,0:T(8,128)}, f32[32,432]{1,0:T(8,128)S(1)}, u32[]{:S(2)}, u32[]{:S(2)}) collective-permute-start(f32[32,432]{1,0:T(8,128)} %bitcast.5), channel_id=1, source_target_pairs={{0,3},{1,2},{2,1},{3,0},{4,7},{5,6},{6,5},{7,4},{8,11},{9,10},{10,... | collective-permute-start | bytes 165896 | tf_op jit(solution)/shard_map/ppermute | solution.py:362
  5.3 4.4 %collective-permute-start = (f32[32,432]{1,0:T(8,128)}, f32[32,432]{1,0:T(8,128)S(1)}, u32[]{:S(2)}, u32[]{:S(2)}) collective-permute-start(f32[32,432]{1,0:T(8,128)} %bitcast.6), channel_id=1, source_target_pairs={{0,1},{1,0},{2,3},{3,2},{4,5},{5,4},{6,7},{7,6},{8,9},{9,8},{10,11... | collective-permute-start | bytes 165896 | tf_op jit(solution)/shard_map/ppermute | solution.py:362
  5.3 5.0 %collective-permute-start.1 = (f32[32,432]{1,0:T(8,128)}, f32[32,432]{1,0:T(8,128)S(1)}, u32[]{:S(2)}, u32[]{:S(2)}) collective-permute-start(f32[32,432]{1,0:T(8,128)} %bitcast.7), channel_id=1, source_target_pairs={{0,2},{1,3},{2,0},{3,1},{4,6},{5,7},{6,4},{7,5},{8,10},{9,11},{10,... | collective-permute-start | bytes 165896 | tf_op jit(solution)/shard_map/ppermute | solution.py:362
  11.0 5.4 %collective-permute-start.3 = (f32[24,432]{1,0:T(8,128)S(1)}, f32[24,432]{1,0:T(8,128)S(1)}, u32[]{:S(2)}, u32[]{:S(2)}) collective-permute-start(f32[24,432]{1,0:T(8,128)S(1)} %get-tuple-element.29.rest_0_), channel_id=1, source_target_pairs={{0,4},{1,5},{2,6},{3,7},{4,0},{5,1},{6,2},{7,3},{8,12},{9,13},{10,... | collective-permute-start | bytes 124424 | tf_op jit(solution)/shard_map/ppermute | solution.py:355
  16.4 7.5 %collective-permute-start.5 = (f32[16,432]{1,0:T(8,128)S(1)}, f32[16,432]{1,0:T(8,128)S(1)}, u32[]{:S(2)}, u32[]{:S(2)}) collective-permute-start(f32[16,432]{1,0:T(8,128)S(1)} %fusion.3.s0), channel_id=1, source_target_pairs={{0,1},{1,0},{2,3},{3,2},{4,5},{5,4},{6,7},{7,6},{8,9},{9,8},{10,11... | collective-permute-start | bytes 82952 | tf_op jit(solution)/shard_map/ppermute | solution.py:362
  18.2 5.7 %collective-permute-start.6 = (f32[16,432]{1,0:T(8,128)S(1)}, f32[16,432]{1,0:T(8,128)S(1)}, u32[]{:S(2)}, u32[]{:S(2)}) collective-permute-start(f32[16,432]{1,0:T(8,128)S(1)} %fusion.3.s0), channel_id=1, source_target_pairs={{0,2},{1,3},{2,0},{3,1},{4,6},{5,7},{6,4},{7,5},{8,10},{9,11},{10,... | collective-permute-start | bytes 82952 | tf_op jit(solution)/shard_map/ppermute | solution.py:362
  19.2 4.0 %collective-permute-start.7 = (f32[16,432]{1,0:T(8,128)S(1)}, f32[16,432]{1,0:T(8,128)S(1)}, u32[]{:S(2)}, u32[]{:S(2)}) collective-permute-start(f32[16,432]{1,0:T(8,128)S(1)} %fusion.3.s0), channel_id=1, source_target_pairs={{0,3},{1,2},{2,1},{3,0},{4,7},{5,6},{6,5},{7,4},{8,11},{9,10},{10,... | collective-permute-start | bytes 82952 | tf_op jit(solution)/shard_map/ppermute | solution.py:362
  24.6 10.3 %collective-permute-start.8 = (f32[24,432]{1,0:T(8,128)S(1)}, f32[24,432]{1,0:T(8,128)S(1)}, u32[]{:S(2)}, u32[]{:S(2)}) collective-permute-start(f32[24,432]{1,0:T(8,128)S(1)} %get-tuple-element.33.rest_0_), channel_id=1, source_target_pairs={{0,8},{1,9},{2,10},{3,11},{4,12},{5,13},{6,14},{7,15},{8,0},{9,1},... | collective-permute-start | bytes 124424 | tf_op jit(solution)/shard_map/ppermute | solution.py:355
  26.3 8.6 %collective-permute-start.9 = (f32[16,432]{1,0:T(8,128)S(1)}, f32[16,432]{1,0:T(8,128)S(1)}, u32[]{:S(2)}, u32[]{:S(2)}) collective-permute-start(f32[16,432]{1,0:T(8,128)S(1)} %get-tuple-element.34), channel_id=1, source_target_pairs={{0,120},{1,121},{2,122},{3,123},{4,124},{5,125},{6,126},{7,127},{8... | collective-permute-start | bytes 82952 | tf_op jit(solution)/shard_map/ppermute | solution.py:355
  34.9 7.3 %collective-permute-start.10 = (f32[16,432]{1,0:T(8,128)S(1)}, f32[16,432]{1,0:T(8,128)S(1)}, u32[]{:S(2)}, u32[]{:S(2)}) collective-permute-start(f32[16,432]{1,0:T(8,128)S(1)} %fusion.2.s0), channel_id=1, source_target_pairs={{0,1},{1,0},{2,3},{3,2},{4,5},{5,4},{6,7},{7,6},{8,9},{9,8},{10,11... | collective-permute-start | bytes 82952 | tf_op jit(solution)/shard_map/ppermute | solution.py:362
  35.0 7.3 %collective-permute-start.11 = (f32[16,432]{1,0:T(8,128)S(1)}, f32[16,432]{1,0:T(8,128)S(1)}, u32[]{:S(2)}, u32[]{:S(2)}) collective-permute-start(f32[16,432]{1,0:T(8,128)S(1)} %fusion.2.s0), channel_id=1, source_target_pairs={{0,2},{1,3},{2,0},{3,1},{4,6},{5,7},{6,4},{7,5},{8,10},{9,11},{10,... | collective-permute-start | bytes 82952 | tf_op jit(solution)/shard_map/ppermute | solution.py:362
  43.0 6.6 %collective-permute-start.13 = (f32[24,432]{1,0:T(8,128)S(1)}, f32[24,432]{1,0:T(8,128)S(1)}, u32[]{:S(2)}, u32[]{:S(2)}) collective-permute-start(f32[24,432]{1,0:T(8,128)S(1)} %get-tuple-element.37.rest_0_), channel_id=1, source_target_pairs={{0,16},{1,17},{2,18},{3,19},{4,20},{5,21},{6,22},{7,23},{8,24},{9,... | collective-permute-start | bytes 124424 | tf_op jit(solution)/shard_map/ppermute | solution.py:355
  43.1 6.5 %collective-permute-start.14 = (f32[16,432]{1,0:T(8,128)S(1)}, f32[16,432]{1,0:T(8,128)S(1)}, u32[]{:S(2)}, u32[]{:S(2)}) collective-permute-start(f32[16,432]{1,0:T(8,128)S(1)} %get-tuple-element.38), channel_id=1, source_target_pairs={{0,112},{1,113},{2,114},{3,115},{4,116},{5,117},{6,118},{7,119},{8... | collective-permute-start | bytes 82952 | tf_op jit(solution)/shard_map/ppermute | solution.py:355
  49.6 7.2 %collective-permute-start.15 = (f32[16,432]{1,0:T(8,128)S(1)}, f32[16,432]{1,0:T(8,128)S(1)}, u32[]{:S(2)}, u32[]{:S(2)}) collective-permute-start(f32[16,432]{1,0:T(8,128)S(1)} %fusion.1.s0), channel_id=1, source_target_pairs={{0,1},{1,0},{2,3},{3,2},{4,5},{5,4},{6,7},{7,6},{8,9},{9,8},{10,11... | collective-permute-start | bytes 82952 | tf_op jit(solution)/shard_map/ppermute | solution.py:362
  49.6 7.1 %collective-permute-start.16 = (f32[16,432]{1,0:T(8,128)S(1)}, f32[16,432]{1,0:T(8,128)S(1)}, u32[]{:S(2)}, u32[]{:S(2)}) collective-permute-start(f32[16,432]{1,0:T(8,128)S(1)} %fusion.1.s0), channel_id=1, source_target_pairs={{0,2},{1,3},{2,0},{3,1},{4,6},{5,7},{6,4},{7,5},{8,10},{9,11},{10,... | collective-permute-start | bytes 82952 | tf_op jit(solution)/shard_map/ppermute | solution.py:362
  57.4 4.2 %collective-permute-start.18 = (f32[24,432]{1,0:T(8,128)S(1)}, f32[24,432]{1,0:T(8,128)S(1)}, u32[]{:S(2)}, u32[]{:S(2)}) collective-permute-start(f32[24,432]{1,0:T(8,128)S(1)} %get-tuple-element.41.rest_0_), channel_id=1, source_target_pairs={{0,32},{1,33},{2,34},{3,35},{4,36},{5,37},{6,38},{7,39},{8,40},{9,... | collective-permute-start | bytes 124424 | tf_op jit(solution)/shard_map/ppermute | solution.py:355
  57.5 4.1 %collective-permute-start.19 = (f32[16,432]{1,0:T(8,128)S(1)}, f32[16,432]{1,0:T(8,128)S(1)}, u32[]{:S(2)}, u32[]{:S(2)}) collective-permute-start(f32[16,432]{1,0:T(8,128)S(1)} %get-tuple-element.42), channel_id=1, source_target_pairs={{0,96},{1,97},{2,98},{3,99},{4,100},{5,101},{6,102},{7,103},{8,104... | collective-permute-start | bytes 82952 | tf_op jit(solution)/shard_map/ppermute | solution.py:355
  61.6 7.3 %collective-permute-start.20 = (f32[16,432]{1,0:T(8,128)S(1)}, f32[16,432]{1,0:T(8,128)S(1)}, u32[]{:S(2)}, u32[]{:S(2)}) collective-permute-start(f32[16,432]{1,0:T(8,128)S(1)} %fusion.s0), channel_id=1, source_target_pairs={{0,1},{1,0},{2,3},{3,2},{4,5},{5,4},{6,7},{7,6},{8,9},{9,8},{10,11... | collective-permute-start | bytes 82952 | tf_op jit(solution)/shard_map/ppermute | solution.py:362
  61.9 7.0 %collective-permute-start.21 = (f32[16,432]{1,0:T(8,128)S(1)}, f32[16,432]{1,0:T(8,128)S(1)}, u32[]{:S(2)}, u32[]{:S(2)}) collective-permute-start(f32[16,432]{1,0:T(8,128)S(1)} %fusion.s0), channel_id=1, source_target_pairs={{0,2},{1,3},{2,0},{3,1},{4,6},{5,7},{6,4},{7,5},{8,10},{9,11},{10,... | collective-permute-start | bytes 82952 | tf_op jit(solution)/shard_map/ppermute | solution.py:362
  69.3 4.5 %collective-permute-start.23 = (f32[24,432]{1,0:T(8,128)S(1)}, f32[24,432]{1,0:T(8,128)S(1)}, u32[]{:S(2)}, u32[]{:S(2)}) collective-permute-start(f32[24,432]{1,0:T(8,128)S(1)} %level.9), channel_id=1, source_target_pairs={{0,64},{1,65},{2,66},{3,67},{4,68},{5,69},{6,70},{7,71},{8,72},{9,... | collective-permute-start | bytes 124424 | tf_op jit(solution)/shard_map/ppermute | solution.py:355
  73.9 6.1 %collective-permute-start.24 = (f32[24,432]{1,0:T(8,128)S(1)}, f32[24,432]{1,0:T(8,128)S(1)}, u32[]{:S(2)}, u32[]{:S(2)}) collective-permute-start(f32[24,432]{1,0:T(8,128)S(1)} %select_maximum_fusion._.s0), channel_id=1, source_target_pairs={{0,1},{1,0},{2,3},{3,2},{4,5},{5,4},{6,7},{7,6},{8,9},{9,8},{10,11... | collective-permute-start | bytes 124424 | tf_op jit(solution)/shard_map/ppermute | solution.py:362
  74.0 6.0 %collective-permute-start.25 = (f32[24,432]{1,0:T(8,128)S(1)}, f32[24,432]{1,0:T(8,128)S(1)}, u32[]{:S(2)}, u32[]{:S(2)}) collective-permute-start(f32[24,432]{1,0:T(8,128)S(1)} %select_maximum_fusion._.s0), channel_id=1, source_target_pairs={{0,2},{1,3},{2,0},{3,1},{4,6},{5,7},{6,4},{7,5},{8,10},{9,11},{10,... | collective-permute-start | bytes 124424 | tf_op jit(solution)/shard_map/ppermute | solution.py:362
  76.4 4.2 %collective-permute-start.26 = (f32[24,432]{1,0:T(8,128)S(1)}, f32[24,432]{1,0:T(8,128)S(1)}, u32[]{:S(2)}, u32[]{:S(2)}) collective-permute-start(f32[24,432]{1,0:T(8,128)S(1)} %select_maximum_fusion._.s0), channel_id=1, source_target_pairs={{0,3},{1,2},{2,1},{3,0},{4,7},{5,6},{6,5},{7,4},{8,11},{9,10},{10,... | collective-permute-start | bytes 124424 | tf_op jit(solution)/shard_map/ppermute | solution.py:362
  82.0 13.8 %collective-permute-start.27 = (f32[8,128]{1,0:T(8,128)S(1)}, f32[8,128]{1,0:T(8,128)S(1)}, u32[]{:S(2)}, u32[]{:S(2)}) collective-permute-start(f32[8,128]{1,0:T(8,128)S(1)} %get-tuple-element.43), channel_id=1, source_target_pairs={{0,4},{1,5},{2,6},{3,7},{4,0},{5,1},{6,2},{7,3},{8,12},{9,13},{10,... | collective-permute-start | bytes 12296 | tf_op jit(solution)/shard_map/ppermute | solution.py:355
  (6 other events, 31.3 us)

commit v4 on v3

--- a/solution.py
+++ b/solution.py
@@ -144,15 +144,6 @@
         compiler_params=pltpu.CompilerParams(vmem_limit_bytes=8 << 20),
         name="prep_pivots",
     )(far(pivots), near(after))
-
-
-def gather_rows(slices, whole):
-    rad = lax.axis_index("rad")
-    for m, piece in enumerate(slices):
-        first = piece.shape[0] - NRHS if piece.shape[0] > NRHS + 8 else 0
-        whole[rad ^ m] = piece[first : first + NRHS, :]
-    v = jnp.concatenate([whole[t] for t in range(4)], axis=1)
-    return jnp.concatenate(split2(v), axis=0)
 
 
 OUTER = ((0, (("s", 0), 80)), (1280, (16, ("s", 3))))
@@ -256,24 +247,69 @@
     )(*map(near, args))
 
 
-def solve_kernel(s0, s1, s2, s3, p_ref, stored_ref, x_ref, part_ref, g_ref, whole, gs):
+def half_solution(ranges, p_ref, whole):
+    x = None
+    for start, items in ranges:
+        pieces = [
+            whole[item[1]] if isinstance(item, tuple) else jnp.zeros((NRHS, item), jnp.float32)
+            for item in items
+        ]
+        lhs = jnp.concatenate(split2(jnp.concatenate(pieces, axis=1)), axis=0)
+        size = lhs.shape[1]
+        both = nt_dot(lhs, p_ref[0, :, start : start + size])
+        one = both[:NRHS] + both[NRHS:] + nt_dot(lhs[:NRHS], p_ref[1, :, start : start + size])
+        x = one if x is None else x + one
+    return x
+
+
+def near_solve_kernel(s0, s3, p_ref, half_ref, whole):
     rad = lax.axis_index("rad")
-    lhs = gather_rows((s0, s1, s2, s3), whole)
-    both = nt_dot(lhs, p_ref[0])
-    x = both[:NRHS] + both[NRHS:] + nt_dot(lhs[:NRHS], p_ref[1])
-    x_ref[...] = x
-    t = jnp.concatenate(
-        [nt_dot(x, stored_ref[0], precise), nt_dot(x, x, precise)], axis=1
-    )
+    whole[rad] = s0[:NRHS, :]
+    whole[rad ^ 3] = s3[:NRHS, :]
+
+    def run(ranges):
+        half_ref[...] = half_solution(ranges, p_ref, whole)
+
+    edge = (rad == 0) | (rad == 3)
+    pl.when(edge)(lambda: run(OUTER))
+    pl.when(jnp.logical_not(edge))(lambda: run(INNER))
+
+
+def near_solve(own, third, pivots):
+    rows = pivots.shape[1]
+    return pl.pallas_call(
+        near_solve_kernel,
+        out_shape=made((NRHS, rows)),
+        in_specs=[VMEM] * 3,
+        out_specs=VMEM,
+        scratch_shapes=[pltpu.VMEM((4, NRHS, rows), jnp.float32)],
+        compiler_params=pltpu.CompilerParams(vmem_limit_bytes=4 << 20),
+        name="nearsolve",
+    )(*map(near, (own, third, pivots)))
+
+
+def solve_kernel(s0, s1, s2, s3, p_ref, stored_ref, half_ref, x_ref, part_ref, g_ref, whole, gs):
+    rad = lax.axis_index("rad")
+    whole[rad ^ 1] = s1[:NRHS, :]
+    whole[rad ^ 2] = s2[:NRHS, :]
+
+    def run(ranges):
+        x_ref[...] = half_ref[...] + half_solution(ranges, p_ref, whole)
+
+    edge = (rad == 0) | (rad == 3)
+    pl.when(edge)(lambda: run(INNER))
+    pl.when(jnp.logical_not(edge))(lambda: run(OUTER))
+    for m, piece in enumerate((s0, s1, s2, s3)):
+        gs[rad ^ m] = piece[NRHS:, :128]
+    x = x_ref[...]
+    t = nt_dot(x, jnp.concatenate([stored_ref[0], x], axis=0), precise)
     part_ref[...] = jnp.concatenate(
         [t[:8], t[8:], jnp.zeros((8, 32), jnp.float32)], axis=1
     )
-    for m, piece in enumerate((s0, s1, s2, s3)):
-        gs[rad ^ m] = piece[NRHS:, :128]
     g_ref[...] = (gs[0] + gs[1]) + (gs[2] + gs[3])
 
 
-def solve(slices, pivots, krylov):
+def solve(slices, pivots, krylov, half):
     rows = pivots.shape[1]
     return pl.pallas_call(
         solve_kernel,
@@ -282,7 +318,7 @@
             made((8, 128)),
             made((8, 128)),
         ],
-        in_specs=[VMEM] * 6,
+        in_specs=[VMEM] * 7,
         out_specs=[VMEM] * 3,
         scratch_shapes=[
             pltpu.VMEM((4, NRHS, rows), jnp.float32),
@@ -290,7 +326,7 @@
         ],
         compiler_params=pltpu.CompilerParams(vmem_limit_bytes=8 << 20),
         name="solve",
-    )(*map(near, (*slices, pivots, krylov)))
+    )(*map(near, (*slices, pivots, krylov, half)))
 
 
 def finish_kernel(total, parts_ref, g_ref, x_ref, stored_ref, basis_ref, coef_ref, upper_ref):
@@ -383,7 +419,9 @@
         if rung == 0:
             g = halves[slots]
         sent = level(rung, slots, points, slices, weights, masks, g, halves[:slots])
-        if not last:
+        if last:
+            weights = prep_pivots(pivots, sent[0])
+        else:
             weights = fetch(rung + 1, 1 if rung + 2 == levels else 2, couplings, sent[0])
         got = swap(sent[0], blocks, rads, stride, 0)
         other = None if last else swap(sent[1], blocks, rads, stride, 1)
@@ -399,8 +437,8 @@
             payload = jnp.concatenate([residue, tail], axis=0)
         slices = gather(payload, blocks, rads)
         if last:
-            weights = prep_pivots(pivots, payload)
-    x, part, g = solve(slices, weights, krylov)
+            half = near_solve(slices[0], slices[3], weights)
+    x, part, g = solve(slices, weights, krylov, half)
     part = part + swap(part, blocks, rads, 1, 0)
     chips = blocks // 2 * rads
     parts = lax.all_to_all(

time: 113 us -> 113 us (level)
  blocking collectives: 15 us -> 16.5 us
    all_to_all x1, blocking collectives: 15 us -> 16.5 us  [step(): lax.all_to_all(jnp.broadcast_to(part[None], (chips,) + part.shape), ('chi...]
  transfers between devices with their start and end apart: 28 -> 28, of which waited for: 11 -> 10; matrix products, arithmetic and copies ran while one was open for 0% -> 0% of each run, Pallas kernels for 13% -> 14%
where the time goes in v4:
time: 113 us
  starting transfers between devices  54 us (48%)
  Pallas kernels  20.9 us (18%)
  waiting for transfers between devices  20 us (18%)
  blocking collectives  16.5 us (15%)
    ppermute x10, starting transfers between devices, swap(): return lax.ppermute(value, ALL, pairs)  27.9 us
    ppermute x18, starting transfers between devices, gather(): out.append(lax.ppermute(value, ALL, pairs))  26.1 us
    all_to_all x1, blocking collectives, step(): lax.all_to_all(jnp.broadcast_to(part[None], (chips,) + part.shape), ('chi...  16.5 us
    ppermute x18, waiting for transfers between devices, gather(): out.append(lax.ppermute(value, ALL, pairs))  11.1 us
    pallas_call x5, Pallas kernels, fetch(): pl.pallas_call(functools.partial(fetch_kernel, rung, slots), out_shape=ma...  8.93 us
    ppermute x10, waiting for transfers between devices, swap(): return lax.ppermute(value, ALL, pairs)  8.84 us
    pallas_call x5, Pallas kernels, near_half(): pl.pallas_call(functools.partial(near_half_kernel, rung, slots, points),...  3.25 us
    pallas_call x5, Pallas kernels, level(): pl.pallas_call(functools.partial(far_half_kernel, rung, slots, points), o...  3.15 us
  transfers between devices with their start and end apart: 28, of which 10 were waited for; matrix products, arithmetic and copies ran while one was open for 0% of the time, Pallas kernels for 14%

profile of v4, /device:TPU:1, one launch (start us, length us, event | category | flops | bytes accessed | tf_op | source)
XLA Modules:
  0.0 112.5 jit_solution(10224735850122247950)
XLA Ops:
  0.7 4.7 %collective-permute-start.2 = (f32[32,432]{1,0:T(8,128)}, f32[32,432]{1,0:T(8,128)S(1)}, u32[]{:S(2)}, u32[]{:S(2)}) collective-permute-start(f32[32,432]{1,0:T(8,128)} %bitcast.5), channel_id=1, source_target_pairs={{0,3},{1,2},{2,1},{3,0},{4,7},{5,6},{6,5},{7,4},{8,11},{9,10},{10,... | collective-permute-start | bytes 165896 | tf_op jit(solution)/shard_map/ppermute | solution.py:398
  6.6 1.9 %shard_map.67.w_ref = bf16[2,432,1728]{2,1,0:T(8,128)(2,1)S(1)} custom-call(bf16[1,10,432,1728]{3,2,1,0:T(8,128)(2,1)} %couplings_ref.9), custom_call_target="tpu_custom_call" | custom-call | tf_op jit(solution)/shard_map/pallas_call | solution.py:107
  11.0 2.0 %collective-permute-start.3 = (f32[24,432]{1,0:T(8,128)S(1)}, f32[24,432]{1,0:T(8,128)S(1)}, u32[]{:S(2)}, u32[]{:S(2)}) collective-permute-start(f32[24,432]{1,0:T(8,128)S(1)} %get-tuple-element.29.rest_0_), channel_id=1, source_target_pairs={{0,4},{1,5},{2,6},{3,7},{4,0},{5,1},{6,2},{7,3},{8,12},{9,13},{10,... | collective-permute-start | bytes 124424 | tf_op jit(solution)/shard_map/ppermute | solution.py:391
  14.3 1.9 %shard_map.68.w_ref = bf16[2,432,1728]{2,1,0:T(8,128)(2,1)S(1)} custom-call(bf16[1,10,432,1728]{3,2,1,0:T(8,128)(2,1)} %couplings_ref.9, f32[24,432]{1,0:T(8,128)S(1)} %get-tuple-element.29.rest_0_), custom_call_target="tpu_custom_call" | custom-call | tf_op jit(solution)/shard_map/pallas_call | solution.py:107
  16.4 1.8 %collective-permute-start.5 = (f32[16,432]{1,0:T(8,128)S(1)}, f32[16,432]{1,0:T(8,128)S(1)}, u32[]{:S(2)}, u32[]{:S(2)}) collective-permute-start(f32[16,432]{1,0:T(8,128)S(1)} %fusion.3.s0), channel_id=1, source_target_pairs={{0,1},{1,0},{2,3},{3,2},{4,5},{5,4},{6,7},{7,6},{8,9},{9,8},{10,11... | collective-permute-start | bytes 82952 | tf_op jit(solution)/shard_map/ppermute | solution.py:398
  20.7 2.5 %collective-permute-done.7.s3 = f32[16,432]{1,0:T(8,128)S(1)} collective-permute-done((f32[16,432]{1,0:T(8,128)S(1)}, f32[16,432]{1,0:T(8,128)S(1)}, u32[]{:S(2)}, u32[]{:S(2)}) %collective-permute-start.7) | collective-permute-done | bytes 27680 | tf_op jit(solution)/shard_map/ppermute | solution.py:398
  24.6 1.7 %collective-permute-start.8 = (f32[24,432]{1,0:T(8,128)S(1)}, f32[24,432]{1,0:T(8,128)S(1)}, u32[]{:S(2)}, u32[]{:S(2)}) collective-permute-start(f32[24,432]{1,0:T(8,128)S(1)} %get-tuple-element.33.rest_0_), channel_id=1, source_target_pairs={{0,8},{1,9},{2,10},{3,11},{4,12},{5,13},{6,14},{7,15},{8,0},{9,1},... | collective-permute-start | bytes 124424 | tf_op jit(solution)/shard_map/ppermute | solution.py:391
  26.3 6.7 %collective-permute-start.9 = (f32[16,432]{1,0:T(8,128)S(1)}, f32[16,432]{1,0:T(8,128)S(1)}, u32[]{:S(2)}, u32[]{:S(2)}) collective-permute-start(f32[16,432]{1,0:T(8,128)S(1)} %get-tuple-element.34), channel_id=1, source_target_pairs={{0,120},{1,121},{2,122},{3,123},{4,124},{5,125},{6,126},{7,127},{8... | collective-permute-start | bytes 82952 | tf_op jit(solution)/shard_map/ppermute | solution.py:391
  33.0 1.9 %shard_map.69.w_ref = bf16[2,432,1728]{2,1,0:T(8,128)(2,1)S(1)} custom-call(bf16[1,10,432,1728]{3,2,1,0:T(8,128)(2,1)} %couplings_ref.9, f32[24,432]{1,0:T(8,128)S(1)} %get-tuple-element.33.rest_0_), custom_call_target="tpu_custom_call" | custom-call | tf_op jit(solution)/shard_map/pallas_call | solution.py:107
  35.0 2.6 %collective-permute-start.11 = (f32[16,432]{1,0:T(8,128)S(1)}, f32[16,432]{1,0:T(8,128)S(1)}, u32[]{:S(2)}, u32[]{:S(2)}) collective-permute-start(f32[16,432]{1,0:T(8,128)S(1)} %fusion.2.s0), channel_id=1, source_target_pairs={{0,2},{1,3},{2,0},{3,1},{4,6},{5,7},{6,4},{7,5},{8,10},{9,11},{10,... | collective-permute-start | bytes 82952 | tf_op jit(solution)/shard_map/ppermute | solution.py:398
  38.9 2.7 %collective-permute-done.12.s3 = f32[16,432]{1,0:T(8,128)S(1)} collective-permute-done((f32[16,432]{1,0:T(8,128)S(1)}, f32[16,432]{1,0:T(8,128)S(1)}, u32[]{:S(2)}, u32[]{:S(2)}) %collective-permute-start.12) | collective-permute-done | bytes 27680 | tf_op jit(solution)/shard_map/ppermute | solution.py:398
  43.1 2.0 %collective-permute-start.14 = (f32[16,432]{1,0:T(8,128)S(1)}, f32[16,432]{1,0:T(8,128)S(1)}, u32[]{:S(2)}, u32[]{:S(2)}) collective-permute-start(f32[16,432]{1,0:T(8,128)S(1)} %get-tuple-element.38), channel_id=1, source_target_pairs={{0,112},{1,113},{2,114},{3,115},{4,116},{5,117},{6,118},{7,119},{8... | collective-permute-start | bytes 82952 | tf_op jit(solution)/shard_map/ppermute | solution.py:391
  45.1 1.9 %shard_map.70.w_ref = bf16[2,432,1728]{2,1,0:T(8,128)(2,1)S(1)} custom-call(bf16[1,10,432,1728]{3,2,1,0:T(8,128)(2,1)} %couplings_ref.9, f32[24,432]{1,0:T(8,128)S(1)} %get-tuple-element.37.rest_0_), custom_call_target="tpu_custom_call" | custom-call | tf_op jit(solution)/shard_map/pallas_call | solution.py:107
  47.0 2.5 %collective-permute-done.14 = f32[16,432]{1,0:T(8,128)S(1)} collective-permute-done((f32[16,432]{1,0:T(8,128)S(1)}, f32[16,432]{1,0:T(8,128)S(1)}, u32[]{:S(2)}, u32[]{:S(2)}) %collective-permute-start.14) | collective-permute-done | bytes 27680 | tf_op jit(solution)/shard_map/ppermute | solution.py:391
  49.6 2.4 %collective-permute-start.16 = (f32[16,432]{1,0:T(8,128)S(1)}, f32[16,432]{1,0:T(8,128)S(1)}, u32[]{:S(2)}, u32[]{:S(2)}) collective-permute-start(f32[16,432]{1,0:T(8,128)S(1)} %fusion.1.s0), channel_id=1, source_target_pairs={{0,2},{1,3},{2,0},{3,1},{4,6},{5,7},{6,4},{7,5},{8,10},{9,11},{10,... | collective-permute-start | bytes 82952 | tf_op jit(solution)/shard_map/ppermute | solution.py:398
  53.5 2.5 %collective-permute-done.17.s3 = f32[16,432]{1,0:T(8,128)S(1)} collective-permute-done((f32[16,432]{1,0:T(8,128)S(1)}, f32[16,432]{1,0:T(8,128)S(1)}, u32[]{:S(2)}, u32[]{:S(2)}) %collective-permute-start.17) | collective-permute-done | bytes 27680 | tf_op jit(solution)/shard_map/ppermute | solution.py:398
  61.9 2.6 %collective-permute-start.21 = (f32[16,432]{1,0:T(8,128)S(1)}, f32[16,432]{1,0:T(8,128)S(1)}, u32[]{:S(2)}, u32[]{:S(2)}) collective-permute-start(f32[16,432]{1,0:T(8,128)S(1)} %fusion.s0), channel_id=1, source_target_pairs={{0,2},{1,3},{2,0},{3,1},{4,6},{5,7},{6,4},{7,5},{8,10},{9,11},{10,... | collective-permute-start | bytes 82952 | tf_op jit(solution)/shard_map/ppermute | solution.py:398
  65.7 2.7 %collective-permute-done.22.s3 = f32[16,432]{1,0:T(8,128)S(1)} collective-permute-done((f32[16,432]{1,0:T(8,128)S(1)}, f32[16,432]{1,0:T(8,128)S(1)}, u32[]{:S(2)}, u32[]{:S(2)}) %collective-permute-start.22) | collective-permute-done | bytes 27680 | tf_op jit(solution)/shard_map/ppermute | solution.py:398
  70.2 3.6 %collective-permute-done.23 = f32[24,432]{1,0:T(8,128)S(1)} collective-permute-done((f32[24,432]{1,0:T(8,128)S(1)}, f32[24,432]{1,0:T(8,128)S(1)}, u32[]{:S(2)}, u32[]{:S(2)}) %collective-permute-start.23) | collective-permute-done | bytes 41504 | tf_op jit(solution)/shard_map/ppermute | solution.py:391
  75.2 2.6 %collective-permute-start.25 = (f32[24,432]{1,0:T(8,128)S(1)}, f32[24,432]{1,0:T(8,128)S(1)}, u32[]{:S(2)}, u32[]{:S(2)}) collective-permute-start(f32[24,432]{1,0:T(8,128)S(1)} %select_maximum_fusion.s0), channel_id=1, source_target_pairs={{0,2},{1,3},{2,0},{3,1},{4,6},{5,7},{6,4},{7,5},{8,10},{9,11},{10,... | collective-permute-start | bytes 124424 | tf_op jit(solution)/shard_map/ppermute | solution.py:398
  77.8 2.1 %prep_pivots.1.p_ref = bf16[2,432,1728]{2,1,0:T(8,128)(2,1)S(1)} custom-call(f32[1,432,1728]{2,1,0:T(8,128)} %pivots_ref.1, f32[24,432]{1,0:T(8,128)S(1)} %level.9._), custom_call_target="tpu_custom_call" | custom-call | tf_op jit(solution)/shard_map/prep_pivots/pallas_call | solution.py:138
  81.5 12.0 %collective-permute-start.27 = (f32[8,128]{1,0:T(8,128)S(1)}, f32[8,128]{1,0:T(8,128)S(1)}, u32[]{:S(2)}, u32[]{:S(2)}) collective-permute-start(f32[8,128]{1,0:T(8,128)S(1)} %get-tuple-element.43), channel_id=1, source_target_pairs={{0,4},{1,5},{2,6},{3,7},{4,0},{5,1},{6,2},{7,3},{8,12},{9,13},{10,... | collective-permute-start | bytes 12296 | tf_op jit(solution)/shard_map/ppermute | solution.py:391
  94.3 16.5 %all_to_all.5.parts_ref = f32[64,8,128]{2,1,0:T(8,128)S(1)} all-to-all(f32[64,8,128]{2,1,0:T(8,128)S(1)} %broadcast_in_dim.14), channel_id=1, replica_groups=mesh['chip'=16,'core'=2,'rad'=4] {'chip','rad'}, dimensions={0} | all-to-all | bytes 524288 | tf_op jit(solution)/shard_map/all_to_all | solution.py:444
  110.9 1.7 %finish.1 = (f32[1,16,432]{2,1,0:T(8,128)}, f32[16,32]{1,0:T(8,128)}, f32[16,16]{1,0:T(8,128)}) custom-call(f32[64,8,128]{2,1,0:T(8,128)S(1)} %all_to_all.5.parts_ref, f32[8,128]{1,0:T(8,128)S(1)} %get-tuple-element.44.g_ref, f32[16,432]{1,0:T(8,128)S(1)} %get-tuple-element.45.x_ref, f32[1,32,432]{2,1,0:T(8,128)S(1)} %copy-done), custom_call_target="tpu_custom_call" | custom-call | tf_op jit(solution)/shard_map/finish/pallas_call | solution.py:368
  (70 shorter events, 25.8 us)
Async XLA Ops:
  0.7 8.2 %collective-permute-start.2 = (f32[32,432]{1,0:T(8,128)}, f32[32,432]{1,0:T(8,128)S(1)}, u32[]{:S(2)}, u32[]{:S(2)}) collective-permute-start(f32[32,432]{1,0:T(8,128)} %bitcast.5), channel_id=1, source_target_pairs={{0,3},{1,2},{2,1},{3,0},{4,7},{5,6},{6,5},{7,4},{8,11},{9,10},{10,... | collective-permute-start | bytes 165896 | tf_op jit(solution)/shard_map/ppermute | solution.py:398
  5.3 4.4 %collective-permute-start = (f32[32,432]{1,0:T(8,128)}, f32[32,432]{1,0:T(8,128)S(1)}, u32[]{:S(2)}, u32[]{:S(2)}) collective-permute-start(f32[32,432]{1,0:T(8,128)} %bitcast.6), channel_id=1, source_target_pairs={{0,1},{1,0},{2,3},{3,2},{4,5},{5,4},{6,7},{7,6},{8,9},{9,8},{10,11... | collective-permute-start | bytes 165896 | tf_op jit(solution)/shard_map/ppermute | solution.py:398
  5.3 5.0 %collective-permute-start.1 = (f32[32,432]{1,0:T(8,128)}, f32[32,432]{1,0:T(8,128)S(1)}, u32[]{:S(2)}, u32[]{:S(2)}) collective-permute-start(f32[32,432]{1,0:T(8,128)} %bitcast.7), channel_id=1, source_target_pairs={{0,2},{1,3},{2,0},{3,1},{4,6},{5,7},{6,4},{7,5},{8,10},{9,11},{10,... | collective-permute-start | bytes 165896 | tf_op jit(solution)/shard_map/ppermute | solution.py:398
  11.0 5.4 %collective-permute-start.3 = (f32[24,432]{1,0:T(8,128)S(1)}, f32[24,432]{1,0:T(8,128)S(1)}, u32[]{:S(2)}, u32[]{:S(2)}) collective-permute-start(f32[24,432]{1,0:T(8,128)S(1)} %get-tuple-element.29.rest_0_), channel_id=1, source_target_pairs={{0,4},{1,5},{2,6},{3,7},{4,0},{5,1},{6,2},{7,3},{8,12},{9,13},{10,... | collective-permute-start | bytes 124424 | tf_op jit(solution)/shard_map/ppermute | solution.py:391
  16.4 7.5 %collective-permute-start.5 = (f32[16,432]{1,0:T(8,128)S(1)}, f32[16,432]{1,0:T(8,128)S(1)}, u32[]{:S(2)}, u32[]{:S(2)}) collective-permute-start(f32[16,432]{1,0:T(8,128)S(1)} %fusion.3.s0), channel_id=1, source_target_pairs={{0,1},{1,0},{2,3},{3,2},{4,5},{5,4},{6,7},{7,6},{8,9},{9,8},{10,11... | collective-permute-start | bytes 82952 | tf_op jit(solution)/shard_map/ppermute | solution.py:398
  18.2 5.7 %collective-permute-start.6 = (f32[16,432]{1,0:T(8,128)S(1)}, f32[16,432]{1,0:T(8,128)S(1)}, u32[]{:S(2)}, u32[]{:S(2)}) collective-permute-start(f32[16,432]{1,0:T(8,128)S(1)} %fusion.3.s0), channel_id=1, source_target_pairs={{0,2},{1,3},{2,0},{3,1},{4,6},{5,7},{6,4},{7,5},{8,10},{9,11},{10,... | collective-permute-start | bytes 82952 | tf_op jit(solution)/shard_map/ppermute | solution.py:398
  19.2 4.0 %collective-permute-start.7 = (f32[16,432]{1,0:T(8,128)S(1)}, f32[16,432]{1,0:T(8,128)S(1)}, u32[]{:S(2)}, u32[]{:S(2)}) collective-permute-start(f32[16,432]{1,0:T(8,128)S(1)} %fusion.3.s0), channel_id=1, source_target_pairs={{0,3},{1,2},{2,1},{3,0},{4,7},{5,6},{6,5},{7,4},{8,11},{9,10},{10,... | collective-permute-start | bytes 82952 | tf_op jit(solution)/shard_map/ppermute | solution.py:398
  24.6 10.3 %collective-permute-start.8 = (f32[24,432]{1,0:T(8,128)S(1)}, f32[24,432]{1,0:T(8,128)S(1)}, u32[]{:S(2)}, u32[]{:S(2)}) collective-permute-start(f32[24,432]{1,0:T(8,128)S(1)} %get-tuple-element.33.rest_0_), channel_id=1, source_target_pairs={{0,8},{1,9},{2,10},{3,11},{4,12},{5,13},{6,14},{7,15},{8,0},{9,1},... | collective-permute-start | bytes 124424 | tf_op jit(solution)/shard_map/ppermute | solution.py:391
  26.3 8.6 %collective-permute-start.9 = (f32[16,432]{1,0:T(8,128)S(1)}, f32[16,432]{1,0:T(8,128)S(1)}, u32[]{:S(2)}, u32[]{:S(2)}) collective-permute-start(f32[16,432]{1,0:T(8,128)S(1)} %get-tuple-element.34), channel_id=1, source_target_pairs={{0,120},{1,121},{2,122},{3,123},{4,124},{5,125},{6,126},{7,127},{8... | collective-permute-start | bytes 82952 | tf_op jit(solution)/shard_map/ppermute | solution.py:391
  34.9 7.3 %collective-permute-start.10 = (f32[16,432]{1,0:T(8,128)S(1)}, f32[16,432]{1,0:T(8,128)S(1)}, u32[]{:S(2)}, u32[]{:S(2)}) collective-permute-start(f32[16,432]{1,0:T(8,128)S(1)} %fusion.2.s0), channel_id=1, source_target_pairs={{0,1},{1,0},{2,3},{3,2},{4,5},{5,4},{6,7},{7,6},{8,9},{9,8},{10,11... | collective-permute-start | bytes 82952 | tf_op jit(solution)/shard_map/ppermute | solution.py:398
  35.0 7.3 %collective-permute-start.11 = (f32[16,432]{1,0:T(8,128)S(1)}, f32[16,432]{1,0:T(8,128)S(1)}, u32[]{:S(2)}, u32[]{:S(2)}) collective-permute-start(f32[16,432]{1,0:T(8,128)S(1)} %fusion.2.s0), channel_id=1, source_target_pairs={{0,2},{1,3},{2,0},{3,1},{4,6},{5,7},{6,4},{7,5},{8,10},{9,11},{10,... | collective-permute-start | bytes 82952 | tf_op jit(solution)/shard_map/ppermute | solution.py:398
  43.0 6.6 %collective-permute-start.13 = (f32[24,432]{1,0:T(8,128)S(1)}, f32[24,432]{1,0:T(8,128)S(1)}, u32[]{:S(2)}, u32[]{:S(2)}) collective-permute-start(f32[24,432]{1,0:T(8,128)S(1)} %get-tuple-element.37.rest_0_), channel_id=1, source_target_pairs={{0,16},{1,17},{2,18},{3,19},{4,20},{5,21},{6,22},{7,23},{8,24},{9,... | collective-permute-start | bytes 124424 | tf_op jit(solution)/shard_map/ppermute | solution.py:391
  43.1 6.5 %collective-permute-start.14 = (f32[16,432]{1,0:T(8,128)S(1)}, f32[16,432]{1,0:T(8,128)S(1)}, u32[]{:S(2)}, u32[]{:S(2)}) collective-permute-start(f32[16,432]{1,0:T(8,128)S(1)} %get-tuple-element.38), channel_id=1, source_target_pairs={{0,112},{1,113},{2,114},{3,115},{4,116},{5,117},{6,118},{7,119},{8... | collective-permute-start | bytes 82952 | tf_op jit(solution)/shard_map/ppermute | solution.py:391
  49.6 7.2 %collective-permute-start.15 = (f32[16,432]{1,0:T(8,128)S(1)}, f32[16,432]{1,0:T(8,128)S(1)}, u32[]{:S(2)}, u32[]{:S(2)}) collective-permute-start(f32[16,432]{1,0:T(8,128)S(1)} %fusion.1.s0), channel_id=1, source_target_pairs={{0,1},{1,0},{2,3},{3,2},{4,5},{5,4},{6,7},{7,6},{8,9},{9,8},{10,11... | collective-permute-start | bytes 82952 | tf_op jit(solution)/shard_map/ppermute | solution.py:398
  49.6 7.1 %collective-permute-start.16 = (f32[16,432]{1,0:T(8,128)S(1)}, f32[16,432]{1,0:T(8,128)S(1)}, u32[]{:S(2)}, u32[]{:S(2)}) collective-permute-start(f32[16,432]{1,0:T(8,128)S(1)} %fusion.1.s0), channel_id=1, source_target_pairs={{0,2},{1,3},{2,0},{3,1},{4,6},{5,7},{6,4},{7,5},{8,10},{9,11},{10,... | collective-permute-start | bytes 82952 | tf_op jit(solution)/shard_map/ppermute | solution.py:398
  57.4 4.2 %collective-permute-start.18 = (f32[24,432]{1,0:T(8,128)S(1)}, f32[24,432]{1,0:T(8,128)S(1)}, u32[]{:S(2)}, u32[]{:S(2)}) collective-permute-start(f32[24,432]{1,0:T(8,128)S(1)} %get-tuple-element.41.rest_0_), channel_id=1, source_target_pairs={{0,32},{1,33},{2,34},{3,35},{4,36},{5,37},{6,38},{7,39},{8,40},{9,... | collective-permute-start | bytes 124424 | tf_op jit(solution)/shard_map/ppermute | solution.py:391
  57.5 4.1 %collective-permute-start.19 = (f32[16,432]{1,0:T(8,128)S(1)}, f32[16,432]{1,0:T(8,128)S(1)}, u32[]{:S(2)}, u32[]{:S(2)}) collective-permute-start(f32[16,432]{1,0:T(8,128)S(1)} %get-tuple-element.42), channel_id=1, source_target_pairs={{0,96},{1,97},{2,98},{3,99},{4,100},{5,101},{6,102},{7,103},{8,104... | collective-permute-start | bytes 82952 | tf_op jit(solution)/shard_map/ppermute | solution.py:391
  61.6 7.3 %collective-permute-start.20 = (f32[16,432]{1,0:T(8,128)S(1)}, f32[16,432]{1,0:T(8,128)S(1)}, u32[]{:S(2)}, u32[]{:S(2)}) collective-permute-start(f32[16,432]{1,0:T(8,128)S(1)} %fusion.s0), channel_id=1, source_target_pairs={{0,1},{1,0},{2,3},{3,2},{4,5},{5,4},{6,7},{7,6},{8,9},{9,8},{10,11... | collective-permute-start | bytes 82952 | tf_op jit(solution)/shard_map/ppermute | solution.py:398
  61.9 7.0 %collective-permute-start.21 = (f32[16,432]{1,0:T(8,128)S(1)}, f32[16,432]{1,0:T(8,128)S(1)}, u32[]{:S(2)}, u32[]{:S(2)}) collective-permute-start(f32[16,432]{1,0:T(8,128)S(1)} %fusion.s0), channel_id=1, source_target_pairs={{0,2},{1,3},{2,0},{3,1},{4,6},{5,7},{6,4},{7,5},{8,10},{9,11},{10,... | collective-permute-start | bytes 82952 | tf_op jit(solution)/shard_map/ppermute | solution.py:398
  69.3 4.5 %collective-permute-start.23 = (f32[24,432]{1,0:T(8,128)S(1)}, f32[24,432]{1,0:T(8,128)S(1)}, u32[]{:S(2)}, u32[]{:S(2)}) collective-permute-start(f32[24,432]{1,0:T(8,128)S(1)} %level.9._), channel_id=1, source_target_pairs={{0,64},{1,65},{2,66},{3,67},{4,68},{5,69},{6,70},{7,71},{8,72},{9,... | collective-permute-start | bytes 124424 | tf_op jit(solution)/shard_map/ppermute | solution.py:391
  73.9 6.1 %collective-permute-start.26 = (f32[24,432]{1,0:T(8,128)S(1)}, f32[24,432]{1,0:T(8,128)S(1)}, u32[]{:S(2)}, u32[]{:S(2)}) collective-permute-start(f32[24,432]{1,0:T(8,128)S(1)} %select_maximum_fusion.s0), channel_id=1, source_target_pairs={{0,3},{1,2},{2,1},{3,0},{4,7},{5,6},{6,5},{7,4},{8,11},{9,10},{10,... | collective-permute-start | bytes 124424 | tf_op jit(solution)/shard_map/ppermute | solution.py:398
  75.2 5.3 %collective-permute-start.24 = (f32[24,432]{1,0:T(8,128)S(1)}, f32[24,432]{1,0:T(8,128)S(1)}, u32[]{:S(2)}, u32[]{:S(2)}) collective-permute-start(f32[24,432]{1,0:T(8,128)S(1)} %select_maximum_fusion.s0), channel_id=1, source_target_pairs={{0,1},{1,0},{2,3},{3,2},{4,5},{5,4},{6,7},{7,6},{8,9},{9,8},{10,11... | collective-permute-start | bytes 124424 | tf_op jit(solution)/shard_map/ppermute | solution.py:398
  75.2 5.4 %collective-permute-start.25 = (f32[24,432]{1,0:T(8,128)S(1)}, f32[24,432]{1,0:T(8,128)S(1)}, u32[]{:S(2)}, u32[]{:S(2)}) collective-permute-start(f32[24,432]{1,0:T(8,128)S(1)} %select_maximum_fusion.s0), channel_id=1, source_target_pairs={{0,2},{1,3},{2,0},{3,1},{4,6},{5,7},{6,4},{7,5},{8,10},{9,11},{10,... | collective-permute-start | bytes 124424 | tf_op jit(solution)/shard_map/ppermute | solution.py:398
  81.5 12.9 %collective-permute-start.27 = (f32[8,128]{1,0:T(8,128)S(1)}, f32[8,128]{1,0:T(8,128)S(1)}, u32[]{:S(2)}, u32[]{:S(2)}) collective-permute-start(f32[8,128]{1,0:T(8,128)S(1)} %get-tuple-element.43), channel_id=1, source_target_pairs={{0,4},{1,5},{2,6},{3,7},{4,0},{5,1},{6,2},{7,3},{8,12},{9,13},{10,... | collective-permute-start | bytes 12296 | tf_op jit(solution)/shard_map/ppermute | solution.py:391
  (6 other events, 31.3 us)

commit v5 on v4

--- a/solution.py
+++ b/solution.py
@@ -50,7 +50,7 @@
 
 
 def masks_kernel(pattern_ref, out_ref):
-    spanned, kinds_pad, width = out_ref.shape
+    spanned, _, kinds_pad, width = out_ref.shape
     fields, _, _, kinds = pattern_ref.shape
     points = width // fields
     first = lax.axis_index("rad") * (width // lax.axis_size("rad")) // points
@@ -67,15 +67,17 @@
         keep = jnp.zeros((kinds_pad, width), jnp.float32)
         for col in range(fields):
             keep = jnp.where(col_field == col, by_kind[:, col : col + 1], keep)
-        out_ref[local] = keep
+        for kind in range(kinds):
+            line = jnp.broadcast_to(keep[kind : kind + 1, :], (16, width))
+            out_ref[local, kind] = line.astype(jnp.bfloat16)
 
 
 def make_masks(pattern, rows, width):
-    fields, _, _, _ = pattern.shape
+    fields, _, _, kinds = pattern.shape
     spanned = rows // (width // fields) + 1
     return pl.pallas_call(
         masks_kernel,
-        out_shape=made((spanned, 16, width)),
+        out_shape=made((spanned, kinds, 16, width), jnp.bfloat16),
         in_specs=[VMEM],
         out_specs=VMEM,
         compiler_params=pltpu.CompilerParams(vmem_limit_bytes=4 << 20),
@@ -163,8 +165,7 @@
         size = lhs.shape[1]
         parts = []
         for local in range(spanned):
-            keep = masks_ref[local, pl.ds(kind, 1), start : start + size]
-            keep = jnp.broadcast_to(keep, (16, size)).astype(jnp.bfloat16)
+            keep = masks_ref[local, kind, :, start : start + size]
             parts.append(lhs * jnp.concatenate([keep, keep], axis=0))
         one = nt_dot(jnp.concatenate(parts, axis=0), w_ref[slot, :, start : start + size])
         product = one if product is None else product + one

time: 113 us -> 113 us (level)
  no operation moved by 1% of the time
where the time goes in v5:
time: 113 us
  starting transfers between devices  54.1 us (48%)
  Pallas kernels  21 us (19%)
  waiting for transfers between devices  19.9 us (18%)
  blocking collectives  16.4 us (15%)
    ppermute x10, starting transfers between devices, swap(): return lax.ppermute(value, ALL, pairs)  28 us
    ppermute x18, starting transfers between devices, gather(): out.append(lax.ppermute(value, ALL, pairs))  26.1 us
    all_to_all x1, blocking collectives, step(): lax.all_to_all(jnp.broadcast_to(part[None], (chips,) + part.shape), ('chi...  16.4 us
    ppermute x18, waiting for transfers between devices, gather(): out.append(lax.ppermute(value, ALL, pairs))  11 us
    pallas_call x5, Pallas kernels, fetch(): pl.pallas_call(functools.partial(fetch_kernel, rung, slots), out_shape=ma...  8.93 us
    ppermute x10, waiting for transfers between devices, swap(): return lax.ppermute(value, ALL, pairs)  8.84 us
    pallas_call x5, Pallas kernels, near_half(): pl.pallas_call(functools.partial(near_half_kernel, rung, slots, points),...  3.26 us
    pallas_call x5, Pallas kernels, level(): pl.pallas_call(functools.partial(far_half_kernel, rung, slots, points), o...  3.15 us
  transfers between devices with their start and end apart: 28, of which 10 were waited for; matrix products, arithmetic and copies ran while one was open for 0% of the time, Pallas kernels for 14%

profile of v5, /device:TPU:1, one launch (start us, length us, event | category | flops | bytes accessed | tf_op | source)
XLA Modules:
  0.0 112.6 jit_solution(14648659814254861918)
XLA Ops:
  0.7 4.7 %collective-permute-start.2 = (f32[32,432]{1,0:T(8,128)}, f32[32,432]{1,0:T(8,128)S(1)}, u32[]{:S(2)}, u32[]{:S(2)}) collective-permute-start(f32[32,432]{1,0:T(8,128)} %bitcast.5), channel_id=1, source_target_pairs={{0,3},{1,2},{2,1},{3,0},{4,7},{5,6},{6,5},{7,4},{8,11},{9,10},{10,... | collective-permute-start | bytes 165896 | tf_op jit(solution)/shard_map/ppermute | solution.py:399
  6.6 1.9 %shard_map.67.w_ref = bf16[2,432,1728]{2,1,0:T(8,128)(2,1)S(1)} custom-call(bf16[1,10,432,1728]{3,2,1,0:T(8,128)(2,1)} %couplings_ref.9), custom_call_target="tpu_custom_call" | custom-call | tf_op jit(solution)/shard_map/pallas_call | solution.py:109
  11.0 2.0 %collective-permute-start.3 = (f32[24,432]{1,0:T(8,128)S(1)}, f32[24,432]{1,0:T(8,128)S(1)}, u32[]{:S(2)}, u32[]{:S(2)}) collective-permute-start(f32[24,432]{1,0:T(8,128)S(1)} %get-tuple-element.29.rest_0_), channel_id=1, source_target_pairs={{0,4},{1,5},{2,6},{3,7},{4,0},{5,1},{6,2},{7,3},{8,12},{9,13},{10,... | collective-permute-start | bytes 124424 | tf_op jit(solution)/shard_map/ppermute | solution.py:392
  14.3 1.9 %shard_map.68.w_ref = bf16[2,432,1728]{2,1,0:T(8,128)(2,1)S(1)} custom-call(bf16[1,10,432,1728]{3,2,1,0:T(8,128)(2,1)} %couplings_ref.9, f32[24,432]{1,0:T(8,128)S(1)} %get-tuple-element.29.rest_0_), custom_call_target="tpu_custom_call" | custom-call | tf_op jit(solution)/shard_map/pallas_call | solution.py:109
  16.4 1.8 %collective-permute-start.5 = (f32[16,432]{1,0:T(8,128)S(1)}, f32[16,432]{1,0:T(8,128)S(1)}, u32[]{:S(2)}, u32[]{:S(2)}) collective-permute-start(f32[16,432]{1,0:T(8,128)S(1)} %fusion.3.s0), channel_id=1, source_target_pairs={{0,1},{1,0},{2,3},{3,2},{4,5},{5,4},{6,7},{7,6},{8,9},{9,8},{10,11... | collective-permute-start | bytes 82952 | tf_op jit(solution)/shard_map/ppermute | solution.py:399
  20.7 2.6 %collective-permute-done.7.s3 = f32[16,432]{1,0:T(8,128)S(1)} collective-permute-done((f32[16,432]{1,0:T(8,128)S(1)}, f32[16,432]{1,0:T(8,128)S(1)}, u32[]{:S(2)}, u32[]{:S(2)}) %collective-permute-start.7) | collective-permute-done | bytes 27680 | tf_op jit(solution)/shard_map/ppermute | solution.py:399
  24.7 1.7 %collective-permute-start.8 = (f32[24,432]{1,0:T(8,128)S(1)}, f32[24,432]{1,0:T(8,128)S(1)}, u32[]{:S(2)}, u32[]{:S(2)}) collective-permute-start(f32[24,432]{1,0:T(8,128)S(1)} %get-tuple-element.33.rest_0_), channel_id=1, source_target_pairs={{0,8},{1,9},{2,10},{3,11},{4,12},{5,13},{6,14},{7,15},{8,0},{9,1},... | collective-permute-start | bytes 124424 | tf_op jit(solution)/shard_map/ppermute | solution.py:392
  26.4 6.7 %collective-permute-start.9 = (f32[16,432]{1,0:T(8,128)S(1)}, f32[16,432]{1,0:T(8,128)S(1)}, u32[]{:S(2)}, u32[]{:S(2)}) collective-permute-start(f32[16,432]{1,0:T(8,128)S(1)} %get-tuple-element.34), channel_id=1, source_target_pairs={{0,120},{1,121},{2,122},{3,123},{4,124},{5,125},{6,126},{7,127},{8... | collective-permute-start | bytes 82952 | tf_op jit(solution)/shard_map/ppermute | solution.py:392
  33.1 1.9 %shard_map.69.w_ref = bf16[2,432,1728]{2,1,0:T(8,128)(2,1)S(1)} custom-call(bf16[1,10,432,1728]{3,2,1,0:T(8,128)(2,1)} %couplings_ref.9, f32[24,432]{1,0:T(8,128)S(1)} %get-tuple-element.33.rest_0_), custom_call_target="tpu_custom_call" | custom-call | tf_op jit(solution)/shard_map/pallas_call | solution.py:109
  35.1 2.5 %collective-permute-start.11 = (f32[16,432]{1,0:T(8,128)S(1)}, f32[16,432]{1,0:T(8,128)S(1)}, u32[]{:S(2)}, u32[]{:S(2)}) collective-permute-start(f32[16,432]{1,0:T(8,128)S(1)} %fusion.2.s0), channel_id=1, source_target_pairs={{0,2},{1,3},{2,0},{3,1},{4,6},{5,7},{6,4},{7,5},{8,10},{9,11},{10,... | collective-permute-start | bytes 82952 | tf_op jit(solution)/shard_map/ppermute | solution.py:399
  39.0 2.6 %collective-permute-done.12.s3 = f32[16,432]{1,0:T(8,128)S(1)} collective-permute-done((f32[16,432]{1,0:T(8,128)S(1)}, f32[16,432]{1,0:T(8,128)S(1)}, u32[]{:S(2)}, u32[]{:S(2)}) %collective-permute-start.12) | collective-permute-done | bytes 27680 | tf_op jit(solution)/shard_map/ppermute | solution.py:399
  43.1 2.0 %collective-permute-start.14 = (f32[16,432]{1,0:T(8,128)S(1)}, f32[16,432]{1,0:T(8,128)S(1)}, u32[]{:S(2)}, u32[]{:S(2)}) collective-permute-start(f32[16,432]{1,0:T(8,128)S(1)} %get-tuple-element.38), channel_id=1, source_target_pairs={{0,112},{1,113},{2,114},{3,115},{4,116},{5,117},{6,118},{7,119},{8... | collective-permute-start | bytes 82952 | tf_op jit(solution)/shard_map/ppermute | solution.py:392
  45.1 1.9 %shard_map.70.w_ref = bf16[2,432,1728]{2,1,0:T(8,128)(2,1)S(1)} custom-call(bf16[1,10,432,1728]{3,2,1,0:T(8,128)(2,1)} %couplings_ref.9, f32[24,432]{1,0:T(8,128)S(1)} %get-tuple-element.37.rest_0_), custom_call_target="tpu_custom_call" | custom-call | tf_op jit(solution)/shard_map/pallas_call | solution.py:109
  47.0 2.6 %collective-permute-done.14 = f32[16,432]{1,0:T(8,128)S(1)} collective-permute-done((f32[16,432]{1,0:T(8,128)S(1)}, f32[16,432]{1,0:T(8,128)S(1)}, u32[]{:S(2)}, u32[]{:S(2)}) %collective-permute-start.14) | collective-permute-done | bytes 27680 | tf_op jit(solution)/shard_map/ppermute | solution.py:392
  49.7 2.5 %collective-permute-start.16 = (f32[16,432]{1,0:T(8,128)S(1)}, f32[16,432]{1,0:T(8,128)S(1)}, u32[]{:S(2)}, u32[]{:S(2)}) collective-permute-start(f32[16,432]{1,0:T(8,128)S(1)} %fusion.1.s0), channel_id=1, source_target_pairs={{0,2},{1,3},{2,0},{3,1},{4,6},{5,7},{6,4},{7,5},{8,10},{9,11},{10,... | collective-permute-start | bytes 82952 | tf_op jit(solution)/shard_map/ppermute | solution.py:399
  53.5 2.6 %collective-permute-done.17.s3 = f32[16,432]{1,0:T(8,128)S(1)} collective-permute-done((f32[16,432]{1,0:T(8,128)S(1)}, f32[16,432]{1,0:T(8,128)S(1)}, u32[]{:S(2)}, u32[]{:S(2)}) %collective-permute-start.17) | collective-permute-done | bytes 27680 | tf_op jit(solution)/shard_map/ppermute | solution.py:399
  62.0 2.5 %collective-permute-start.21 = (f32[16,432]{1,0:T(8,128)S(1)}, f32[16,432]{1,0:T(8,128)S(1)}, u32[]{:S(2)}, u32[]{:S(2)}) collective-permute-start(f32[16,432]{1,0:T(8,128)S(1)} %fusion.s0), channel_id=1, source_target_pairs={{0,2},{1,3},{2,0},{3,1},{4,6},{5,7},{6,4},{7,5},{8,10},{9,11},{10,... | collective-permute-start | bytes 82952 | tf_op jit(solution)/shard_map/ppermute | solution.py:399
  65.8 2.6 %collective-permute-done.22.s3 = f32[16,432]{1,0:T(8,128)S(1)} collective-permute-done((f32[16,432]{1,0:T(8,128)S(1)}, f32[16,432]{1,0:T(8,128)S(1)}, u32[]{:S(2)}, u32[]{:S(2)}) %collective-permute-start.22) | collective-permute-done | bytes 27680 | tf_op jit(solution)/shard_map/ppermute | solution.py:399
  70.2 3.6 %collective-permute-done.23 = f32[24,432]{1,0:T(8,128)S(1)} collective-permute-done((f32[24,432]{1,0:T(8,128)S(1)}, f32[24,432]{1,0:T(8,128)S(1)}, u32[]{:S(2)}, u32[]{:S(2)}) %collective-permute-start.23) | collective-permute-done | bytes 41504 | tf_op jit(solution)/shard_map/ppermute | solution.py:392
  75.3 2.5 %collective-permute-start.25 = (f32[24,432]{1,0:T(8,128)S(1)}, f32[24,432]{1,0:T(8,128)S(1)}, u32[]{:S(2)}, u32[]{:S(2)}) collective-permute-start(f32[24,432]{1,0:T(8,128)S(1)} %select_maximum_fusion.s0), channel_id=1, source_target_pairs={{0,2},{1,3},{2,0},{3,1},{4,6},{5,7},{6,4},{7,5},{8,10},{9,11},{10,... | collective-permute-start | bytes 124424 | tf_op jit(solution)/shard_map/ppermute | solution.py:399
  77.8 2.1 %prep_pivots.1.p_ref = bf16[2,432,1728]{2,1,0:T(8,128)(2,1)S(1)} custom-call(f32[1,432,1728]{2,1,0:T(8,128)} %pivots_ref.1, f32[24,432]{1,0:T(8,128)S(1)} %level.9._), custom_call_target="tpu_custom_call" | custom-call | tf_op jit(solution)/shard_map/prep_pivots/pallas_call | solution.py:140
  81.5 12.1 %collective-permute-start.27 = (f32[8,128]{1,0:T(8,128)S(1)}, f32[8,128]{1,0:T(8,128)S(1)}, u32[]{:S(2)}, u32[]{:S(2)}) collective-permute-start(f32[8,128]{1,0:T(8,128)S(1)} %get-tuple-element.43), channel_id=1, source_target_pairs={{0,4},{1,5},{2,6},{3,7},{4,0},{5,1},{6,2},{7,3},{8,12},{9,13},{10,... | collective-permute-start | bytes 12296 | tf_op jit(solution)/shard_map/ppermute | solution.py:392
  94.5 16.4 %all_to_all.5.parts_ref = f32[64,8,128]{2,1,0:T(8,128)S(1)} all-to-all(f32[64,8,128]{2,1,0:T(8,128)S(1)} %broadcast_in_dim.14), channel_id=1, replica_groups=mesh['chip'=16,'core'=2,'rad'=4] {'chip','rad'}, dimensions={0} | all-to-all | bytes 524288 | tf_op jit(solution)/shard_map/all_to_all | solution.py:445
  110.9 1.7 %finish.1 = (f32[1,16,432]{2,1,0:T(8,128)}, f32[16,32]{1,0:T(8,128)}, f32[16,16]{1,0:T(8,128)}) custom-call(f32[64,8,128]{2,1,0:T(8,128)S(1)} %all_to_all.5.parts_ref, f32[8,128]{1,0:T(8,128)S(1)} %get-tuple-element.44.g_ref, f32[16,432]{1,0:T(8,128)S(1)} %get-tuple-element.45.x_ref, f32[1,32,432]{2,1,0:T(8,128)S(1)} %copy-done), custom_call_target="tpu_custom_call" | custom-call | tf_op jit(solution)/shard_map/finish/pallas_call | solution.py:369
  (70 shorter events, 26.0 us)
Async XLA Ops:
  0.7 8.3 %collective-permute-start.2 = (f32[32,432]{1,0:T(8,128)}, f32[32,432]{1,0:T(8,128)S(1)}, u32[]{:S(2)}, u32[]{:S(2)}) collective-permute-start(f32[32,432]{1,0:T(8,128)} %bitcast.5), channel_id=1, source_target_pairs={{0,3},{1,2},{2,1},{3,0},{4,7},{5,6},{6,5},{7,4},{8,11},{9,10},{10,... | collective-permute-start | bytes 165896 | tf_op jit(solution)/shard_map/ppermute | solution.py:399
  5.3 4.5 %collective-permute-start = (f32[32,432]{1,0:T(8,128)}, f32[32,432]{1,0:T(8,128)S(1)}, u32[]{:S(2)}, u32[]{:S(2)}) collective-permute-start(f32[32,432]{1,0:T(8,128)} %bitcast.6), channel_id=1, source_target_pairs={{0,1},{1,0},{2,3},{3,2},{4,5},{5,4},{6,7},{7,6},{8,9},{9,8},{10,11... | collective-permute-start | bytes 165896 | tf_op jit(solution)/shard_map/ppermute | solution.py:399
  5.3 5.0 %collective-permute-start.1 = (f32[32,432]{1,0:T(8,128)}, f32[32,432]{1,0:T(8,128)S(1)}, u32[]{:S(2)}, u32[]{:S(2)}) collective-permute-start(f32[32,432]{1,0:T(8,128)} %bitcast.7), channel_id=1, source_target_pairs={{0,2},{1,3},{2,0},{3,1},{4,6},{5,7},{6,4},{7,5},{8,10},{9,11},{10,... | collective-permute-start | bytes 165896 | tf_op jit(solution)/shard_map/ppermute | solution.py:399
  11.0 5.4 %collective-permute-start.3 = (f32[24,432]{1,0:T(8,128)S(1)}, f32[24,432]{1,0:T(8,128)S(1)}, u32[]{:S(2)}, u32[]{:S(2)}) collective-permute-start(f32[24,432]{1,0:T(8,128)S(1)} %get-tuple-element.29.rest_0_), channel_id=1, source_target_pairs={{0,4},{1,5},{2,6},{3,7},{4,0},{5,1},{6,2},{7,3},{8,12},{9,13},{10,... | collective-permute-start | bytes 124424 | tf_op jit(solution)/shard_map/ppermute | solution.py:392
  16.4 7.6 %collective-permute-start.5 = (f32[16,432]{1,0:T(8,128)S(1)}, f32[16,432]{1,0:T(8,128)S(1)}, u32[]{:S(2)}, u32[]{:S(2)}) collective-permute-start(f32[16,432]{1,0:T(8,128)S(1)} %fusion.3.s0), channel_id=1, source_target_pairs={{0,1},{1,0},{2,3},{3,2},{4,5},{5,4},{6,7},{7,6},{8,9},{9,8},{10,11... | collective-permute-start | bytes 82952 | tf_op jit(solution)/shard_map/ppermute | solution.py:399
  18.2 5.8 %collective-permute-start.6 = (f32[16,432]{1,0:T(8,128)S(1)}, f32[16,432]{1,0:T(8,128)S(1)}, u32[]{:S(2)}, u32[]{:S(2)}) collective-permute-start(f32[16,432]{1,0:T(8,128)S(1)} %fusion.3.s0), channel_id=1, source_target_pairs={{0,2},{1,3},{2,0},{3,1},{4,6},{5,7},{6,4},{7,5},{8,10},{9,11},{10,... | collective-permute-start | bytes 82952 | tf_op jit(solution)/shard_map/ppermute | solution.py:399
  19.3 4.0 %collective-permute-start.7 = (f32[16,432]{1,0:T(8,128)S(1)}, f32[16,432]{1,0:T(8,128)S(1)}, u32[]{:S(2)}, u32[]{:S(2)}) collective-permute-start(f32[16,432]{1,0:T(8,128)S(1)} %fusion.3.s0), channel_id=1, source_target_pairs={{0,3},{1,2},{2,1},{3,0},{4,7},{5,6},{6,5},{7,4},{8,11},{9,10},{10,... | collective-permute-start | bytes 82952 | tf_op jit(solution)/shard_map/ppermute | solution.py:399
  24.7 10.3 %collective-permute-start.8 = (f32[24,432]{1,0:T(8,128)S(1)}, f32[24,432]{1,0:T(8,128)S(1)}, u32[]{:S(2)}, u32[]{:S(2)}) collective-permute-start(f32[24,432]{1,0:T(8,128)S(1)} %get-tuple-element.33.rest_0_), channel_id=1, source_target_pairs={{0,8},{1,9},{2,10},{3,11},{4,12},{5,13},{6,14},{7,15},{8,0},{9,1},... | collective-permute-start | bytes 124424 | tf_op jit(solution)/shard_map/ppermute | solution.py:392
  26.4 8.6 %collective-permute-start.9 = (f32[16,432]{1,0:T(8,128)S(1)}, f32[16,432]{1,0:T(8,128)S(1)}, u32[]{:S(2)}, u32[]{:S(2)}) collective-permute-start(f32[16,432]{1,0:T(8,128)S(1)} %get-tuple-element.34), channel_id=1, source_target_pairs={{0,120},{1,121},{2,122},{3,123},{4,124},{5,125},{6,126},{7,127},{8... | collective-permute-start | bytes 82952 | tf_op jit(solution)/shard_map/ppermute | solution.py:392
  35.0 7.2 %collective-permute-start.10 = (f32[16,432]{1,0:T(8,128)S(1)}, f32[16,432]{1,0:T(8,128)S(1)}, u32[]{:S(2)}, u32[]{:S(2)}) collective-permute-start(f32[16,432]{1,0:T(8,128)S(1)} %fusion.2.s0), channel_id=1, source_target_pairs={{0,1},{1,0},{2,3},{3,2},{4,5},{5,4},{6,7},{7,6},{8,9},{9,8},{10,11... | collective-permute-start | bytes 82952 | tf_op jit(solution)/shard_map/ppermute | solution.py:399
  35.1 7.2 %collective-permute-start.11 = (f32[16,432]{1,0:T(8,128)S(1)}, f32[16,432]{1,0:T(8,128)S(1)}, u32[]{:S(2)}, u32[]{:S(2)}) collective-permute-start(f32[16,432]{1,0:T(8,128)S(1)} %fusion.2.s0), channel_id=1, source_target_pairs={{0,2},{1,3},{2,0},{3,1},{4,6},{5,7},{6,4},{7,5},{8,10},{9,11},{10,... | collective-permute-start | bytes 82952 | tf_op jit(solution)/shard_map/ppermute | solution.py:399
  43.0 6.6 %collective-permute-start.13 = (f32[24,432]{1,0:T(8,128)S(1)}, f32[24,432]{1,0:T(8,128)S(1)}, u32[]{:S(2)}, u32[]{:S(2)}) collective-permute-start(f32[24,432]{1,0:T(8,128)S(1)} %get-tuple-element.37.rest_0_), channel_id=1, source_target_pairs={{0,16},{1,17},{2,18},{3,19},{4,20},{5,21},{6,22},{7,23},{8,24},{9,... | collective-permute-start | bytes 124424 | tf_op jit(solution)/shard_map/ppermute | solution.py:392
  43.1 6.5 %collective-permute-start.14 = (f32[16,432]{1,0:T(8,128)S(1)}, f32[16,432]{1,0:T(8,128)S(1)}, u32[]{:S(2)}, u32[]{:S(2)}) collective-permute-start(f32[16,432]{1,0:T(8,128)S(1)} %get-tuple-element.38), channel_id=1, source_target_pairs={{0,112},{1,113},{2,114},{3,115},{4,116},{5,117},{6,118},{7,119},{8... | collective-permute-start | bytes 82952 | tf_op jit(solution)/shard_map/ppermute | solution.py:392
  49.6 7.2 %collective-permute-start.15 = (f32[16,432]{1,0:T(8,128)S(1)}, f32[16,432]{1,0:T(8,128)S(1)}, u32[]{:S(2)}, u32[]{:S(2)}) collective-permute-start(f32[16,432]{1,0:T(8,128)S(1)} %fusion.1.s0), channel_id=1, source_target_pairs={{0,1},{1,0},{2,3},{3,2},{4,5},{5,4},{6,7},{7,6},{8,9},{9,8},{10,11... | collective-permute-start | bytes 82952 | tf_op jit(solution)/shard_map/ppermute | solution.py:399
  49.7 7.2 %collective-permute-start.16 = (f32[16,432]{1,0:T(8,128)S(1)}, f32[16,432]{1,0:T(8,128)S(1)}, u32[]{:S(2)}, u32[]{:S(2)}) collective-permute-start(f32[16,432]{1,0:T(8,128)S(1)} %fusion.1.s0), channel_id=1, source_target_pairs={{0,2},{1,3},{2,0},{3,1},{4,6},{5,7},{6,4},{7,5},{8,10},{9,11},{10,... | collective-permute-start | bytes 82952 | tf_op jit(solution)/shard_map/ppermute | solution.py:399
  57.5 4.2 %collective-permute-start.18 = (f32[24,432]{1,0:T(8,128)S(1)}, f32[24,432]{1,0:T(8,128)S(1)}, u32[]{:S(2)}, u32[]{:S(2)}) collective-permute-start(f32[24,432]{1,0:T(8,128)S(1)} %get-tuple-element.41.rest_0_), channel_id=1, source_target_pairs={{0,32},{1,33},{2,34},{3,35},{4,36},{5,37},{6,38},{7,39},{8,40},{9,... | collective-permute-start | bytes 124424 | tf_op jit(solution)/shard_map/ppermute | solution.py:392
  57.6 4.1 %collective-permute-start.19 = (f32[16,432]{1,0:T(8,128)S(1)}, f32[16,432]{1,0:T(8,128)S(1)}, u32[]{:S(2)}, u32[]{:S(2)}) collective-permute-start(f32[16,432]{1,0:T(8,128)S(1)} %get-tuple-element.42), channel_id=1, source_target_pairs={{0,96},{1,97},{2,98},{3,99},{4,100},{5,101},{6,102},{7,103},{8,104... | collective-permute-start | bytes 82952 | tf_op jit(solution)/shard_map/ppermute | solution.py:392
  61.7 7.2 %collective-permute-start.20 = (f32[16,432]{1,0:T(8,128)S(1)}, f32[16,432]{1,0:T(8,128)S(1)}, u32[]{:S(2)}, u32[]{:S(2)}) collective-permute-start(f32[16,432]{1,0:T(8,128)S(1)} %fusion.s0), channel_id=1, source_target_pairs={{0,1},{1,0},{2,3},{3,2},{4,5},{5,4},{6,7},{7,6},{8,9},{9,8},{10,11... | collective-permute-start | bytes 82952 | tf_op jit(solution)/shard_map/ppermute | solution.py:399
  62.0 6.9 %collective-permute-start.21 = (f32[16,432]{1,0:T(8,128)S(1)}, f32[16,432]{1,0:T(8,128)S(1)}, u32[]{:S(2)}, u32[]{:S(2)}) collective-permute-start(f32[16,432]{1,0:T(8,128)S(1)} %fusion.s0), channel_id=1, source_target_pairs={{0,2},{1,3},{2,0},{3,1},{4,6},{5,7},{6,4},{7,5},{8,10},{9,11},{10,... | collective-permute-start | bytes 82952 | tf_op jit(solution)/shard_map/ppermute | solution.py:399
  69.3 4.5 %collective-permute-start.23 = (f32[24,432]{1,0:T(8,128)S(1)}, f32[24,432]{1,0:T(8,128)S(1)}, u32[]{:S(2)}, u32[]{:S(2)}) collective-permute-start(f32[24,432]{1,0:T(8,128)S(1)} %level.9._), channel_id=1, source_target_pairs={{0,64},{1,65},{2,66},{3,67},{4,68},{5,69},{6,70},{7,71},{8,72},{9,... | collective-permute-start | bytes 124424 | tf_op jit(solution)/shard_map/ppermute | solution.py:392
  73.9 6.1 %collective-permute-start.26 = (f32[24,432]{1,0:T(8,128)S(1)}, f32[24,432]{1,0:T(8,128)S(1)}, u32[]{:S(2)}, u32[]{:S(2)}) collective-permute-start(f32[24,432]{1,0:T(8,128)S(1)} %select_maximum_fusion.s0), channel_id=1, source_target_pairs={{0,3},{1,2},{2,1},{3,0},{4,7},{5,6},{6,5},{7,4},{8,11},{9,10},{10,... | collective-permute-start | bytes 124424 | tf_op jit(solution)/shard_map/ppermute | solution.py:399
  75.3 5.2 %collective-permute-start.24 = (f32[24,432]{1,0:T(8,128)S(1)}, f32[24,432]{1,0:T(8,128)S(1)}, u32[]{:S(2)}, u32[]{:S(2)}) collective-permute-start(f32[24,432]{1,0:T(8,128)S(1)} %select_maximum_fusion.s0), channel_id=1, source_target_pairs={{0,1},{1,0},{2,3},{3,2},{4,5},{5,4},{6,7},{7,6},{8,9},{9,8},{10,11... | collective-permute-start | bytes 124424 | tf_op jit(solution)/shard_map/ppermute | solution.py:399
  75.3 5.3 %collective-permute-start.25 = (f32[24,432]{1,0:T(8,128)S(1)}, f32[24,432]{1,0:T(8,128)S(1)}, u32[]{:S(2)}, u32[]{:S(2)}) collective-permute-start(f32[24,432]{1,0:T(8,128)S(1)} %select_maximum_fusion.s0), channel_id=1, source_target_pairs={{0,2},{1,3},{2,0},{3,1},{4,6},{5,7},{6,4},{7,5},{8,10},{9,11},{10,... | collective-permute-start | bytes 124424 | tf_op jit(solution)/shard_map/ppermute | solution.py:399
  81.5 13.0 %collective-permute-start.27 = (f32[8,128]{1,0:T(8,128)S(1)}, f32[8,128]{1,0:T(8,128)S(1)}, u32[]{:S(2)}, u32[]{:S(2)}) collective-permute-start(f32[8,128]{1,0:T(8,128)S(1)} %get-tuple-element.43), channel_id=1, source_target_pairs={{0,4},{1,5},{2,6},{3,7},{4,0},{5,1},{6,2},{7,3},{8,12},{9,13},{10,... | collective-permute-start | bytes 12296 | tf_op jit(solution)/shard_map/ppermute | solution.py:392
  (6 other events, 31.4 us)
